TPU v7x, 512 devices: a whole 4x4x16 slice. The times are simulated.
512 devices in a mesh: dp: 32 (over z_hi, x, core), tensor: 16 (over z_lo, y).
Axes of the slice: x: 4, y: 4, z: 16 (z_hi: 4, z_lo: 4; z = z_hi * 4 + z_lo), core: 2. Of those that a mesh axis runs over, the one named last changes fastest.
Arguments:
- tokens: bfloat16 [4096, 8192], P('dp', 'tensor'), may hold values from -6 to 6
- cotangent: bfloat16 [4096, 8192], P('dp', 'tensor'), may hold values from -6 to 6
- up_blocks: bfloat16 [5, 64, 128, 256], P(None, 'tensor'), may hold values from -0.15625 to 0.15625
- up_left: bfloat16 [8192, 128], P('tensor'), may hold values from -0.0625 to 0.0625
- up_right: bfloat16 [128, 16384], P(None, 'tensor'), may hold values from -0.375 to 0.375
- down_blocks: bfloat16 [5, 64, 256, 128], P(None, 'tensor'), may hold values from -0.125 to 0.125
- down_left: bfloat16 [16384, 128], P('tensor'), may hold values from -0.046875 to 0.046875
- down_right: bfloat16 [128, 8192], P(None, 'tensor'), may hold values from -0.375 to 0.375
Outputs:
- out: bfloat16 [4096, 8192], P('dp', 'tensor')
- tokens_grad: bfloat16 [4096, 8192], P('dp', 'tensor')
- up_blocks_grad: bfloat16 [5, 64, 128, 256], P(None, 'tensor', 'dp')
- up_left_grad: bfloat16 [8192, 128], P('tensor', 'dp')
- up_right_grad: bfloat16 [128, 16384], P('dp', 'tensor')
- down_blocks_grad: bfloat16 [5, 64, 256, 128], P(None, 'tensor', 'dp')
- down_left_grad: bfloat16 [16384, 128], P('tensor', 'dp')
- down_right_grad: bfloat16 [128, 8192], P('dp', 'tensor')
All inputs are finite; a program needn't handle non-finite values.
Results may differ from a plain program's by a relative error of at most 0.03.
Values may be sent and summed in bfloat16 or wider, within the bound.
No kernel may reach another device: no remote copies, remote signals or barrier semaphores. Data moves between devices by JAX's collectives and lax.ppermute only.
A program may use at most 64 MiB of HBM per device.

v0:
```python
import math

import jax
import jax.numpy as jnp
from jax import lax
from jax.sharding import PartitionSpec as P


def partner(block, axis, bit):
    count = lax.axis_size(axis)
    route = []
    for low in range(count):
        high = low | 1 << bit
        if high != low and high < count:
            route += [(low, high), (high, low)]
    return lax.ppermute(block, axis, route)


def smooth_gate(values):
    return jax.nn.gelu(values, approximate=False)


def blockwise(left, blocks, form, width_out):
    row_count = left.shape[0]
    block_count = blocks.shape[0]
    pieces = left.reshape(row_count, block_count, -1)
    result = jnp.einsum(form, pieces, blocks, preferred_element_type=jnp.float32)
    return result.reshape(row_count, block_count * width_out)


def block_outer(left, right, block_count, form):
    row_count = left.shape[0]
    left_pieces = left.reshape(row_count, block_count, -1)
    right_pieces = right.reshape(row_count, block_count, -1)
    return jnp.einsum(form, left_pieces, right_pieces, preferred_element_type=jnp.float32)


def body(tokens, cotangent, up_blocks, up_left, up_right, down_blocks, down_left, down_right):
    row_count = tokens.shape[0]
    block_count = up_blocks.shape[1]
    block_side = up_blocks.shape[2]
    hidden_side = up_blocks.shape[3]
    sections = lax.axis_size("tensor").bit_length() - 1
    section_bits = list(range(sections))
    grad_scale = 1.0 / math.sqrt(row_count * lax.axis_size("dp"))
    low_sums = lax.psum(
        (
            jnp.dot(tokens, up_left, preferred_element_type=jnp.float32),
            jnp.einsum("nd,rd->nr", cotangent, down_right, preferred_element_type=jnp.float32),
        ),
        "tensor",
    )
    low_up = low_sums[0].astype(jnp.bfloat16)
    low_cot = low_sums[1].astype(jnp.bfloat16)
    hidden_pre = blockwise(tokens, up_blocks[0], "nbi,bih->nbh", hidden_side)
    hidden_pre = hidden_pre + jnp.dot(low_up, up_right, preferred_element_type=jnp.float32)
    partner_tokens = {}
    partner_cot = {}
    for section_bit in section_bits:
        arrived = partner((tokens, cotangent), "tensor", section_bit)
        partner_tokens[section_bit] = arrived[0]
        partner_cot[section_bit] = arrived[1]
        hidden_pre = hidden_pre + blockwise(
            arrived[0], up_blocks[section_bit + 1], "nbi,bih->nbh", hidden_side
        )
    active, gelu_back = jax.vjp(smooth_gate, hidden_pre)
    hidden = active.astype(jnp.bfloat16)
    low_down = lax.psum(
        jnp.dot(hidden, down_left, preferred_element_type=jnp.float32), "tensor"
    ).astype(jnp.bfloat16)
    out_sum = blockwise(hidden, down_blocks[0], "nbh,bhi->nbi", block_side)
    out_sum = out_sum + jnp.dot(low_down, down_right, preferred_element_type=jnp.float32)
    for section_bit in section_bits:
        partial_out = blockwise(hidden, down_blocks[section_bit + 1], "nbh,bhi->nbi", block_side)
        out_sum = out_sum + partner(partial_out, "tensor", section_bit)
    out = out_sum.astype(jnp.bfloat16)
    hidden_grad = jnp.einsum("nr,hr->nh", low_cot, down_left, preferred_element_type=jnp.float32)
    hidden_grad = hidden_grad + blockwise(cotangent, down_blocks[0], "nbi,bhi->nbh", hidden_side)
    for section_bit in section_bits:
        hidden_grad = hidden_grad + blockwise(
            partner_cot[section_bit], down_blocks[section_bit + 1], "nbi,bhi->nbh", hidden_side
        )
    down_block_terms = (
        jnp.stack(
            [block_outer(hidden, cotangent, block_count, "nbh,nbi->bhi")]
            + [
                block_outer(hidden, partner_cot[section], block_count, "nbh,nbi->bhi")
                for section in range(sections)
            ]
        )
        * grad_scale
    )
    down_left_terms = (
        jnp.einsum("nh,nr->hr", hidden, low_cot, preferred_element_type=jnp.float32) * grad_scale
    )
    down_right_terms = (
        jnp.einsum("nr,nd->rd", low_down, cotangent, preferred_element_type=jnp.float32)
        * grad_scale
    )
    pre_grad = gelu_back(hidden_grad)[0].astype(jnp.bfloat16)
    low_pre = lax.psum(
        jnp.einsum("nh,rh->nr", pre_grad, up_right, preferred_element_type=jnp.float32), "tensor"
    ).astype(jnp.bfloat16)
    tokens_sum = jnp.einsum("nr,dr->nd", low_pre, up_left, preferred_element_type=jnp.float32)
    tokens_sum = tokens_sum + blockwise(pre_grad, up_blocks[0], "nbh,bih->nbi", block_side)
    for section_bit in section_bits:
        partial_grad = blockwise(pre_grad, up_blocks[section_bit + 1], "nbh,bih->nbi", block_side)
        tokens_sum = tokens_sum + partner(partial_grad, "tensor", section_bit)
    tokens_grad = tokens_sum.astype(jnp.bfloat16)
    up_block_terms = (
        jnp.stack(
            [block_outer(tokens, pre_grad, block_count, "nbi,nbh->bih")]
            + [
                block_outer(partner_tokens[section], pre_grad, block_count, "nbi,nbh->bih")
                for section in range(sections)
            ]
        )
        * grad_scale
    )
    up_left_terms = (
        jnp.einsum("nd,nr->dr", tokens, low_pre, preferred_element_type=jnp.float32) * grad_scale
    )
    up_right_terms = (
        jnp.einsum("nr,nh->rh", low_up, pre_grad, preferred_element_type=jnp.float32) * grad_scale
    )
    summed = (
        lax.psum_scatter(
            up_block_terms.astype(jnp.bfloat16), "dp", scatter_dimension=2, tiled=True
        ).astype(jnp.float32),
        lax.psum_scatter(
            up_left_terms.astype(jnp.bfloat16), "dp", scatter_dimension=1, tiled=True
        ).astype(jnp.float32),
        lax.psum_scatter(
            up_right_terms.astype(jnp.bfloat16), "dp", scatter_dimension=0, tiled=True
        ).astype(jnp.float32),
        lax.psum_scatter(
            down_block_terms.astype(jnp.bfloat16), "dp", scatter_dimension=2, tiled=True
        ).astype(jnp.float32),
        lax.psum_scatter(
            down_left_terms.astype(jnp.bfloat16), "dp", scatter_dimension=1, tiled=True
        ).astype(jnp.float32),
        lax.psum_scatter(
            down_right_terms.astype(jnp.bfloat16), "dp", scatter_dimension=0, tiled=True
        ).astype(jnp.float32),
    )
    grads = tuple((total.astype(jnp.bfloat16) for total in summed))
    return (out, tokens_grad, grads[0], grads[1], grads[2], grads[3], grads[4], grads[5])


def solution(mesh):
    in_specs = (
        P("dp", "tensor"),
        P("dp", "tensor"),
        P(None, "tensor", None, None),
        P("tensor", None),
        P(None, "tensor"),
        P(None, "tensor", None, None),
        P("tensor", None),
        P(None, "tensor"),
    )
    out_specs = (
        P("dp", "tensor"),
        P("dp", "tensor"),
        P(None, "tensor", "dp", None),
        P("tensor", "dp"),
        P("dp", "tensor"),
        P(None, "tensor", "dp", None),
        P("tensor", "dp"),
        P("dp", "tensor"),
    )
    return jax.shard_map(body, mesh=mesh, in_specs=in_specs, out_specs=out_specs, check_vma=False)
```

profile of v0, /device:TPU:24, one launch (start us, length us, event | category | flops | bytes accessed | tf_op | source)
XLA Modules:
  0.0 662.4 jit_solution(13627168601672628714)
XLA Ops:
  8.9 2.6 collective-permute-start
  11.6 8.2 %collective-permute-start.1 = (bf16[128,512]{0,1:T(8,128)(2,1)}, bf16[128,512]{0,1:T(8,128)(2,1)S(1)}, u32[]{:S(2)}, u32[]{:S(2)}) collective-permute-start(bf16[128,512]{0,1:T(8,128)(2,1)} %copy.174), channel_id=1, source_target_pairs={{0,2},{2,0},{1,3},{3,1},{4,6},{6,4},{5,7},{7,5},{8,10},{10,8},{9,1... | collective-permute-start | bytes 393224 | tf_op jit(solution)/shard_map/ppermute | solution.py:16
  25.3 2.7 collective-permute-start.8
  33.6 71.1 %all-reduce.13 = (bf16[128,128]{1,0:T(8,128)(2,1)S(1)}, bf16[128,128]{1,0:T(8,128)(2,1)S(1)}) all-reduce(f32[128,128]{1,0:T(8,128)} %fusion.107, f32[128,128]{1,0:T(8,128)} %fusion.109), channel_id=1, replica_groups=mesh['dp'=32,'tensor'=16] {'tensor'}, use_global_device_ids=true, to_apply=%region_0.0 | all-reduce | flops 32768 | bytes 196608 | tf_op jit(solution)/shard_map/psum | solution.py:46
  109.8 7.9 %collective-permute-start.9 = (bf16[128,512]{0,1:T(8,128)(2,1)}, bf16[128,512]{0,1:T(8,128)(2,1)}, u32[]{:S(2)}, u32[]{:S(2)}) collective-permute-start(bf16[128,512]{0,1:T(8,128)(2,1)} %copy.207), channel_id=1, source_target_pairs={{0,2},{2,0},{1,3},{3,1},{4,6},{6,4},{5,7},{7,5},{8,10},{10,8},{9,1... | collective-permute-start | bytes 393224 | tf_op jit(solution)/shard_map/ppermute | solution.py:16
  121.4 4.3 collective-permute-start.11
  127.7 2.1 copy.288
  131.9 2.0 copy.289
  139.8 2.1 copy.296
  143.8 2.0 copy.297
  147.7 2.1 copy.298
  149.8 4.4 add_convert_fusion
  161.4 2.1 copy.337
  163.5 3.5 reshape.172
  174.4 3.7 copy.248
  180.0 73.7 %all-reduce.14 = (bf16[128,128]{1,0:T(8,128)(2,1)}, bf16[128,128]{1,0:T(8,128)(2,1)}) all-reduce(f32[128,128]{1,0:T(8,128)} %fusion.108, f32[128,128]{1,0:T(8,128)} %fusion.110), channel_id=1, replica_groups=mesh['dp'=32,'tensor'=16] {'tensor'}, use_global_device_ids=true, to_apply=%region_1.0 | all-reduce | flops 32768 | bytes 196608 | tf_op jit(solution)/shard_map/psum | solution.py:68
  266.3 6.0 collective-permute-start.12
  274.1 8.1 %collective-permute-start.13 = (f32[128,512]{1,0:T(8,128)}, f32[128,512]{1,0:T(8,128)}, u32[]{:S(2)}, u32[]{:S(2)}) collective-permute-start(f32[128,512]{1,0:T(8,128)} %copy.301), channel_id=1, source_target_pairs={{0,2},{2,0},{1,3},{3,1},{4,6},{6,4},{5,7},{7,5},{8,10},{10,8},{9,1... | collective-permute-start | bytes 786440 | tf_op jit(solution)/shard_map/ppermute | solution.py:16
  297.7 5.7 collective-permute-start.5
  305.4 3.0 collective-permute-start.7
  308.4 2.1 fusion.23
  310.5 3.4 collective-permute-done.6
  313.9 5.4 collective-permute-done.7
  321.6 327.3 %all-reduce.12.cloned.1.call-done = (bf16[5,4,128,256]{3,1,0,2:T(4,128)(2,1)}, bf16[512,128]{0,1:T(8,128)(2,1)}, bf16[128,1024]{1,0:T(8,128)(2,1)}, bf16[1024,128]{0,1:T(8,128)(2,1)}, bf16[128,512]{1,0:T(8,128)(2,1)}) async-done(((bf16[5,4,128,256]{3,1,0,2:T(4,128)(2,1)}, bf16[512,128]{0,1:T(8,128)(2,1)}, bf16[128,1024]{1,0:T(8,128)(2,1)}, bf16[1024,128]{0,1:T(8,128)(2,1)}, bf16[128,512]{1,0:T(8,128)(2,1)}), ...) | async-done | bytes 2097168
  (132 shorter events, 91.6 us)
Async XLA Ops:
  7.2 99.5 %copy-start = (bf16[1024,128]{1,0:T(8,128)(2,1)S(1)}, bf16[1024,128]{1,0:T(8,128)(2,1)}, u32[]{:S(2)}) copy-start(bf16[1024,128]{1,0:T(8,128)(2,1)} %param.14) | copy-start | bytes 786436
  7.2 313.0 %reduce-scatter.4.cloned.1.call-start = ((), (), s32[]{:S(2)}) async-start(), calls=%async_computation.1 | async-start | bytes 1351680
  8.9 100.8 %collective-permute-start = (bf16[128,512]{0,1:T(8,128)(2,1)}, bf16[128,512]{0,1:T(8,128)(2,1)S(1)}, u32[]{:S(2)}, u32[]{:S(2)}) collective-permute-start(bf16[128,512]{0,1:T(8,128)(2,1)} %copy.174), channel_id=1, source_target_pairs={{0,1},{1,0},{2,3},{3,2},{4,5},{5,4},{6,7},{7,6},{8,9},{9,8},{10,11... | collective-permute-start | bytes 393224 | tf_op jit(solution)/shard_map/ppermute | solution.py:16
  11.6 106.6 %collective-permute-start.1 = (bf16[128,512]{0,1:T(8,128)(2,1)}, bf16[128,512]{0,1:T(8,128)(2,1)S(1)}, u32[]{:S(2)}, u32[]{:S(2)}) collective-permute-start(bf16[128,512]{0,1:T(8,128)(2,1)} %copy.174), channel_id=1, source_target_pairs={{0,2},{2,0},{1,3},{3,1},{4,6},{6,4},{5,7},{7,5},{8,10},{10,8},{9,1... | collective-permute-start | bytes 393224 | tf_op jit(solution)/shard_map/ppermute | solution.py:16
  19.8 101.6 %collective-permute-start.2 = (bf16[128,512]{0,1:T(8,128)(2,1)}, bf16[128,512]{0,1:T(8,128)(2,1)}, u32[]{:S(2)}, u32[]{:S(2)}) collective-permute-start(bf16[128,512]{0,1:T(8,128)(2,1)} %copy.174), channel_id=1, source_target_pairs={{0,4},{4,0},{1,5},{5,1},{2,6},{6,2},{3,7},{7,3},{8,12},{12,8},{9,1... | collective-permute-start | bytes 393224 | tf_op jit(solution)/shard_map/ppermute | solution.py:16
  21.7 108.1 %collective-permute-start.3 = (bf16[128,512]{0,1:T(8,128)(2,1)}, bf16[128,512]{0,1:T(8,128)(2,1)}, u32[]{:S(2)}, u32[]{:S(2)}) collective-permute-start(bf16[128,512]{0,1:T(8,128)(2,1)} %copy.174), channel_id=1, source_target_pairs={{0,8},{8,0},{1,9},{9,1},{2,10},{10,2},{3,11},{11,3},{4,12},{12,4},... | collective-permute-start | bytes 393224 | tf_op jit(solution)/shard_map/ppermute | solution.py:16
  25.3 108.6 %collective-permute-start.8 = (bf16[128,512]{0,1:T(8,128)(2,1)}, bf16[128,512]{0,1:T(8,128)(2,1)}, u32[]{:S(2)}, u32[]{:S(2)}) collective-permute-start(bf16[128,512]{0,1:T(8,128)(2,1)} %copy.207), channel_id=1, source_target_pairs={{0,1},{1,0},{2,3},{3,2},{4,5},{5,4},{6,7},{7,6},{8,9},{9,8},{10,11... | collective-permute-start | bytes 393224 | tf_op jit(solution)/shard_map/ppermute | solution.py:16
  109.8 28.1 %collective-permute-start.9 = (bf16[128,512]{0,1:T(8,128)(2,1)}, bf16[128,512]{0,1:T(8,128)(2,1)}, u32[]{:S(2)}, u32[]{:S(2)}) collective-permute-start(bf16[128,512]{0,1:T(8,128)(2,1)} %copy.207), channel_id=1, source_target_pairs={{0,2},{2,0},{1,3},{3,1},{4,6},{6,4},{5,7},{7,5},{8,10},{10,8},{9,1... | collective-permute-start | bytes 393224 | tf_op jit(solution)/shard_map/ppermute | solution.py:16
  118.2 9.6 %copy-start.9 = (bf16[128,512]{0,1:T(8,128)(2,1)}, bf16[128,512]{0,1:T(8,128)(2,1)S(1)}, u32[]{:S(2)}) copy-start(bf16[128,512]{0,1:T(8,128)(2,1)S(1)} %collective-permute-done.1) | copy-start | bytes 393220
  118.2 23.7 %collective-permute-start.10 = (bf16[128,512]{0,1:T(8,128)(2,1)}, bf16[128,512]{0,1:T(8,128)(2,1)}, u32[]{:S(2)}, u32[]{:S(2)}) collective-permute-start(bf16[128,512]{0,1:T(8,128)(2,1)} %copy.207), channel_id=1, source_target_pairs={{0,4},{4,0},{1,5},{5,1},{2,6},{6,2},{3,7},{7,3},{8,12},{12,8},{9,1... | collective-permute-start | bytes 393224 | tf_op jit(solution)/shard_map/ppermute | solution.py:16
  121.4 24.4 %collective-permute-start.11 = (bf16[128,512]{0,1:T(8,128)(2,1)}, bf16[128,512]{0,1:T(8,128)(2,1)}, u32[]{:S(2)}, u32[]{:S(2)}) collective-permute-start(bf16[128,512]{0,1:T(8,128)(2,1)} %copy.207), channel_id=1, source_target_pairs={{0,8},{8,0},{1,9},{9,1},{2,10},{10,2},{3,11},{11,3},{4,12},{12,4},... | collective-permute-start | bytes 393224 | tf_op jit(solution)/shard_map/ppermute | solution.py:16
  167.0 481.9 %all-reduce.12.cloned.1.call-start = ((), (), s32[]{:S(2)}) async-start(), calls=%async_computation.2 | async-start | bytes 4194304
  266.3 31.4 %collective-permute-start.12 = (f32[128,512]{1,0:T(8,128)}, f32[128,512]{1,0:T(8,128)}, u32[]{:S(2)}, u32[]{:S(2)}) collective-permute-start(f32[128,512]{1,0:T(8,128)} %copy.300), channel_id=1, source_target_pairs={{0,1},{1,0},{2,3},{3,2},{4,5},{5,4},{6,7},{7,6},{8,9},{9,8},{10,11... | collective-permute-start | bytes 786440 | tf_op jit(solution)/shard_map/ppermute | solution.py:16
  274.1 29.3 %collective-permute-start.13 = (f32[128,512]{1,0:T(8,128)}, f32[128,512]{1,0:T(8,128)}, u32[]{:S(2)}, u32[]{:S(2)}) collective-permute-start(f32[128,512]{1,0:T(8,128)} %copy.301), channel_id=1, source_target_pairs={{0,2},{2,0},{1,3},{3,1},{4,6},{6,4},{5,7},{7,5},{8,10},{10,8},{9,1... | collective-permute-start | bytes 786440 | tf_op jit(solution)/shard_map/ppermute | solution.py:16
  284.1 21.3 %collective-permute-start.14 = (f32[128,512]{1,0:T(8,128)}, f32[128,512]{1,0:T(8,128)}, u32[]{:S(2)}, u32[]{:S(2)}) collective-permute-start(f32[128,512]{1,0:T(8,128)} %copy.302), channel_id=1, source_target_pairs={{0,4},{4,0},{1,5},{5,1},{2,6},{6,2},{3,7},{7,3},{8,12},{12,8},{9,1... | collective-permute-start | bytes 786440 | tf_op jit(solution)/shard_map/ppermute | solution.py:16
  287.8 20.6 %collective-permute-start.15 = (f32[128,512]{1,0:T(8,128)}, f32[128,512]{1,0:T(8,128)}, u32[]{:S(2)}, u32[]{:S(2)}) collective-permute-start(f32[128,512]{1,0:T(8,128)} %copy.303), channel_id=1, source_target_pairs={{0,8},{8,0},{1,9},{9,1},{2,10},{10,2},{3,11},{11,3},{4,12},{12,4},... | collective-permute-start | bytes 786440 | tf_op jit(solution)/shard_map/ppermute | solution.py:16
  292.9 17.6 %collective-permute-start.4 = (f32[128,512]{1,0:T(8,128)}, f32[128,512]{1,0:T(8,128)S(1)}, u32[]{:S(2)}, u32[]{:S(2)}) collective-permute-start(f32[128,512]{1,0:T(8,128)} %copy.290), channel_id=1, source_target_pairs={{0,1},{1,0},{2,3},{3,2},{4,5},{5,4},{6,7},{7,6},{8,9},{9,8},{10,11... | collective-permute-start | bytes 786440 | tf_op jit(solution)/shard_map/ppermute | solution.py:16
  295.6 12.8 %copy-start.11 = (bf16[512,128]{1,0:T(8,128)(2,1)S(1)}, bf16[512,128]{1,0:T(8,128)(2,1)}, u32[]{:S(2)}) copy-start(bf16[512,128]{1,0:T(8,128)(2,1)} %param.11) | copy-start | bytes 393220
  295.6 12.8 %copy-start.14 = (bf16[128,128]{1,0:T(8,128)(2,1)S(1)}, bf16[128,128]{1,0:T(8,128)(2,1)}, u32[]{:S(2)}) copy-start(bf16[128,128]{1,0:T(8,128)(2,1)} %get-tuple-element.33) | copy-start | bytes 98308
  297.3 22.0 %copy-start.12 = (bf16[128,512]{1,0:T(8,128)(2,1)S(1)}, bf16[128,512]{1,0:T(8,128)(2,1)}, u32[]{:S(2)}) copy-start(bf16[128,512]{1,0:T(8,128)(2,1)} %param.15) | copy-start | bytes 393220
  297.3 22.0 %copy-start.13 = (bf16[128,128]{1,0:T(8,128)(2,1)S(1)}, bf16[128,128]{1,0:T(8,128)(2,1)}, u32[]{:S(2)}) copy-start(bf16[128,128]{1,0:T(8,128)(2,1)} %get-tuple-element.32) | copy-start | bytes 98308
  297.7 12.8 %collective-permute-start.5 = (f32[128,512]{1,0:T(8,128)}, f32[128,512]{1,0:T(8,128)S(1)}, u32[]{:S(2)}, u32[]{:S(2)}) collective-permute-start(f32[128,512]{1,0:T(8,128)} %copy.291), channel_id=1, source_target_pairs={{0,2},{2,0},{1,3},{3,1},{4,6},{6,4},{5,7},{7,5},{8,10},{10,8},{9,1... | collective-permute-start | bytes 786440 | tf_op jit(solution)/shard_map/ppermute | solution.py:16
  303.5 10.4 %collective-permute-start.6 = (f32[128,512]{1,0:T(8,128)}, f32[128,512]{1,0:T(8,128)S(1)}, u32[]{:S(2)}, u32[]{:S(2)}) collective-permute-start(f32[128,512]{1,0:T(8,128)} %copy.292), channel_id=1, source_target_pairs={{0,4},{4,0},{1,5},{5,1},{2,6},{6,2},{3,7},{7,3},{8,12},{12,8},{9,1... | collective-permute-start | bytes 786440 | tf_op jit(solution)/shard_map/ppermute | solution.py:16
  305.4 13.9 %collective-permute-start.7 = (f32[128,512]{1,0:T(8,128)}, f32[128,512]{1,0:T(8,128)S(1)}, u32[]{:S(2)}, u32[]{:S(2)}) collective-permute-start(f32[128,512]{1,0:T(8,128)} %copy.293), channel_id=1, source_target_pairs={{0,8},{8,0},{1,9},{9,1},{2,10},{10,2},{3,11},{11,3},{4,12},{12,4},... | collective-permute-start | bytes 786440 | tf_op jit(solution)/shard_map/ppermute | solution.py:16
  (11 other events, 47.8 us)
Sparse Core Ops, SparseCore 0:
  167.1 119.4 reduce-scatter.3
  290.2 358.6 all-reduce.11
where the time goes:
time: 665 us; the launch traced here: 662 us
  waiting for transfers between devices  336 us (51%)
  blocking collectives  145 us (22%)
  starting transfers between devices  62.1 us (9%)
  matrix products  48.6 us (7%)
  local copies, waits for them, and re-layouts  48.2 us (7%)
  between operations  15.2 us (2%)
  other arithmetic  7.2 us (1%)
    unnamed x4, waiting for transfers between devices  327 us
    psum x1, blocking collectives, body(): lax.psum(jnp.dot(hidden, down_left, preferred_element_type=jnp.float32),...  73.7 us
    psum x1, blocking collectives, body(): lax.psum((jnp.dot(tokens, up_left, preferred_element_type=jnp.float32), j...  71.1 us
    ppermute x16, starting transfers between devices, partner(): return lax.ppermute(block, axis, route)  62 us
    reshape x20, local copies, waits for them, and re-layouts, blockwise(): return result.reshape(row_count, block_count * width_out)  24.8 us
    dot_general x20, matrix products, blockwise(): jnp.einsum(form, pieces, blocks, preferred_element_type=jnp.float32)  19.7 us
    unnamed x47, local copies, waits for them, and re-layouts  18.5 us
  transfers between devices with their start and end apart: 18, of which 3 were waited for; matrix products, arithmetic and copies ran while one was open for 11% of the time, Pallas kernels for 0%

commit v1 on v0

v1 whole, which is shorter than its diff:
```python
import functools
import math

import jax
import jax.numpy as jnp
from jax import lax
from jax.experimental import pallas as pl
from jax.experimental.pallas import tpu as pltpu
from jax.sharding import Mesh
from jax.sharding import PartitionSpec as P

DP = ("zh", "x", "core")
TENSOR = ("zl", "y")
SIZES = (4, 4, 2, 4, 4)
ROWS = 128
SIDE = 256
SLAB = 512
HIDDEN = 1024
BLOCKS = 4
FACTORS = 5
F32 = jnp.float32
BF16 = jnp.bfloat16

GROUP = BLOCKS * SIDE
DOWN_AT = 3 * GROUP
LEFT_AT = DOWN_AT + BLOCKS * FACTORS * ROWS
MAIN = LEFT_AT + SLAB
MINI = SLAB
LIMIT = 48 * 1024 * 1024


def mm(a, b):
    return lax.dot_general(a, b, (((1,), (0,)), ((), ())), preferred_element_type=F32)


def mt(a, b):
    return lax.dot_general(a, b, (((1,), (1,)), ((), ())), preferred_element_type=F32)


def pick(core):
    row = lax.broadcasted_iota(jnp.int32, (SIDE, SIDE), 0)
    column = lax.broadcasted_iota(jnp.int32, (SIDE, SIDE), 1)
    quarter, half = row & 3, (row >> 2) & 1
    zh, x = (row >> 3) & 3, (row >> 5) & 3
    at = (zh * 8 + x * 2) + ((row >> 7) ^ core)
    pair = (column == half * ROWS + at * 4 + quarter).astype(BF16)
    whole = (column == at * 8 + half * 4 + quarter).astype(BF16)
    return pair, whole


def low_body(tokens, cotangent, up_left, down_right, low, both):
    t, c = tokens[...], cotangent[...]
    both[:ROWS, :] = t
    both[ROWS:, :] = c
    low[:, :ROWS] = mm(t, up_left[...])
    low[:, ROWS:] = mt(c, down_right[...])


def main_body(
    scale, core, own, one, two, three, four, low, up, up_right, down, down_left,
    local, out_one, out_two, out_three, out_four, low_next, keep, send,
):
    arrived = (own, one, two, three, four)
    sent = (local, out_one, out_two, out_three, out_four)
    pair, whole = pick(core[0])
    low_up, low_cot = low[:, :ROWS], low[:, ROWS:]

    def put(at, value):
        value = (value * scale).astype(BF16)
        keep[:, at : at + value.shape[1]] = value[:ROWS]
        send[:, at : at + value.shape[1]] = value[ROWS:]

    hidden_parts = []
    low_down = jnp.zeros((ROWS, ROWS), F32)
    low_pre = jnp.zeros((ROWS, ROWS), F32)
    for b in range(BLOCKS):
        features = slice(b * ROWS, (b + 1) * ROWS)
        units = slice(b * SIDE, (b + 1) * SIDE)
        tok = [a[:ROWS, features] for a in arrived]
        cot = [a[ROWS:, features] for a in arrived]
        value = mm(low_up, up_right[:, units])
        grad = mt(low_cot, down_left[units, :])
        for k in range(FACTORS):
            value = value + mm(tok[k], up[k, b])
            grad = grad + mt(cot[k], down[k, b])
        phi = 0.5 + 0.5 * lax.erf(value * math.sqrt(0.5))
        density = jnp.exp(-0.5 * value * value) * (1.0 / math.sqrt(2.0 * math.pi))
        hidden = (value * phi).astype(BF16)
        pre = (grad * (phi + value * density)).astype(BF16)
        hidden_parts.append(hidden)
        for k in range(FACTORS):
            kind = sent[k].dtype
            sent[k][:ROWS, features] = mm(hidden, down[k, b]).astype(kind)
            sent[k][ROWS:, features] = mt(pre, up[k, b]).astype(kind)
        low_down = low_down + mm(hidden, down_left[units, :])
        low_pre = low_pre + mt(pre, up_right[:, units])
        left = tok + [low_up]
        for g in range(3):
            rows = jnp.concatenate([left[2 * g], left[2 * g + 1]], axis=1)
            put(g * GROUP + b * SIDE, mm(mt(pair, rows).astype(BF16), pre))
        rows = mt(whole, hidden).astype(BF16)
        put(DOWN_AT + b * FACTORS * ROWS, mm(rows, jnp.concatenate(cot, axis=1)))
    low_next[:, :ROWS] = low_down
    low_next[:, ROWS:] = low_pre
    zero = jnp.zeros_like(low_cot)
    upper = mt(pair, jnp.concatenate([low_cot, zero], axis=1)).astype(BF16)
    lower = mt(pair, jnp.concatenate([zero, low_cot], axis=1)).astype(BF16)
    put(
        LEFT_AT,
        mm(upper, jnp.concatenate(hidden_parts[:2], axis=1))
        + mm(lower, jnp.concatenate(hidden_parts[2:], axis=1)),
    )


def mini_body(scale, core, own, low, keep, send):
    pair, _ = pick(core[0])
    low_down, low_pre = low[:, :ROWS], low[:, ROWS:]
    zero = jnp.zeros_like(low_pre)
    upper = mt(pair, jnp.concatenate([low_pre, zero], axis=1)).astype(BF16)
    lower = mt(pair, jnp.concatenate([zero, low_down], axis=1)).astype(BF16)
    value = ((mm(upper, own[:ROWS, :]) + mm(lower, own[ROWS:, :])) * scale).astype(BF16)
    keep[...] = value[:ROWS]
    send[...] = value[ROWS:]


def last_body(local, one, two, three, four, low, up_left, down_right, out, grad):
    total = local[...]
    for a in (one, two, three, four):
        total = total + a[...].astype(F32)
    out[...] = (total[:ROWS] + mm(low[:, :ROWS], down_right[...])).astype(BF16)
    grad[...] = (total[ROWS:] + mt(low[:, ROWS:], up_left[...])).astype(BF16)


def unpack_body(parts, up, up_left, up_right, down, down_left, down_right):
    total = parts[0].astype(F32)
    for z in range(1, parts.shape[0]):
        total = total + parts[z].astype(F32)
    top, low = total[:4].astype(BF16), total[4:].astype(BF16)
    total = total.astype(BF16)
    for b in range(BLOCKS):
        for k in range(FACTORS):
            at = (k // 2) * GROUP + b * SIDE
            up[k, b] = (low if k % 2 else top)[:, at : at + SIDE]
            at = DOWN_AT + (b * FACTORS + k) * ROWS
            down[k, b] = total[:, at : at + ROWS]
    up_right[...] = low[:, 2 * GROUP : 3 * GROUP]
    down_left[:, :SLAB] = top[:, LEFT_AT:MAIN]
    down_left[:, SLAB:] = low[:, LEFT_AT:MAIN]
    up_left[...] = top[:, MAIN:]
    down_right[...] = low[:, MAIN:]


def call(body, outs, scalars=0, cost=(0, 0)):
    vmem = pl.BlockSpec(memory_space=pltpu.VMEM)
    smem = pl.BlockSpec(memory_space=pltpu.SMEM)

    def run(*args):
        return pl.pallas_call(
            body,
            out_shape=[jax.ShapeDtypeStruct(s, d) for s, d in outs],
            in_specs=[smem] * scalars + [vmem] * (len(args) - scalars),
            out_specs=[vmem] * len(outs),
            compiler_params=pltpu.CompilerParams(vmem_limit_bytes=LIMIT),
            cost_estimate=pl.CostEstimate(
                flops=cost[0], bytes_accessed=cost[1], transcendentals=0
            ),
        )(*args)

    return run


def swap(block, axis, mask):
    count = lax.axis_size(axis)
    return lax.ppermute(block, axis, [(i, i ^ mask) for i in range(count)])


def all_sum(partial):
    count = SIZES[3] * SIZES[4]
    pieces = partial.reshape(count, ROWS // count, 2 * ROWS)
    pieces = lax.all_to_all(pieces, TENSOR, 0, 0)
    piece = jnp.sum(pieces, axis=0).astype(BF16)
    pieces = jnp.broadcast_to(piece, pieces.shape)
    return lax.all_to_all(pieces, TENSOR, 0, 0).reshape(ROWS, 2 * ROWS)


def add(a, b):
    return (a.astype(F32) + b.astype(F32)).astype(BF16)


def over_x(block):
    pieces = block.reshape(SIZES[1], -1, block.shape[1])
    pieces = lax.all_to_all(pieces, "x", 0, 0)
    return jnp.sum(pieces.astype(F32), axis=0).astype(BF16)


def body(tokens, cotangent, up_blocks, up_left, up_right, down_blocks, down_left, down_right):
    scale = 1.0 / math.sqrt(ROWS * SIZES[0] * SIZES[1] * SIZES[2])
    core = lax.axis_index("core").astype(jnp.int32).reshape(1)
    wide = (2 * ROWS, SLAB)
    hops = (("y", 1), ("y", 2), ("zl", 1), ("zl", 2))

    low, own = call(
        low_body, [((ROWS, 2 * ROWS), F32), (wide, BF16)], cost=(40_000_000, 1_000_000)
    )(tokens, cotangent, up_left, down_right)
    arrived = [swap(own, axis, mask) for axis, mask in hops]
    low = all_sum(low)

    half = (ROWS, MAIN)
    local, *terms, low_next, keep, send = call(
        functools.partial(main_body, scale),
        [(wide, F32)] + [(wide, BF16)] * 4 + [((ROWS, 2 * ROWS), F32), (half, BF16), (half, BF16)],
        scalars=1,
        cost=(1_500_000_000, 10_000_000),
    )(core, own, *arrived, low, up_blocks, up_right, down_blocks, down_left)

    reduced = over_x(add(keep, swap(send, "core", 1)))
    terms = [swap(term, axis, mask) for term, (axis, mask) in zip(terms, hops)]
    low_next = all_sum(low_next)

    half = (ROWS, MINI)
    keep, send = call(
        functools.partial(mini_body, scale), [(half, BF16)] * 2, scalars=1, cost=(40_000_000, 1_000_000)
    )(core, own, low_next)
    mini = over_x(add(keep, swap(send, "core", 1)))

    out, tokens_grad = call(
        last_body, [((ROWS, SLAB), BF16)] * 2, cost=(40_000_000, 2_000_000)
    )(local, *terms, low_next, up_left, down_right)

    pieces = jnp.concatenate([reduced, mini], axis=1).reshape(SIZES[0], 8, MAIN + MINI)
    pieces = lax.all_to_all(pieces, "zh", 0, 0)
    up_g, up_left_g, up_right_g, down_g, down_left_g, down_right_g = call(
        unpack_body,
        [
            ((FACTORS, BLOCKS, 4, SIDE), BF16),
            ((4, SLAB), BF16),
            ((4, HIDDEN), BF16),
            ((FACTORS, BLOCKS, 8, ROWS), BF16),
            ((4, HIDDEN), BF16),
            ((4, SLAB), BF16),
        ],
        cost=(1_000_000, 1_000_000),
    )(pieces)
    return (out, tokens_grad, up_g, up_left_g.T, up_right_g, down_g, down_left_g.T, down_right_g)


def solution(mesh):
    fine = Mesh(mesh.devices.reshape(SIZES), DP + TENSOR)
    in_specs = (
        P(DP, TENSOR),
        P(DP, TENSOR),
        P(None, TENSOR, None, None),
        P(TENSOR, None),
        P(None, TENSOR),
        P(None, TENSOR, None, None),
        P(TENSOR, None),
        P(None, TENSOR),
    )
    out_specs = (
        P(DP, TENSOR),
        P(DP, TENSOR),
        P(None, TENSOR, DP, None),
        P(TENSOR, DP),
        P(DP, TENSOR),
        P(None, TENSOR, DP, None),
        P(TENSOR, DP),
        P(DP, TENSOR),
    )
    return jax.shard_map(body, mesh=fine, in_specs=in_specs, out_specs=out_specs, check_vma=False)
```

time: 665 us -> 166 us (0.25)
  waiting for transfers between devices: 336 us -> 49.4 us
  blocking collectives: 145 us -> 24.1 us
  matrix products: 48.6 us -> 0 us
  local copies, waits for them, and re-layouts: 48.2 us -> 7.49 us
  between operations: 15.2 us -> 0.82 us
  Pallas kernels: 0 us -> 10 us
    unnamed x4 -> x0, waiting for transfers between devices: 327 us -> none
    psum x2 -> x0, blocking collectives: 145 us -> none  [the longest x1 73.7 us: body(): lax.psum(jnp.dot(hidden, down_left, preferred_element_type=jnp.float32),...]
    dot_general x42 -> x0, matrix products: 48.6 us -> none  [the longest x20 19.7 us: blockwise(): jnp.einsum(form, pieces, blocks, preferred_element_type=jnp.float32)]
    all_to_all x0 -> x5, starting transfers between devices: none -> 35.7 us  [the longest x1 12.4 us: body(): pieces = lax.all_to_all(pieces, 'zh', 0, 0)]
    ppermute x16 -> x10, starting transfers between devices: 62 us -> 29.5 us  [swap(): return lax.ppermute(block, axis, [(i, i ^ mask) for i in range(count)])]
    all_to_all x0 -> x5, waiting for transfers between devices: none -> 27 us  [the longest x2 22.9 us: over_x(): pieces = lax.all_to_all(pieces, 'x', 0, 0)]
    reshape x22 -> x0, local copies, waits for them, and re-layouts: 26.1 us -> none  [the longest x20 24.8 us: blockwise(): return result.reshape(row_count, block_count * width_out)]
    all_to_all x0 -> x2, blocking collectives: none -> 24.1 us  [the longest x1 12.1 us: all_sum(): pieces = lax.all_to_all(pieces, TENSOR, 0, 0)]
  transfers between devices with their start and end apart: 18 -> 15, of which waited for: 3 -> 9; matrix products, arithmetic and copies ran while one was open for 11% -> 3% of each run, Pallas kernels for 0% -> 1%
where the time goes in v1:
time: 166 us; the launch traced here: 164 us
  starting transfers between devices  65.2 us (39%)
  waiting for transfers between devices  49.4 us (30%)
  blocking collectives  24.1 us (15%)
  Pallas kernels  10 us (6%)
  local copies, waits for them, and re-layouts  7.49 us (5%)
  other arithmetic  7.05 us (4%)
    ppermute x10, starting transfers between devices, swap(): return lax.ppermute(block, axis, [(i, i ^ mask) for i in range(count)])  29.5 us
    all_to_all x2, waiting for transfers between devices, over_x(): pieces = lax.all_to_all(pieces, 'x', 0, 0)  22.9 us
    ppermute x10, waiting for transfers between devices, swap(): return lax.ppermute(block, axis, [(i, i ^ mask) for i in range(count)])  22.4 us
    all_to_all x1, starting transfers between devices, body(): pieces = lax.all_to_all(pieces, 'zh', 0, 0)  12.4 us
    all_to_all x1, blocking collectives, all_sum(): pieces = lax.all_to_all(pieces, TENSOR, 0, 0)  12.1 us
    all_to_all x1, blocking collectives, all_sum(): return lax.all_to_all(pieces, TENSOR, 0, 0).reshape(ROWS, 2 * ROWS)  12 us
    pallas_call x5, Pallas kernels, run(): pl.pallas_call(body, out_shape=[jax.ShapeDtypeStruct(s, d) for s, d in ou...  10 us
    all_to_all x1, starting transfers between devices, all_sum(): pieces = lax.all_to_all(pieces, TENSOR, 0, 0)  8.91 us
  transfers between devices with their start and end apart: 15, of which 9 were waited for; matrix products, arithmetic and copies ran while one was open for 3% of the time, Pallas kernels for 1%

profile of v1, /device:TPU:24, one launch (start us, length us, event | category | flops | bytes accessed | tf_op | source)
XLA Modules:
  0.0 164.1 jit_solution(15498007355710067532)
XLA Ops:
  5.1 8.9 %all-to-all-start = ((f32[16,8,256]{2,1,0:T(8,128)}), f32[16,8,256]{2,1,0:T(8,128)S(1)}, u32[]{:S(2)}, u32[]{:S(2)}) async-start(f32[16,8,256]{2,1,0:T(8,128)} %bitcast.1), calls=%async_computation | async-start | bytes 262144 | tf_op jit(solution)/shard_map/all_to_all | solution.py:180
  14.0 4.3 %collective-permute-start.3 = (bf16[256,512]{1,0:T(8,128)(2,1)S(1)}, bf16[256,512]{1,0:T(8,128)(2,1)S(1)}, u32[]{:S(2)}, u32[]{:S(2)}) collective-permute-start(bf16[256,512]{1,0:T(8,128)(2,1)S(1)} %get-tuple-element.28.own), channel_id=1, source_target_pairs={{0,8},{4,12},{8,0},{12,4},{1,9},{5,13},{9,1},{13,5},{2,10},{6,14},... | collective-permute-start | bytes 786440 | tf_op jit(solution)/shard_map/ppermute | solution.py:174
  18.4 3.4 %collective-permute-start.2 = (bf16[256,512]{1,0:T(8,128)(2,1)S(1)}, bf16[256,512]{1,0:T(8,128)(2,1)S(1)}, u32[]{:S(2)}, u32[]{:S(2)}) collective-permute-start(bf16[256,512]{1,0:T(8,128)(2,1)S(1)} %get-tuple-element.28.own), channel_id=1, source_target_pairs={{0,4},{4,0},{8,12},{12,8},{1,5},{5,1},{9,13},{13,9},{2,6},{6,2},{1... | collective-permute-start | bytes 786440 | tf_op jit(solution)/shard_map/ppermute | solution.py:174
  21.8 3.4 %collective-permute-start.1 = (bf16[256,512]{1,0:T(8,128)(2,1)S(1)}, bf16[256,512]{1,0:T(8,128)(2,1)S(1)}, u32[]{:S(2)}, u32[]{:S(2)}) collective-permute-start(bf16[256,512]{1,0:T(8,128)(2,1)S(1)} %get-tuple-element.28.own), channel_id=1, source_target_pairs={{0,2},{1,3},{2,0},{3,1},{4,6},{5,7},{6,4},{7,5},{8,10},{9,11},{10,... | collective-permute-start | bytes 786440 | tf_op jit(solution)/shard_map/ppermute | solution.py:174
  25.1 1.9 %collective-permute-start = (bf16[256,512]{1,0:T(8,128)(2,1)S(1)}, bf16[256,512]{1,0:T(8,128)(2,1)S(1)}, u32[]{:S(2)}, u32[]{:S(2)}) collective-permute-start(bf16[256,512]{1,0:T(8,128)(2,1)S(1)} %get-tuple-element.28.own), channel_id=1, source_target_pairs={{0,1},{1,0},{2,3},{3,2},{4,5},{5,4},{6,7},{7,6},{8,9},{9,8},{10,11... | collective-permute-start | bytes 786440 | tf_op jit(solution)/shard_map/ppermute | solution.py:174
  27.7 6.0 %all-to-all-start.1 = ((bf16[16,8,256]{2,1,0:T(8,128)(2,1)}), bf16[16,8,256]{2,1,0:T(8,128)(2,1)S(1)}, u32[]{:S(2)}, u32[]{:S(2)}) async-start(bf16[16,8,256]{2,1,0:T(8,128)(2,1)} %broadcast_in_dim.6), calls=%async_computation.1 | async-start | bytes 131072 | tf_op jit(solution)/shard_map/all_to_all | solution.py:183
  35.6 4.1 %all-to-all-done.1 = bf16[16,8,256]{2,1,0:T(8,128)(2,1)S(1)} async-done(((bf16[16,8,256]{2,1,0:T(8,128)(2,1)}), bf16[16,8,256]{2,1,0:T(8,128)(2,1)S(1)}, u32[]{:S(2)}, u32[]{:S(2)}) %all-to-all-start.1) | async-done | bytes 65568 | tf_op jit(solution)/shard_map/all_to_all | solution.py:183
  42.9 7.1 %shard_map.144 = (f32[256,512]{1,0:T(8,128)S(1)}, bf16[256,512]{1,0:T(8,128)(2,1)S(1)}, bf16[256,512]{1,0:T(8,128)(2,1)S(1)}, bf16[256,512]{1,0:T(8,128)(2,1)S(1...) custom-call(s32[1]{0:T(128)} %bitcast.core, ...), custom_call_target="tpu_custom_call" | custom-call | flops 1500000000 | bytes 10000000 | tf_op jit(solution)/shard_map/pallas_call | solution.py:158
  50.1 2.0 %collective-permute-start.8 = (bf16[128,6144]{1,0:T(8,128)(2,1)}, bf16[128,6144]{1,0:T(8,128)(2,1)}, u32[]{:S(2)}, u32[]{:S(2)}) collective-permute-start(bf16[128,6144]{1,0:T(8,128)(2,1)} %get-tuple-element.39), channel_id=1, source_target_pairs={{0,16},{16,0},{1,17},{17,1},{2,18},{18,2},{3,19},{19,3},{4,20},{20... | collective-permute-start | bytes 4718600 | tf_op jit(solution)/shard_map/ppermute | solution.py:174
  52.1 12.1 %all_to_all.35 = f32[16,8,256]{2,1,0:T(8,128)} all-to-all(f32[16,8,256]{2,1,0:T(8,128)S(1)} %bitcast.13), channel_id=1, replica_groups=mesh['zh'=4,'x'=4,'core'=2,'zl'=4,'y'=4] {'zl','y'}, dimensions={0} | all-to-all | bytes 262144 | tf_op jit(solution)/shard_map/all_to_all | solution.py:180
  65.2 12.0 %all_to_all.36 = bf16[16,8,256]{2,1,0:T(8,128)(2,1)S(1)} all-to-all(bf16[16,8,256]{2,1,0:T(8,128)(2,1)S(1)} %broadcast_in_dim.7), channel_id=1, replica_groups=mesh['zh'=4,'x'=4,'core'=2,'zl'=4,'y'=4] {'zl','y'}, dimensions={0} | all-to-all | bytes 131072 | tf_op jit(solution)/shard_map/all_to_all | solution.py:183
  81.6 4.1 %all-to-all-start.5 = ((bf16[4,32,512]{2,1,0:T(8,128)(2,1)}), bf16[4,32,512]{2,1,0:T(8,128)(2,1)S(1)}, u32[]{:S(2)}, u32[]{:S(2)}) async-start(bf16[4,32,512]{2,1,0:T(8,128)(2,1)} %bitcast.6), calls=%async_computation.5 | async-start | bytes 262144 | tf_op jit(solution)/shard_map/all_to_all | solution.py:192
  85.6 2.9 %add_convert_fusion = bf16[128,6144]{1,0:T(8,128)(2,1)} fusion(bf16[128,6144]{1,0:T(8,128)(2,1)} %collective-permute-done.8, bf16[128,6144]{1,0:T(8,128)(2,1)S(1)} %copy-done.9), kind=kLoop, calls=%fused_computation | loop fusion | flops 3145728 | bytes 4718592 | tf_op jit(solution)/shard_map/convert_element_type | solution.py:187
  88.5 3.1 %all-to-all-done.5 = bf16[4,32,512]{2,1,0:T(8,128)(2,1)S(1)} async-done(((bf16[4,32,512]{2,1,0:T(8,128)(2,1)}), bf16[4,32,512]{2,1,0:T(8,128)(2,1)S(1)}, u32[]{:S(2)}, u32[]{:S(2)}) %all-to-all-start.5) | async-done | bytes 131104 | tf_op jit(solution)/shard_map/all_to_all | solution.py:192
  91.6 4.3 %all-to-all-start.4 = ((bf16[4,32,6144]{2,1,0:T(8,128)(2,1)}), bf16[4,32,6144]{2,1,0:T(8,128)(2,1)}, u32[]{:S(2)}, u32[]{:S(2)}) async-start(bf16[4,32,6144]{2,1,0:T(8,128)(2,1)} %bitcast.5), calls=%async_computation.4 | async-start | bytes 3145728 | tf_op jit(solution)/shard_map/all_to_all | solution.py:192
  96.0 19.9 %all-to-all-done.4 = bf16[4,32,6144]{2,1,0:T(8,128)(2,1)} async-done(((bf16[4,32,6144]{2,1,0:T(8,128)(2,1)}), bf16[4,32,6144]{2,1,0:T(8,128)(2,1)}, u32[]{:S(2)}, u32[]{:S(2)}) %all-to-all-start.4) | async-done | bytes 1572896 | tf_op jit(solution)/shard_map/all_to_all | solution.py:192
  118.4 12.4 %all-to-all-start.6 = ((bf16[4,8,6656]{2,1,0:T(8,128)(2,1)}), bf16[4,8,6656]{2,1,0:T(8,128)(2,1)S(1)}, u32[]{:S(2)}, u32[]{:S(2)}) async-start(bf16[4,8,6656]{2,1,0:T(8,128)(2,1)} %maximum_bitcast_fusion), calls=%async_computation.6 | async-start | bytes 851968 | tf_op jit(solution)/shard_map/all_to_all | solution.py:231
  130.8 2.7 %collective-permute-start.4 = (bf16[256,512]{1,0:T(8,128)(2,1)S(1)}, bf16[256,512]{1,0:T(8,128)(2,1)S(1)}, u32[]{:S(2)}, u32[]{:S(2)}) collective-permute-start(bf16[256,512]{1,0:T(8,128)(2,1)S(1)} %get-tuple-element.31), channel_id=1, source_target_pairs={{0,1},{1,0},{2,3},{3,2},{4,5},{5,4},{6,7},{7,6},{8,9},{9,8},{10,11... | collective-permute-start | bytes 786440 | tf_op jit(solution)/shard_map/ppermute | solution.py:174
  133.5 5.1 %collective-permute-start.5 = (bf16[256,512]{1,0:T(8,128)(2,1)S(1)}, bf16[256,512]{1,0:T(8,128)(2,1)S(1)}, u32[]{:S(2)}, u32[]{:S(2)}) collective-permute-start(bf16[256,512]{1,0:T(8,128)(2,1)S(1)} %get-tuple-element.32), channel_id=1, source_target_pairs={{0,2},{1,3},{2,0},{3,1},{4,6},{5,7},{6,4},{7,5},{8,10},{9,11},{10,... | collective-permute-start | bytes 786440 | tf_op jit(solution)/shard_map/ppermute | solution.py:174
  138.6 2.1 %collective-permute-start.6 = (bf16[256,512]{1,0:T(8,128)(2,1)S(1)}, bf16[256,512]{1,0:T(8,128)(2,1)S(1)}, u32[]{:S(2)}, u32[]{:S(2)}) collective-permute-start(bf16[256,512]{1,0:T(8,128)(2,1)S(1)} %get-tuple-element.33), channel_id=1, source_target_pairs={{0,4},{4,0},{8,12},{12,8},{1,5},{5,1},{9,13},{13,9},{2,6},{6,2},{1... | collective-permute-start | bytes 786440 | tf_op jit(solution)/shard_map/ppermute | solution.py:174
  140.6 2.7 %collective-permute-start.7 = (bf16[256,512]{1,0:T(8,128)(2,1)S(1)}, bf16[256,512]{1,0:T(8,128)(2,1)S(1)}, u32[]{:S(2)}, u32[]{:S(2)}) collective-permute-start(bf16[256,512]{1,0:T(8,128)(2,1)S(1)} %get-tuple-element.34), channel_id=1, source_target_pairs={{0,8},{4,12},{8,0},{12,4},{1,9},{5,13},{9,1},{13,5},{2,10},{6,14},... | collective-permute-start | bytes 786440 | tf_op jit(solution)/shard_map/ppermute | solution.py:174
  143.3 2.6 %collective-permute-done.5.two = bf16[256,512]{1,0:T(8,128)(2,1)S(1)} collective-permute-done((bf16[256,512]{1,0:T(8,128)(2,1)S(1)}, bf16[256,512]{1,0:T(8,128)(2,1)S(1)}, u32[]{:S(2)}, u32[]{:S(2)}) %collective-permute-start.5) | collective-permute-done | bytes 262176 | tf_op jit(solution)/shard_map/ppermute | solution.py:174
  145.9 12.9 %collective-permute-done.6.three = bf16[256,512]{1,0:T(8,128)(2,1)S(1)} collective-permute-done((bf16[256,512]{1,0:T(8,128)(2,1)S(1)}, bf16[256,512]{1,0:T(8,128)(2,1)S(1)}, u32[]{:S(2)}, u32[]{:S(2)}) %collective-permute-start.6) | collective-permute-done | bytes 262176 | tf_op jit(solution)/shard_map/ppermute | solution.py:174
  158.8 3.7 %collective-permute-done.7.four = bf16[256,512]{1,0:T(8,128)(2,1)S(1)} collective-permute-done((bf16[256,512]{1,0:T(8,128)(2,1)S(1)}, bf16[256,512]{1,0:T(8,128)(2,1)S(1)}, u32[]{:S(2)}, u32[]{:S(2)}) %collective-permute-start.7) | collective-permute-done | bytes 262176 | tf_op jit(solution)/shard_map/ppermute | solution.py:174
  (42 shorter events, 19.7 us)
Async XLA Ops:
  0.6 0.9 copy-start
  1.5 0.9 copy-start.2
  2.4 0.9 copy-start.4
  5.1 21.9 %all-to-all-start = ((f32[16,8,256]{2,1,0:T(8,128)}), f32[16,8,256]{2,1,0:T(8,128)S(1)}, u32[]{:S(2)}, u32[]{:S(2)}) async-start(f32[16,8,256]{2,1,0:T(8,128)} %bitcast.1), calls=%async_computation | async-start | bytes 262144 | tf_op jit(solution)/shard_map/all_to_all | solution.py:180
  14.0 19.7 %collective-permute-start.3 = (bf16[256,512]{1,0:T(8,128)(2,1)S(1)}, bf16[256,512]{1,0:T(8,128)(2,1)S(1)}, u32[]{:S(2)}, u32[]{:S(2)}) collective-permute-start(bf16[256,512]{1,0:T(8,128)(2,1)S(1)} %get-tuple-element.28.own), channel_id=1, source_target_pairs={{0,8},{4,12},{8,0},{12,4},{1,9},{5,13},{9,1},{13,5},{2,10},{6,14},... | collective-permute-start | bytes 786440 | tf_op jit(solution)/shard_map/ppermute | solution.py:174
  18.4 15.4 %collective-permute-start.2 = (bf16[256,512]{1,0:T(8,128)(2,1)S(1)}, bf16[256,512]{1,0:T(8,128)(2,1)S(1)}, u32[]{:S(2)}, u32[]{:S(2)}) collective-permute-start(bf16[256,512]{1,0:T(8,128)(2,1)S(1)} %get-tuple-element.28.own), channel_id=1, source_target_pairs={{0,4},{4,0},{8,12},{12,8},{1,5},{5,1},{9,13},{13,9},{2,6},{6,2},{1... | collective-permute-start | bytes 786440 | tf_op jit(solution)/shard_map/ppermute | solution.py:174
  21.8 12.6 %collective-permute-start.1 = (bf16[256,512]{1,0:T(8,128)(2,1)S(1)}, bf16[256,512]{1,0:T(8,128)(2,1)S(1)}, u32[]{:S(2)}, u32[]{:S(2)}) collective-permute-start(bf16[256,512]{1,0:T(8,128)(2,1)S(1)} %get-tuple-element.28.own), channel_id=1, source_target_pairs={{0,2},{1,3},{2,0},{3,1},{4,6},{5,7},{6,4},{7,5},{8,10},{9,11},{10,... | collective-permute-start | bytes 786440 | tf_op jit(solution)/shard_map/ppermute | solution.py:174
  25.1 10.5 %collective-permute-start = (bf16[256,512]{1,0:T(8,128)(2,1)S(1)}, bf16[256,512]{1,0:T(8,128)(2,1)S(1)}, u32[]{:S(2)}, u32[]{:S(2)}) collective-permute-start(bf16[256,512]{1,0:T(8,128)(2,1)S(1)} %get-tuple-element.28.own), channel_id=1, source_target_pairs={{0,1},{1,0},{2,3},{3,2},{4,5},{5,4},{6,7},{7,6},{8,9},{9,8},{10,11... | collective-permute-start | bytes 786440 | tf_op jit(solution)/shard_map/ppermute | solution.py:174
  27.7 12.0 %all-to-all-start.1 = ((bf16[16,8,256]{2,1,0:T(8,128)(2,1)}), bf16[16,8,256]{2,1,0:T(8,128)(2,1)S(1)}, u32[]{:S(2)}, u32[]{:S(2)}) async-start(bf16[16,8,256]{2,1,0:T(8,128)(2,1)} %broadcast_in_dim.6), calls=%async_computation.1 | async-start | bytes 131072 | tf_op jit(solution)/shard_map/all_to_all | solution.py:183
  39.7 1.3 copy-start.6
  41.0 0.9 copy-start.7
  42.0 0.9 copy-start.8
  50.1 35.5 %copy-start.9 = (bf16[128,6144]{1,0:T(8,128)(2,1)S(1)}, bf16[128,6144]{1,0:T(8,128)(2,1)}, u32[]{:S(2)}) copy-start(bf16[128,6144]{1,0:T(8,128)(2,1)} %get-tuple-element.38) | copy-start | bytes 4718596
  50.1 35.5 %collective-permute-start.8 = (bf16[128,6144]{1,0:T(8,128)(2,1)}, bf16[128,6144]{1,0:T(8,128)(2,1)}, u32[]{:S(2)}, u32[]{:S(2)}) collective-permute-start(bf16[128,6144]{1,0:T(8,128)(2,1)} %get-tuple-element.39), channel_id=1, source_target_pairs={{0,16},{16,0},{1,17},{17,1},{2,18},{18,2},{3,19},{19,3},{4,20},{20... | collective-permute-start | bytes 4718600 | tf_op jit(solution)/shard_map/ppermute | solution.py:174
  77.6 3.2 %collective-permute-start.9 = (bf16[128,512]{1,0:T(8,128)(2,1)S(1)}, bf16[128,512]{1,0:T(8,128)(2,1)S(1)}, u32[]{:S(2)}, u32[]{:S(2)}) collective-permute-start(bf16[128,512]{1,0:T(8,128)(2,1)S(1)} %get-tuple-element.41), channel_id=1, source_target_pairs={{0,16},{16,0},{1,17},{17,1},{2,18},{18,2},{3,19},{19,3},{4,20},{20... | collective-permute-start | bytes 393224 | tf_op jit(solution)/shard_map/ppermute | solution.py:174
  81.6 10.0 %all-to-all-start.5 = ((bf16[4,32,512]{2,1,0:T(8,128)(2,1)}), bf16[4,32,512]{2,1,0:T(8,128)(2,1)S(1)}, u32[]{:S(2)}, u32[]{:S(2)}) async-start(bf16[4,32,512]{2,1,0:T(8,128)(2,1)} %bitcast.6), calls=%async_computation.5 | async-start | bytes 262144 | tf_op jit(solution)/shard_map/all_to_all | solution.py:192
  91.6 24.3 %all-to-all-start.4 = ((bf16[4,32,6144]{2,1,0:T(8,128)(2,1)}), bf16[4,32,6144]{2,1,0:T(8,128)(2,1)}, u32[]{:S(2)}, u32[]{:S(2)}) async-start(bf16[4,32,6144]{2,1,0:T(8,128)(2,1)} %bitcast.5), calls=%async_computation.4 | async-start | bytes 3145728 | tf_op jit(solution)/shard_map/all_to_all | solution.py:192
  96.0 66.5 %copy-start.1 = (bf16[512,128]{1,0:T(8,128)(2,1)S(1)}, bf16[512,128]{1,0:T(8,128)(2,1)}, u32[]{:S(2)}) copy-start(bf16[512,128]{1,0:T(8,128)(2,1)} %up_left.3) | copy-start | bytes 393220
  96.0 66.5 %copy-start.3 = (bf16[128,512]{1,0:T(8,128)(2,1)S(1)}, bf16[128,512]{1,0:T(8,128)(2,1)}, u32[]{:S(2)}) copy-start(bf16[128,512]{1,0:T(8,128)(2,1)} %down_right.3) | copy-start | bytes 393220
  118.4 45.1 %all-to-all-start.6 = ((bf16[4,8,6656]{2,1,0:T(8,128)(2,1)}), bf16[4,8,6656]{2,1,0:T(8,128)(2,1)S(1)}, u32[]{:S(2)}, u32[]{:S(2)}) async-start(bf16[4,8,6656]{2,1,0:T(8,128)(2,1)} %maximum_bitcast_fusion), calls=%async_computation.6 | async-start | bytes 851968 | tf_op jit(solution)/shard_map/all_to_all | solution.py:231
  130.8 12.6 %collective-permute-start.4 = (bf16[256,512]{1,0:T(8,128)(2,1)S(1)}, bf16[256,512]{1,0:T(8,128)(2,1)S(1)}, u32[]{:S(2)}, u32[]{:S(2)}) collective-permute-start(bf16[256,512]{1,0:T(8,128)(2,1)S(1)} %get-tuple-element.31), channel_id=1, source_target_pairs={{0,1},{1,0},{2,3},{3,2},{4,5},{5,4},{6,7},{7,6},{8,9},{9,8},{10,11... | collective-permute-start | bytes 786440 | tf_op jit(solution)/shard_map/ppermute | solution.py:174
  133.5 12.5 %collective-permute-start.5 = (bf16[256,512]{1,0:T(8,128)(2,1)S(1)}, bf16[256,512]{1,0:T(8,128)(2,1)S(1)}, u32[]{:S(2)}, u32[]{:S(2)}) collective-permute-start(bf16[256,512]{1,0:T(8,128)(2,1)S(1)} %get-tuple-element.32), channel_id=1, source_target_pairs={{0,2},{1,3},{2,0},{3,1},{4,6},{5,7},{6,4},{7,5},{8,10},{9,11},{10,... | collective-permute-start | bytes 786440 | tf_op jit(solution)/shard_map/ppermute | solution.py:174
  138.6 20.2 %collective-permute-start.6 = (bf16[256,512]{1,0:T(8,128)(2,1)S(1)}, bf16[256,512]{1,0:T(8,128)(2,1)S(1)}, u32[]{:S(2)}, u32[]{:S(2)}) collective-permute-start(bf16[256,512]{1,0:T(8,128)(2,1)S(1)} %get-tuple-element.33), channel_id=1, source_target_pairs={{0,4},{4,0},{8,12},{12,8},{1,5},{5,1},{9,13},{13,9},{2,6},{6,2},{1... | collective-permute-start | bytes 786440 | tf_op jit(solution)/shard_map/ppermute | solution.py:174
  140.6 21.9 %collective-permute-start.7 = (bf16[256,512]{1,0:T(8,128)(2,1)S(1)}, bf16[256,512]{1,0:T(8,128)(2,1)S(1)}, u32[]{:S(2)}, u32[]{:S(2)}) collective-permute-start(bf16[256,512]{1,0:T(8,128)(2,1)S(1)} %get-tuple-element.34), channel_id=1, source_target_pairs={{0,8},{4,12},{8,0},{12,4},{1,9},{5,13},{9,1},{13,5},{2,10},{6,14},... | collective-permute-start | bytes 786440 | tf_op jit(solution)/shard_map/ppermute | solution.py:174
  (1 other events, 0.9 us)

commit v2 on v1

v2 whole, which is shorter than its diff:
```python
import functools
import math

import jax
import jax.numpy as jnp
from jax import lax
from jax.experimental import pallas as pl
from jax.experimental.pallas import tpu as pltpu
from jax.sharding import Mesh
from jax.sharding import PartitionSpec as P

DP = ("zh", "x", "core")
TENSOR = ("zl", "y")
SIZES = (4, 4, 2, 4, 4)
ROWS = 128
SIDE = 256
SLAB = 512
HIDDEN = 1024
BLOCKS = 4
FACTORS = 5
F32 = jnp.float32
BF16 = jnp.bfloat16

GROUP = BLOCKS * SIDE
DOWN_AT = 3 * GROUP
LEFT_AT = DOWN_AT + BLOCKS * FACTORS * ROWS
MAIN = LEFT_AT + SLAB
MINI = SLAB
LOW = ROWS // 2
LIMIT = 24 * 1024 * 1024


def mm(a, b):
    return lax.dot_general(a, b, (((1,), (0,)), ((), ())), preferred_element_type=F32)


def mt(a, b):
    return lax.dot_general(a, b, (((1,), (1,)), ((), ())), preferred_element_type=F32)


def pick(place):
    core, x_here, z_here = place[0], place[2], place[3]
    row = lax.broadcasted_iota(jnp.int32, (SIDE, SIDE), 0)
    column = lax.broadcasted_iota(jnp.int32, (SIDE, SIDE), 1)
    quarter, half = row & 3, (row >> 2) & 1
    zh, x = (row >> 3) & 3, (row >> 5) & 3
    at = (zh ^ z_here) * 8 + (x ^ x_here) * 2 + ((row >> 7) ^ core)
    pair = (column == half * ROWS + at * 4 + quarter).astype(BF16)
    whole = (column == at * 8 + half * 4 + quarter).astype(BF16)
    return pair, whole


def pick_mini():
    row = lax.broadcasted_iota(jnp.int32, (SIDE, SIDE), 0)
    column = lax.broadcasted_iota(jnp.int32, (SIDE, SIDE), 1)
    quarter, half = row & 3, (row >> 2) & 1
    at = ((row >> 3) & 3) * 8 + (row >> 5)
    return (column == half * ROWS + at * 4 + quarter).astype(BF16)


class Copies:
    def __init__(self, sems):
        self.sems, self.count = sems, 0

    def start(self, source, target):
        copy = pltpu.make_async_copy(source, target, self.sems.at[self.count])
        self.count += 1
        copy.start()
        return copy


def finish(copies):
    for copy in copies:
        copy.wait()


def fold(low):
    return jnp.concatenate([low[:LOW], low[LOW:]], axis=1).astype(BF16)


def unfold(pieces):
    total = pieces[0].astype(F32)
    for n in range(1, 4):
        total = total + pieces[n].astype(F32)
    total = total.astype(BF16)
    first = jnp.concatenate([total[:, :ROWS], total[:, 2 * ROWS : 3 * ROWS]], axis=0)
    second = jnp.concatenate([total[:, ROWS : 2 * ROWS], total[:, 3 * ROWS :]], axis=0)
    return first, second


def low_body(tokens, cotangent, up_left, down_right, own, packed, both, low, u, d, sems):
    copies = Copies(sems)
    t, c = both.at[:ROWS], both.at[ROWS:]
    first = [copies.start(tokens, t), copies.start(up_left, u)]
    second = [copies.start(cotangent, c), copies.start(down_right, d)]
    finish(first)
    low_up = mm(t[...], u[...])
    finish(second)
    sent = [copies.start(both, own)]
    sent += [copies.start(both, packed.at[n, : 2 * ROWS]) for n in range(4)]
    low_cot = mt(c[...], d[...])
    low[...] = fold(jnp.concatenate([low_up, low_cot], axis=1))
    sent += [copies.start(low, packed.at[n, 2 * ROWS :]) for n in range(4)]
    finish(sent)


def spread_body(near, out, pieces, total, sems):
    copies = Copies(sems)
    copies.start(near.at[:, 2 * ROWS :], pieces).wait()
    value = pieces[0].astype(F32)
    for n in range(1, 4):
        value = value + pieces[n].astype(F32)
    total[...] = value.astype(BF16)
    finish([copies.start(total, out.at[n]) for n in range(4)])


def main_body(
    scale, place, near_hbm, three_hbm, four_hbm, low_hbm, up_hbm, up_right_hbm, down_hbm, down_left_hbm,
    local_out, packed_out, three_out, four_out, keep_out, send_out,
    arrived, low, up, up_right, down, down_left, local, sent, low_next, keep, send, sems,
):
    copies = Copies(sems)
    y = place[1]
    wide = slice(0, 2 * ROWS)
    first = [
        copies.start(low_hbm, low),
        copies.start(up_right_hbm, up_right),
        copies.start(down_left_hbm, down_left),
        copies.start(near_hbm.at[y, wide], arrived.at[0]),
        copies.start(near_hbm.at[y ^ 1, wide], arrived.at[1]),
        copies.start(near_hbm.at[y ^ 2, wide], arrived.at[2]),
        copies.start(three_hbm, arrived.at[3]),
        copies.start(four_hbm, arrived.at[4]),
    ]
    blocks = [
        (copies.start(up_hbm.at[:, b], up.at[:, b]), copies.start(down_hbm.at[:, b], down.at[:, b]))
        for b in range(BLOCKS)
    ]
    pair, whole = pick(place)
    out_going = []

    def put(at, value):
        value = (value * scale).astype(BF16)
        columns = slice(at, at + value.shape[1])
        keep[:, columns] = value[:ROWS]
        send[:, columns] = value[ROWS:]
        out_going.append(copies.start(send.at[:, columns], send_out.at[:, columns]))
        out_going.append(copies.start(keep.at[:, columns], keep_out.at[:, columns]))

    finish(first)
    low_up, low_cot = unfold(low)
    hiddens, pres = [], []
    low_down = jnp.zeros((ROWS, ROWS), F32)
    low_pre = jnp.zeros((ROWS, ROWS), F32)
    for b in range(BLOCKS):
        features = slice(b * ROWS, (b + 1) * ROWS)
        units = slice(b * SIDE, (b + 1) * SIDE)
        tok = [arrived[k, :ROWS, features] for k in range(FACTORS)]
        cot = [arrived[k, ROWS:, features] for k in range(FACTORS)]
        value = mm(low_up, up_right[:, units])
        grad = mt(low_cot, down_left[units, :])
        finish(blocks[b])
        for k in range(FACTORS):
            value = value + mm(tok[k], up[k, b])
            grad = grad + mt(cot[k], down[k, b])
        phi = 0.5 + 0.5 * lax.erf(value * math.sqrt(0.5))
        density = jnp.exp(-0.5 * value * value) * (1.0 / math.sqrt(2.0 * math.pi))
        hidden = (value * phi).astype(BF16)
        pre = (grad * (phi + value * density)).astype(BF16)
        hiddens.append(hidden)
        pres.append(pre)
        left = tok + [low_up]
        for g in range(3):
            rows = jnp.concatenate([left[2 * g], left[2 * g + 1]], axis=1)
            put(g * GROUP + b * SIDE, mm(mt(pair, rows).astype(BF16), pre))
        rows = mt(whole, hidden).astype(BF16)
        put(DOWN_AT + b * FACTORS * ROWS, mm(rows, jnp.concatenate(cot, axis=1)))
    zero = jnp.zeros_like(low_cot)
    upper = mt(pair, jnp.concatenate([low_cot, zero], axis=1)).astype(BF16)
    lower = mt(pair, jnp.concatenate([zero, low_cot], axis=1)).astype(BF16)
    put(
        LEFT_AT,
        mm(upper, jnp.concatenate(hiddens[:2], axis=1))
        + mm(lower, jnp.concatenate(hiddens[2:], axis=1)),
    )
    for b in range(BLOCKS):
        features = slice(b * ROWS, (b + 1) * ROWS)
        units = slice(b * SIDE, (b + 1) * SIDE)
        hidden, pre = hiddens[b], pres[b]
        low_down = low_down + mm(hidden, down_left[units, :])
        low_pre = low_pre + mt(pre, up_right[:, units])
        for k in range(FACTORS):
            upper, lower = mm(hidden, down[k, b]), mt(pre, up[k, b])
            if k:
                sent[k - 1, :ROWS, features] = upper.astype(BF16)
                sent[k - 1, ROWS:, features] = lower.astype(BF16)
            else:
                local[:ROWS, features] = upper
                local[ROWS:, features] = lower
    low_next[...] = fold(jnp.concatenate([low_down, low_pre], axis=1))
    out_going += [
        copies.start(sent.at[0], packed_out.at[y ^ 1, wide]),
        copies.start(sent.at[1], packed_out.at[y ^ 2, wide]),
        copies.start(sent.at[2], three_out),
        copies.start(sent.at[3], four_out),
        copies.start(local, local_out),
    ]
    out_going += [copies.start(sent.at[0], packed_out.at[y, wide])]
    out_going += [copies.start(sent.at[1], packed_out.at[y ^ 3, wide])]
    out_going += [copies.start(low_next, packed_out.at[n, 2 * ROWS :]) for n in range(4)]
    finish(out_going)


def mini_body(scale, own_hbm, pieces_hbm, low, mini, own, pieces, sems):
    copies = Copies(sems)
    first = [copies.start(pieces_hbm, pieces), copies.start(own_hbm, own)]
    pair = pick_mini()
    finish(first)
    low_down, low_pre = unfold(pieces)
    low[:, :ROWS] = low_down
    low[:, ROWS:] = low_pre
    zero = jnp.zeros_like(low_pre)
    upper = mt(pair, jnp.concatenate([low_pre, zero], axis=1)).astype(BF16)
    lower = mt(pair, jnp.concatenate([zero, low_down], axis=1)).astype(BF16)
    value = mm(upper, own[:ROWS, :]) + mm(lower, own[ROWS:, :])
    mini[...] = (value * scale).astype(BF16)


def last_body(
    place, local_hbm, near, three, four, low_hbm, up_left_hbm, down_right_hbm, out, grad,
    local, terms, low, up_left, down_right, sems,
):
    copies = Copies(sems)
    y = place[1]
    wide = slice(0, 2 * ROWS)
    finish([
        copies.start(local_hbm, local),
        copies.start(near.at[y ^ 1, wide], terms.at[0]),
        copies.start(near.at[y ^ 2, wide], terms.at[1]),
        copies.start(three, terms.at[2]),
        copies.start(four, terms.at[3]),
        copies.start(low_hbm, low),
        copies.start(up_left_hbm, up_left),
        copies.start(down_right_hbm, down_right),
    ])
    total = local[...]
    for n in range(4):
        total = total + terms[n].astype(F32)
    out[...] = (total[:ROWS] + mm(low[:, :ROWS], down_right[...])).astype(BF16)
    grad[...] = (total[ROWS:] + mt(low[:, ROWS:], up_left[...])).astype(BF16)


def split_body(a, b, *outs):
    rows = a.shape[0] // len(outs)
    for n, out in enumerate(outs):
        part = slice(n * rows, (n + 1) * rows)
        out[...] = (a[part, :].astype(F32) + b[part, :].astype(F32)).astype(BF16)


def join_body(a, b, c, d, *outs):
    rows = a.shape[0] // len(outs)
    for n, out in enumerate(outs):
        part = slice(n * rows, (n + 1) * rows)
        total = a[part, :].astype(F32) + b[part, :].astype(F32)
        total = total + c[part, :].astype(F32) + d[part, :].astype(F32)
        out[...] = total.astype(BF16)


def unpack_body(one, two, three, four, mini, up, up_left, up_right, down, down_left, down_right):
    total, small = one[...].astype(F32), mini[0].astype(F32)
    for part in (two, three, four):
        total = total + part[...].astype(F32)
    for z in range(1, mini.shape[0]):
        small = small + mini[z].astype(F32)
    top, low = total[:4].astype(BF16), total[4:].astype(BF16)
    total = total.astype(BF16)
    for b in range(BLOCKS):
        for k in range(FACTORS):
            at = (k // 2) * GROUP + b * SIDE
            up[k, b] = (low if k % 2 else top)[:, at : at + SIDE]
            at = DOWN_AT + (b * FACTORS + k) * ROWS
            down[k, b] = total[:, at : at + ROWS]
    up_right[...] = low[:, 2 * GROUP : 3 * GROUP]
    down_left[:, :SLAB] = top[:, LEFT_AT:MAIN]
    down_left[:, SLAB:] = low[:, LEFT_AT:MAIN]
    up_left[...] = small[:4].astype(BF16)
    down_right[...] = small[4:].astype(BF16)


SPACES = {"s": pltpu.SMEM, "v": pltpu.VMEM, "h": pltpu.HBM, "a": pl.ANY}


def call(body, outs, kinds, scratch=(), copies=0, cost=(0, 0)):
    kinds, kinds_out = kinds.split()
    sems = [pltpu.SemaphoreType.DMA((copies,))] if copies else []

    def run(*args):
        args = [
            pltpu.with_memory_space_constraint(a, pltpu.HBM) if k == "h" else a
            for a, k in zip(args, kinds)
        ]
        return pl.pallas_call(
            body,
            out_shape=[jax.ShapeDtypeStruct(s, d) for s, d in outs],
            in_specs=[pl.BlockSpec(memory_space=SPACES[k]) for k in kinds],
            out_specs=[pl.BlockSpec(memory_space=SPACES[k]) for k in kinds_out],
            scratch_shapes=[pltpu.VMEM(s, d) for s, d in scratch] + sems,
            compiler_params=pltpu.CompilerParams(vmem_limit_bytes=LIMIT),
            cost_estimate=pl.CostEstimate(
                flops=cost[0], bytes_accessed=cost[1], transcendentals=0
            ),
        )(*args)

    return run


def in_columns(body, rows_in, rows_out, width, steps, flops=1_000_000):
    spec = lambda rows: pl.BlockSpec((rows, width // steps), lambda i: (0, i))
    return pl.pallas_call(
        body,
        out_shape=[jax.ShapeDtypeStruct((rows, width), BF16) for rows in rows_out],
        grid=(steps,),
        in_specs=[spec(rows) for rows in rows_in],
        out_specs=[spec(rows) for rows in rows_out],
        compiler_params=pltpu.CompilerParams(vmem_limit_bytes=LIMIT),
        cost_estimate=pl.CostEstimate(flops=flops, bytes_accessed=4_000_000, transcendentals=0),
    )


def spread(packed):
    shape = (4, LOW, SLAB)
    return call(
        spread_body, [(shape, BF16)], "a a", [(shape, BF16), (shape[1:], BF16)], 5, cost=(1_000_000, 500_000)
    )(packed)[0]


def swap(block, axis, mask):
    count = lax.axis_size(axis)
    return lax.ppermute(block, axis, [(i, i ^ mask) for i in range(count)])


def exchange(block, axis):
    return lax.all_to_all(block, axis, 0, 0)


def add(a, b):
    return (a.astype(F32) + b.astype(F32)).astype(BF16)


def total_of(pieces):
    return jnp.sum(pieces.astype(F32), axis=0).astype(BF16)


def body(tokens, cotangent, up_blocks, up_left, up_right, down_blocks, down_left, down_right):
    scale = 1.0 / math.sqrt(ROWS * SIZES[0] * SIZES[1] * SIZES[2])
    index = lax.axis_index
    place = jnp.stack([index("core"), index("y"), index("x"), index("zh")]).astype(jnp.int32)
    wide, chunks = (2 * ROWS, SLAB), (4, 2 * ROWS + LOW, SLAB)
    shape = lambda a: (a.shape, a.dtype)

    own, packed = call(
        low_body,
        [(wide, BF16), (chunks, BF16)],
        "hhhh aa",
        [(wide, BF16), ((LOW, SLAB), BF16), shape(up_left), shape(down_right)],
        13,
        cost=(40_000_000, 2_000_000),
    )(tokens, cotangent, up_left, down_right)
    near = exchange(packed, "y")
    far = [swap(own, "zl", mask) for mask in (1, 2)]
    low = exchange(spread(near), "zl")

    half = (ROWS, MAIN)
    weights = (up_blocks, up_right, down_blocks, down_left)
    local, packed, *far, keep, send = call(
        functools.partial(main_body, scale),
        [(wide, F32), (chunks, BF16), (wide, BF16), (wide, BF16), (half, BF16), (half, BF16)],
        "saaaahhhh aaaaaa",
        [((FACTORS, *wide), BF16), shape(low)]
        + [shape(a) for a in weights]
        + [(wide, F32), ((FACTORS - 1, *wide), BF16), ((LOW, SLAB), BF16), (half, BF16), (half, BF16)],
        64,
        cost=(1_500_000_000, 10_000_000),
    )(place, near, *far, low, *weights)

    got = swap(send, "core", 1)
    pieces = in_columns(split_body, [ROWS] * 2, [32] * 4, MAIN, 4)(keep, got)
    packed, far, pieces = lax.optimization_barrier((packed, far, pieces))
    pieces = list(pieces[:1]) + [swap(pieces[mask], "x", mask) for mask in (1, 2, 3)]
    far = [swap(term, "zl", mask) for term, mask in zip(far, (1, 2))]
    near = exchange(packed, "y")
    low = exchange(spread(near), "zl")

    pieces, far = lax.optimization_barrier((pieces, far))
    pieces = in_columns(join_body, [32] * 4, [8] * 4, MAIN, 2, 30_000_000_000)(*pieces)
    low, pieces = lax.optimization_barrier((low, pieces))
    pieces = list(pieces[:1]) + [swap(pieces[mask], "zh", mask) for mask in (1, 2, 3)]

    low, mini = call(
        functools.partial(mini_body, scale),
        [((ROWS, 2 * ROWS), BF16), ((2 * ROWS, MINI), BF16)],
        "aa vv",
        [shape(own), shape(low)],
        2,
        cost=(40_000_000, 1_000_000),
    )(own, low)
    mini = total_of(exchange(mini.reshape(8, -1, MINI), ("x", "core")))
    mini = exchange(mini.reshape(SIZES[0], 8, MINI), "zh")

    out, tokens_grad = call(
        last_body,
        [((ROWS, SLAB), BF16)] * 2,
        "saaaaahh vv",
        [(wide, F32), ((4, *wide), BF16), shape(low), shape(up_left), shape(down_right)],
        8,
        cost=(40_000_000, 2_000_000),
    )(place, local, near, *far, low, up_left, down_right)

    up_g, up_left_g, up_right_g, down_g, down_left_g, down_right_g = call(
        unpack_body,
        [
            ((FACTORS, BLOCKS, 4, SIDE), BF16),
            ((4, SLAB), BF16),
            ((4, HIDDEN), BF16),
            ((FACTORS, BLOCKS, 8, ROWS), BF16),
            ((4, HIDDEN), BF16),
            ((4, SLAB), BF16),
        ],
        "vvvvv vvvvvv",
        cost=(1_000_000, 1_000_000),
    )(*pieces, mini)
    return (out, tokens_grad, up_g, up_left_g.T, up_right_g, down_g, down_left_g.T, down_right_g)


def solution(mesh):
    fine = Mesh(mesh.devices.reshape(SIZES), DP + TENSOR)
    in_specs = (
        P(DP, TENSOR),
        P(DP, TENSOR),
        P(None, TENSOR, None, None),
        P(TENSOR, None),
        P(None, TENSOR),
        P(None, TENSOR, None, None),
        P(TENSOR, None),
        P(None, TENSOR),
    )
    out_specs = (
        P(DP, TENSOR),
        P(DP, TENSOR),
        P(None, TENSOR, DP, None),
        P(TENSOR, DP),
        P(DP, TENSOR),
        P(None, TENSOR, DP, None),
        P(TENSOR, DP),
        P(DP, TENSOR),
    )
    return jax.shard_map(body, mesh=fine, in_specs=in_specs, out_specs=out_specs, check_vma=False)
```

time: 166 us -> 168 us (1.012)
  Pallas kernels: 10 us -> 22.5 us
  waiting for transfers between devices: 49.4 us -> 39.4 us
  starting transfers between devices: 65.2 us -> 75.1 us
  other arithmetic: 7.05 us -> 0.73 us
  blocking collectives: 24.1 us -> 20.3 us
    ppermute x10 -> x11, starting transfers between devices: 29.5 us -> 46.4 us  [swap(): return lax.ppermute(block, axis, [(i, i ^ mask) for i in range(count)])]
    all_to_all x5, waiting for transfers between devices: 27 us -> 11 us  [exchange(): return lax.all_to_all(block, axis, 0, 0)]
    pallas_call x5 -> x7, Pallas kernels: 10 us -> 20.2 us  [run(): pl.pallas_call(body, out_shape=[jax.ShapeDtypeStruct(s, d) for s, d in ou...]
    all_to_all x5, starting transfers between devices: 35.7 us -> 28.6 us  [exchange(): return lax.all_to_all(block, axis, 0, 0)]
    ppermute x10 -> x11, waiting for transfers between devices: 22.4 us -> 28.4 us  [swap(): return lax.ppermute(block, axis, [(i, i ^ mask) for i in range(count)])]
    all_to_all x2 -> x1, blocking collectives: 24.1 us -> 20.3 us  [exchange(): return lax.all_to_all(block, axis, 0, 0)]
    convert_element_type x2 -> x0, other arithmetic: 3.6 us -> none  [add(): return (a.astype(F32) + b.astype(F32)).astype(BF16)]
    pallas_call x0 -> x2, Pallas kernels: none -> 2.35 us  [the longest x1 1.98 us: body(): pieces = in_columns(split_body, [ROWS] * 2, [32] * 4, MAIN, 4)(keep, got)]
  transfers between devices with their start and end apart: 15 -> 16, of which waited for: 9 -> 8; matrix products, arithmetic and copies ran while one was open for 3% -> 0% of each run, Pallas kernels for 1% -> 2%
where the time goes in v2:
time: 168 us; the launch traced here: 166 us
  starting transfers between devices  75.1 us (45%)
  waiting for transfers between devices  39.4 us (23%)
  Pallas kernels  22.5 us (13%)
  blocking collectives  20.3 us (12%)
  local copies, waits for them, and re-layouts  7.23 us (4%)
    ppermute x11, starting transfers between devices, swap(): return lax.ppermute(block, axis, [(i, i ^ mask) for i in range(count)])  46.4 us
    all_to_all x5, starting transfers between devices, exchange(): return lax.all_to_all(block, axis, 0, 0)  28.6 us
    ppermute x11, waiting for transfers between devices, swap(): return lax.ppermute(block, axis, [(i, i ^ mask) for i in range(count)])  28.4 us
    all_to_all x1, blocking collectives, exchange(): return lax.all_to_all(block, axis, 0, 0)  20.3 us
    pallas_call x7, Pallas kernels, run(): pl.pallas_call(body, out_shape=[jax.ShapeDtypeStruct(s, d) for s, d in ou...  20.2 us
    all_to_all x5, waiting for transfers between devices, exchange(): return lax.all_to_all(block, axis, 0, 0)  11 us
    unnamed x20, local copies, waits for them, and re-layouts  7.23 us
  transfers between devices with their start and end apart: 16, of which 8 were waited for; matrix products, arithmetic and copies ran while one was open for 0% of the time, Pallas kernels for 2%

profile of v2, /device:TPU:24, one launch (start us, length us, event | category | flops | bytes accessed | tf_op | source)
XLA Modules:
  0.0 166.2 jit_solution(11302652637363318088)
XLA Ops:
  2.5 20.3 %all_to_all.30.near.near_hbm = bf16[4,320,512]{2,1,0:T(8,128)(2,1)S(1)} all-to-all(bf16[4,320,512]{2,1,0:T(8,128)(2,1)S(1)} %get-tuple-element.52), channel_id=1, replica_groups=mesh['zh'=4,'x'=4,'core'=2,'zl'=4,'y'=4] {'y'}, dimensions={0} | all-to-all | bytes 2621440 | tf_op jit(solution)/shard_map/all_to_all | solution.py:343
  23.6 5.9 %all-to-all-start.1 = ((bf16[4,64,512]{2,1,0:T(8,128)(2,1)}), bf16[4,64,512]{2,1,0:T(8,128)(2,1)S(1)}, u32[]{:S(2)}, u32[]{:S(2)}) async-start(bf16[4,64,512]{2,1,0:T(8,128)(2,1)} %shard_map.144), calls=%async_computation.1 | async-start | bytes 524288 | tf_op jit(solution)/shard_map/all_to_all | solution.py:343
  29.5 4.8 %collective-permute-start.1 = (bf16[256,512]{1,0:T(8,128)(2,1)S(1)}, bf16[256,512]{1,0:T(8,128)(2,1)S(1)}, u32[]{:S(2)}, u32[]{:S(2)}) collective-permute-start(bf16[256,512]{1,0:T(8,128)(2,1)S(1)} %get-tuple-element.53.own_hbm), channel_id=1, source_target_pairs={{0,8},{4,12},{8,0},{12,4},{1,9},{5,13},{9,1},{13,5},{2,10},{6,14},... | collective-permute-start | bytes 786440 | tf_op jit(solution)/shard_map/ppermute | solution.py:339
  34.4 3.4 %collective-permute-start = (bf16[256,512]{1,0:T(8,128)(2,1)S(1)}, bf16[256,512]{1,0:T(8,128)(2,1)S(1)}, u32[]{:S(2)}, u32[]{:S(2)}) collective-permute-start(bf16[256,512]{1,0:T(8,128)(2,1)S(1)} %get-tuple-element.53.own_hbm), channel_id=1, source_target_pairs={{0,4},{4,0},{8,12},{12,8},{1,5},{5,1},{9,13},{13,9},{2,6},{6,2},{1... | collective-permute-start | bytes 786440 | tf_op jit(solution)/shard_map/ppermute | solution.py:339
  37.8 10.6 %collective-permute-done.1.four_hbm = bf16[256,512]{1,0:T(8,128)(2,1)S(1)} collective-permute-done((bf16[256,512]{1,0:T(8,128)(2,1)S(1)}, bf16[256,512]{1,0:T(8,128)(2,1)S(1)}, u32[]{:S(2)}, u32[]{:S(2)}) %collective-permute-start.1) | collective-permute-done | bytes 262176 | tf_op jit(solution)/shard_map/ppermute | solution.py:339
  48.5 12.1 %shard_map.145 = (f32[256,512]{1,0:T(8,128)S(1)}, bf16[4,320,512]{2,1,0:T(8,128)(2,1)}, bf16[256,512]{1,0:T(8,128)(2,1)}, bf16[256,512]{1,0:T(8,128)(2,1)S(1)}, ...) custom-call(s32[4]{0:T(128)S(1)} %pad_add_fusion.place, bf16[4,320,512]{2,1,0:T(8,128)(2,1)S(1)} %all_to_all.30.near.near_hbm, ...), custom_call_target="tpu_custom_call" | custom-call | flops 1500000000 | bytes 10000000 | tf_op jit(solution)/shard_map/pallas_call | solution.py:302
  63.2 3.4 %collective-permute-done.2.b = bf16[128,6144]{1,0:T(8,128)(2,1)S(1)} collective-permute-done((bf16[128,6144]{1,0:T(8,128)(2,1)S(1)}, bf16[128,6144]{1,0:T(8,128)(2,1)S(1)}, u32[]{:S(2)}, u32[]{:S(2)}) %collective-permute-start.2) | collective-permute-done | bytes 1572896 | tf_op jit(solution)/shard_map/ppermute | solution.py:339
  66.6 2.0 %shard_map.146 = (bf16[32,6144]{1,0:T(8,128)(2,1)S(1)}, bf16[32,6144]{1,0:T(8,128)(2,1)}, bf16[32,6144]{1,0:T(8,128)(2,1)}, bf16[32,6144]{1,0:T(8,128)(2,1)}) custom-call(bf16[128,6144]{1,0:T(8,128)(2,1)S(1)} %get-tuple-element.58.a, bf16[128,6144]{1,0:T(8,128)(2,1)S(1)} %collective-permute-done.2.b), custom_call_target="tpu_custom_call" | custom-call | flops 1000000 | bytes 4000000 | tf_op jit(solution)/shard_map/pallas_call | solution.py:387
  68.6 5.7 %all-to-all-start.2 = ((bf16[4,320,512]{2,1,0:T(8,128)(2,1)}), bf16[4,320,512]{2,1,0:T(8,128)(2,1)S(1)}, u32[]{:S(2)}, u32[]{:S(2)}) async-start(bf16[4,320,512]{2,1,0:T(8,128)(2,1)} %get-tuple-element.64), calls=%async_computation.2 | async-start | bytes 2621440 | tf_op jit(solution)/shard_map/all_to_all | solution.py:343
  74.3 3.4 %collective-permute-start.3 = (bf16[32,6144]{1,0:T(8,128)(2,1)}, bf16[32,6144]{1,0:T(8,128)(2,1)S(1)}, u32[]{:S(2)}, u32[]{:S(2)}) collective-permute-start(bf16[32,6144]{1,0:T(8,128)(2,1)} %get-tuple-element.66), channel_id=1, source_target_pairs={{0,32},{32,0},{64,96},{96,64},{1,33},{33,1},{65,97},{97,65},{2,34}... | collective-permute-start | bytes 1179656 | tf_op jit(solution)/shard_map/ppermute | solution.py:339
  77.7 4.6 %collective-permute-start.4 = (bf16[32,6144]{1,0:T(8,128)(2,1)}, bf16[32,6144]{1,0:T(8,128)(2,1)S(1)}, u32[]{:S(2)}, u32[]{:S(2)}) collective-permute-start(bf16[32,6144]{1,0:T(8,128)(2,1)} %get-tuple-element.67), channel_id=1, source_target_pairs={{0,64},{32,96},{64,0},{96,32},{1,65},{33,97},{65,1},{97,33},{2,66}... | collective-permute-start | bytes 1179656 | tf_op jit(solution)/shard_map/ppermute | solution.py:339
  82.3 2.4 %collective-permute-start.5 = (bf16[32,6144]{1,0:T(8,128)(2,1)}, bf16[32,6144]{1,0:T(8,128)(2,1)S(1)}, u32[]{:S(2)}, u32[]{:S(2)}) collective-permute-start(bf16[32,6144]{1,0:T(8,128)(2,1)} %get-tuple-element.68), channel_id=1, source_target_pairs={{0,96},{32,64},{64,32},{96,0},{1,97},{33,65},{65,33},{97,1},{2,98}... | collective-permute-start | bytes 1179656 | tf_op jit(solution)/shard_map/ppermute | solution.py:339
  86.6 4.3 %collective-permute-start.7 = (bf16[256,512]{1,0:T(8,128)(2,1)S(1)}, bf16[256,512]{1,0:T(8,128)(2,1)S(1)}, u32[]{:S(2)}, u32[]{:S(2)}) collective-permute-start(bf16[256,512]{1,0:T(8,128)(2,1)S(1)} %copy-done.7), channel_id=1, source_target_pairs={{0,8},{4,12},{8,0},{12,4},{1,9},{5,13},{9,1},{13,5},{2,10},{6,14},... | collective-permute-start | bytes 786440 | tf_op jit(solution)/shard_map/ppermute | solution.py:339
  90.9 6.2 %collective-permute-done.6.three = bf16[256,512]{1,0:T(8,128)(2,1)S(1)} collective-permute-done((bf16[256,512]{1,0:T(8,128)(2,1)}, bf16[256,512]{1,0:T(8,128)(2,1)S(1)}, u32[]{:S(2)}, u32[]{:S(2)}) %collective-permute-start.6) | collective-permute-done | bytes 262176 | tf_op jit(solution)/shard_map/ppermute | solution.py:339
  97.2 5.2 %collective-permute-done.7.four = bf16[256,512]{1,0:T(8,128)(2,1)S(1)} collective-permute-done((bf16[256,512]{1,0:T(8,128)(2,1)S(1)}, bf16[256,512]{1,0:T(8,128)(2,1)S(1)}, u32[]{:S(2)}, u32[]{:S(2)}) %collective-permute-start.7) | collective-permute-done | bytes 262176 | tf_op jit(solution)/shard_map/ppermute | solution.py:339
  105.9 3.4 %all-to-all-start.3 = ((bf16[4,64,512]{2,1,0:T(8,128)(2,1)}), bf16[4,64,512]{2,1,0:T(8,128)(2,1)S(1)}, u32[]{:S(2)}, u32[]{:S(2)}) async-start(bf16[4,64,512]{2,1,0:T(8,128)(2,1)} %shard_map.147), calls=%async_computation.3 | async-start | bytes 524288 | tf_op jit(solution)/shard_map/all_to_all | solution.py:343
  114.0 3.5 %all-to-all-done.3.pieces_hbm = bf16[4,64,512]{2,1,0:T(8,128)(2,1)S(1)} async-done(((bf16[4,64,512]{2,1,0:T(8,128)(2,1)}), bf16[4,64,512]{2,1,0:T(8,128)(2,1)S(1)}, u32[]{:S(2)}, u32[]{:S(2)}) %all-to-all-start.3) | async-done | bytes 262176 | tf_op jit(solution)/shard_map/all_to_all | solution.py:343
  118.8 3.4 %all-to-all-start.4 = ((bf16[8,32,512]{2,1,0:T(8,128)(2,1)}), bf16[8,32,512]{2,1,0:T(8,128)(2,1)S(1)}, u32[]{:S(2)}, u32[]{:S(2)}) async-start(bf16[8,32,512]{2,1,0:T(8,128)(2,1)} %bitcast.4), calls=%async_computation.4 | async-start | bytes 524288 | tf_op jit(solution)/shard_map/all_to_all | solution.py:343
  122.2 9.1 %collective-permute-start.8 = (bf16[8,6144]{1,0:T(8,128)(2,1)}, bf16[8,6144]{1,0:T(8,128)(2,1)S(1)}, u32[]{:S(2)}, u32[]{:S(2)}) collective-permute-start(bf16[8,6144]{1,0:T(8,128)(2,1)} %copy-done.9), channel_id=1, source_target_pairs={{0,128},{128,0},{256,384},{384,256},{1,129},{129,1},{257,385},{385... | collective-permute-start | bytes 294920 | tf_op jit(solution)/shard_map/ppermute | solution.py:339
  131.3 8.7 %collective-permute-start.9 = (bf16[8,6144]{1,0:T(8,128)(2,1)}, bf16[8,6144]{1,0:T(8,128)(2,1)S(1)}, u32[]{:S(2)}, u32[]{:S(2)}) collective-permute-start(bf16[8,6144]{1,0:T(8,128)(2,1)} %copy-done.8), channel_id=1, source_target_pairs={{0,256},{128,384},{256,0},{384,128},{1,257},{129,385},{257,1},{385... | collective-permute-start | bytes 294920 | tf_op jit(solution)/shard_map/ppermute | solution.py:339
  142.6 10.2 %all-to-all-start.5 = ((bf16[4,8,512]{2,1,0:T(8,128)(2,1)}), bf16[4,8,512]{2,1,0:T(8,128)(2,1)S(1)}, u32[]{:S(2)}, u32[]{:S(2)}) async-start(bf16[4,8,512]{2,1,0:T(8,128)(2,1)} %bitcast.5), calls=%async_computation.5 | async-start | bytes 65536 | tf_op jit(solution)/shard_map/all_to_all | solution.py:343
  152.8 2.7 %shard_map.150 = (bf16[128,512]{1,0:T(8,128)(2,1)}, bf16[128,512]{1,0:T(8,128)(2,1)}) custom-call(s32[4]{0:T(128)S(1)} %pad_add_fusion.place, f32[256,512]{1,0:T(8,128)S(1)} %get-tuple-element.54.local_hbm, bf16[4,320,512]{2,1,0:T(8,128)(2,1)S(1)} %all-to-all-done.2.near, bf16[256,512]{1,0:T(8,128)(2,1)S(1)} %collective-permute-done.6.three, ...), custom_call_target="tpu_custom_call" | custom-call | flops 40000000 | bytes 2000000 | tf_op jit(solution)/shard_map/pallas_call | solution.py:302
  155.5 2.5 %collective-permute-done.10.four = bf16[8,6144]{1,0:T(8,128)(2,1)S(1)} collective-permute-done((bf16[8,6144]{1,0:T(8,128)(2,1)S(1)}, bf16[8,6144]{1,0:T(8,128)(2,1)S(1)}, u32[]{:S(2)}, u32[]{:S(2)}) %collective-permute-start.10) | collective-permute-done | bytes 98336 | tf_op jit(solution)/shard_map/ppermute | solution.py:339
  158.0 7.5 %all-to-all-done.5.mini = bf16[4,8,512]{2,1,0:T(8,128)(2,1)S(1)} async-done(((bf16[4,8,512]{2,1,0:T(8,128)(2,1)}), bf16[4,8,512]{2,1,0:T(8,128)(2,1)S(1)}, u32[]{:S(2)}, u32[]{:S(2)}) %all-to-all-start.5) | async-done | bytes 32800 | tf_op jit(solution)/shard_map/all_to_all | solution.py:343
  (40 shorter events, 20.0 us)
Async XLA Ops:
  23.6 24.8 %all-to-all-start.1 = ((bf16[4,64,512]{2,1,0:T(8,128)(2,1)}), bf16[4,64,512]{2,1,0:T(8,128)(2,1)S(1)}, u32[]{:S(2)}, u32[]{:S(2)}) async-start(bf16[4,64,512]{2,1,0:T(8,128)(2,1)} %shard_map.144), calls=%async_computation.1 | async-start | bytes 524288 | tf_op jit(solution)/shard_map/all_to_all | solution.py:343
  29.5 18.9 %collective-permute-start.1 = (bf16[256,512]{1,0:T(8,128)(2,1)S(1)}, bf16[256,512]{1,0:T(8,128)(2,1)S(1)}, u32[]{:S(2)}, u32[]{:S(2)}) collective-permute-start(bf16[256,512]{1,0:T(8,128)(2,1)S(1)} %get-tuple-element.53.own_hbm), channel_id=1, source_target_pairs={{0,8},{4,12},{8,0},{12,4},{1,9},{5,13},{9,1},{13,5},{2,10},{6,14},... | collective-permute-start | bytes 786440 | tf_op jit(solution)/shard_map/ppermute | solution.py:339
  34.4 14.1 %collective-permute-start = (bf16[256,512]{1,0:T(8,128)(2,1)S(1)}, bf16[256,512]{1,0:T(8,128)(2,1)S(1)}, u32[]{:S(2)}, u32[]{:S(2)}) collective-permute-start(bf16[256,512]{1,0:T(8,128)(2,1)S(1)} %get-tuple-element.53.own_hbm), channel_id=1, source_target_pairs={{0,4},{4,0},{8,12},{12,8},{1,5},{5,1},{9,13},{13,9},{2,6},{6,2},{1... | collective-permute-start | bytes 786440 | tf_op jit(solution)/shard_map/ppermute | solution.py:339
  60.6 0.7 copy-start.6
  61.3 5.3 %collective-permute-start.2 = (bf16[128,6144]{1,0:T(8,128)(2,1)S(1)}, bf16[128,6144]{1,0:T(8,128)(2,1)S(1)}, u32[]{:S(2)}, u32[]{:S(2)}) collective-permute-start(bf16[128,6144]{1,0:T(8,128)(2,1)S(1)} %get-tuple-element.59), channel_id=1, source_target_pairs={{0,16},{16,0},{1,17},{17,1},{2,18},{18,2},{3,19},{19,3},{4,20},{20... | collective-permute-start | bytes 4718600 | tf_op jit(solution)/shard_map/ppermute | solution.py:339
  68.6 18.1 %copy-start.7 = (bf16[256,512]{1,0:T(8,128)(2,1)S(1)}, bf16[256,512]{1,0:T(8,128)(2,1)}, u32[]{:S(2)}) copy-start(bf16[256,512]{1,0:T(8,128)(2,1)} %copy-done.6) | copy-start | bytes 786436
  68.6 36.6 %all-to-all-start.2 = ((bf16[4,320,512]{2,1,0:T(8,128)(2,1)}), bf16[4,320,512]{2,1,0:T(8,128)(2,1)S(1)}, u32[]{:S(2)}, u32[]{:S(2)}) async-start(bf16[4,320,512]{2,1,0:T(8,128)(2,1)} %get-tuple-element.64), calls=%async_computation.2 | async-start | bytes 2621440 | tf_op jit(solution)/shard_map/all_to_all | solution.py:343
  74.3 28.1 %collective-permute-start.3 = (bf16[32,6144]{1,0:T(8,128)(2,1)}, bf16[32,6144]{1,0:T(8,128)(2,1)S(1)}, u32[]{:S(2)}, u32[]{:S(2)}) collective-permute-start(bf16[32,6144]{1,0:T(8,128)(2,1)} %get-tuple-element.66), channel_id=1, source_target_pairs={{0,32},{32,0},{64,96},{96,64},{1,33},{33,1},{65,97},{97,65},{2,34}... | collective-permute-start | bytes 1179656 | tf_op jit(solution)/shard_map/ppermute | solution.py:339
  77.7 25.4 %collective-permute-start.4 = (bf16[32,6144]{1,0:T(8,128)(2,1)}, bf16[32,6144]{1,0:T(8,128)(2,1)S(1)}, u32[]{:S(2)}, u32[]{:S(2)}) collective-permute-start(bf16[32,6144]{1,0:T(8,128)(2,1)} %get-tuple-element.67), channel_id=1, source_target_pairs={{0,64},{32,96},{64,0},{96,32},{1,65},{33,97},{65,1},{97,33},{2,66}... | collective-permute-start | bytes 1179656 | tf_op jit(solution)/shard_map/ppermute | solution.py:339
  82.3 22.1 %collective-permute-start.5 = (bf16[32,6144]{1,0:T(8,128)(2,1)}, bf16[32,6144]{1,0:T(8,128)(2,1)S(1)}, u32[]{:S(2)}, u32[]{:S(2)}) collective-permute-start(bf16[32,6144]{1,0:T(8,128)(2,1)} %get-tuple-element.68), channel_id=1, source_target_pairs={{0,96},{32,64},{64,32},{96,0},{1,97},{33,65},{65,33},{97,1},{2,98}... | collective-permute-start | bytes 1179656 | tf_op jit(solution)/shard_map/ppermute | solution.py:339
  84.7 12.4 %collective-permute-start.6 = (bf16[256,512]{1,0:T(8,128)(2,1)}, bf16[256,512]{1,0:T(8,128)(2,1)S(1)}, u32[]{:S(2)}, u32[]{:S(2)}) collective-permute-start(bf16[256,512]{1,0:T(8,128)(2,1)} %get-tuple-element.69), channel_id=1, source_target_pairs={{0,4},{4,0},{8,12},{12,8},{1,5},{5,1},{9,13},{13,9},{2,6},{6,2},{1... | collective-permute-start | bytes 786440 | tf_op jit(solution)/shard_map/ppermute | solution.py:339
  86.6 15.7 %collective-permute-start.7 = (bf16[256,512]{1,0:T(8,128)(2,1)S(1)}, bf16[256,512]{1,0:T(8,128)(2,1)S(1)}, u32[]{:S(2)}, u32[]{:S(2)}) collective-permute-start(bf16[256,512]{1,0:T(8,128)(2,1)S(1)} %copy-done.7), channel_id=1, source_target_pairs={{0,8},{4,12},{8,0},{12,4},{1,9},{5,13},{9,1},{13,5},{2,10},{6,14},... | collective-permute-start | bytes 786440 | tf_op jit(solution)/shard_map/ppermute | solution.py:339
  102.3 0.8 copy-start
  103.1 0.8 copy-start.2
  104.4 0.8 copy-start.4
  105.9 11.6 %all-to-all-start.3 = ((bf16[4,64,512]{2,1,0:T(8,128)(2,1)}), bf16[4,64,512]{2,1,0:T(8,128)(2,1)S(1)}, u32[]{:S(2)}, u32[]{:S(2)}) async-start(bf16[4,64,512]{2,1,0:T(8,128)(2,1)} %shard_map.147), calls=%async_computation.3 | async-start | bytes 524288 | tf_op jit(solution)/shard_map/all_to_all | solution.py:343
  109.4 1.0 copy-start.1
  110.4 1.0 copy-start.3
  111.4 1.0 copy-start.5
  118.8 23.2 %all-to-all-start.4 = ((bf16[8,32,512]{2,1,0:T(8,128)(2,1)}), bf16[8,32,512]{2,1,0:T(8,128)(2,1)S(1)}, u32[]{:S(2)}, u32[]{:S(2)}) async-start(bf16[8,32,512]{2,1,0:T(8,128)(2,1)} %bitcast.4), calls=%async_computation.4 | async-start | bytes 524288 | tf_op jit(solution)/shard_map/all_to_all | solution.py:343
  122.2 33.3 %collective-permute-start.8 = (bf16[8,6144]{1,0:T(8,128)(2,1)}, bf16[8,6144]{1,0:T(8,128)(2,1)S(1)}, u32[]{:S(2)}, u32[]{:S(2)}) collective-permute-start(bf16[8,6144]{1,0:T(8,128)(2,1)} %copy-done.9), channel_id=1, source_target_pairs={{0,128},{128,0},{256,384},{384,256},{1,129},{129,1},{257,385},{385... | collective-permute-start | bytes 294920 | tf_op jit(solution)/shard_map/ppermute | solution.py:339
  131.3 24.2 %collective-permute-start.9 = (bf16[8,6144]{1,0:T(8,128)(2,1)}, bf16[8,6144]{1,0:T(8,128)(2,1)S(1)}, u32[]{:S(2)}, u32[]{:S(2)}) collective-permute-start(bf16[8,6144]{1,0:T(8,128)(2,1)} %copy-done.8), channel_id=1, source_target_pairs={{0,256},{128,384},{256,0},{384,128},{1,257},{129,385},{257,1},{385... | collective-permute-start | bytes 294920 | tf_op jit(solution)/shard_map/ppermute | solution.py:339
  140.0 18.0 %collective-permute-start.10 = (bf16[8,6144]{1,0:T(8,128)(2,1)S(1)}, bf16[8,6144]{1,0:T(8,128)(2,1)S(1)}, u32[]{:S(2)}, u32[]{:S(2)}) collective-permute-start(bf16[8,6144]{1,0:T(8,128)(2,1)S(1)} %get-tuple-element.88), channel_id=1, source_target_pairs={{0,384},{128,256},{256,128},{384,0},{1,385},{129,257},{257,129},{3... | collective-permute-start | bytes 294920 | tf_op jit(solution)/shard_map/ppermute | solution.py:339
  142.6 22.8 %all-to-all-start.5 = ((bf16[4,8,512]{2,1,0:T(8,128)(2,1)}), bf16[4,8,512]{2,1,0:T(8,128)(2,1)S(1)}, u32[]{:S(2)}, u32[]{:S(2)}) async-start(bf16[4,8,512]{2,1,0:T(8,128)(2,1)} %bitcast.5), calls=%async_computation.5 | async-start | bytes 65536 | tf_op jit(solution)/shard_map/all_to_all | solution.py:343
  (2 other events, 1.3 us)

commit v3 on v1

v3 whole, which is shorter than its diff:
```python
import functools
import math

import jax
import jax.numpy as jnp
from jax import lax
from jax.experimental import pallas as pl
from jax.experimental.pallas import tpu as pltpu
from jax.sharding import Mesh
from jax.sharding import PartitionSpec as P

DP = ("zh", "x", "core")
TENSOR = ("zl", "y")
SIZES = (4, 4, 2, 4, 4)
ROWS = 128
SIDE = 256
SLAB = 512
HIDDEN = 1024
BLOCKS = 4
FACTORS = 5
F32 = jnp.float32
BF16 = jnp.bfloat16

GROUP = BLOCKS * SIDE
DOWN_AT = 3 * GROUP
LEFT_AT = DOWN_AT + BLOCKS * FACTORS * ROWS
MAIN = LEFT_AT + SLAB
MINI = SLAB
LOW = ROWS // 2
LIMIT = 63 * 1024 * 1024
SMALL = 16 * 1024 * 1024


def mm(a, b):
    return lax.dot_general(a, b, (((1,), (0,)), ((), ())), preferred_element_type=F32)


def mt(a, b):
    return lax.dot_general(a, b, (((1,), (1,)), ((), ())), preferred_element_type=F32)


def pick(place):
    core, x_here = place[0], place[1]
    row = lax.broadcasted_iota(jnp.int32, (SIDE, SIDE), 0)
    column = lax.broadcasted_iota(jnp.int32, (SIDE, SIDE), 1)
    quarter, half = row & 3, (row >> 2) & 1
    zh, x = (row >> 3) & 3, (row >> 5) & 3
    at = zh * 8 + (x ^ x_here) * 2 + ((row >> 7) ^ core)
    pair = (column == half * ROWS + at * 4 + quarter).astype(BF16)
    whole = (column == at * 8 + half * 4 + quarter).astype(BF16)
    return pair, whole


def pick_mini():
    row = lax.broadcasted_iota(jnp.int32, (SIDE, SIDE), 0)
    column = lax.broadcasted_iota(jnp.int32, (SIDE, SIDE), 1)
    quarter, half = row & 3, (row >> 2) & 1
    at = ((row >> 3) & 3) * 8 + (row >> 5)
    return (column == half * ROWS + at * 4 + quarter).astype(BF16)


class Copies:
    def __init__(self, sems):
        self.sems, self.count = sems, 0

    def start(self, source, target):
        copy = pltpu.make_async_copy(source, target, self.sems.at[self.count])
        self.count += 1
        copy.start()
        return copy


def finish(copies):
    for copy in copies:
        copy.wait()


def fold(low):
    return jnp.concatenate([low[:LOW], low[LOW:]], axis=1).astype(BF16)


def unfold(pieces):
    total = pieces[0].astype(F32)
    for n in range(1, pieces.shape[0]):
        total = total + pieces[n].astype(F32)
    total = total.astype(BF16)
    first = jnp.concatenate([total[:, :ROWS], total[:, 2 * ROWS : 3 * ROWS]], axis=0)
    second = jnp.concatenate([total[:, ROWS : 2 * ROWS], total[:, 3 * ROWS :]], axis=0)
    return first, second


def low_body(tokens, cotangent, up_left, down_right, own, low, u, d, sems):
    copies = Copies(sems)
    t, c = own.at[:ROWS], own.at[ROWS:]
    first = [copies.start(tokens, t), copies.start(up_left, u)]
    second = [copies.start(cotangent, c), copies.start(down_right, d)]
    finish(first)
    low[:, :ROWS] = mm(t[...], u[...])
    finish(second)
    low[:, ROWS:] = mt(c[...], d[...])


def main_body(
    scale, place, own_at, one_at, two_at, three_at, four_at, low_at, up_at, up_right_at, down_at, down_left_at,
    local_to, one_to, two_to, three_to, four_to, packed_to, keep_to, send_to,
    arrived, low, up, up_right, down, down_left, local, sent, packed, keep, send, sems,
):
    copies = Copies(sems)
    first = [
        copies.start(low_at, low),
        copies.start(up_right_at, up_right),
        copies.start(down_left_at, down_left),
    ]
    first += [
        copies.start(a, arrived.at[n])
        for n, a in enumerate((own_at, one_at, two_at, three_at, four_at))
    ]
    blocks = [
        (copies.start(up_at.at[:, b], up.at[:, b]), copies.start(down_at.at[:, b], down.at[:, b]))
        for b in range(BLOCKS)
    ]
    pair, whole = pick(place)
    out_going = []

    def put(at, value):
        value = (value * scale).astype(BF16)
        columns = slice(at, at + value.shape[1])
        keep[:, columns] = value[:ROWS]
        send[:, columns] = value[ROWS:]
        out_going.append(copies.start(send.at[:, columns], send_to.at[:, columns]))
        out_going.append(copies.start(keep.at[:, columns], keep_to.at[:, columns]))

    finish(first)
    low_up, low_cot = low[:, :ROWS], low[:, ROWS:]
    hiddens, pres = [], []
    low_down = jnp.zeros((ROWS, ROWS), F32)
    low_pre = jnp.zeros((ROWS, ROWS), F32)
    for b in range(BLOCKS):
        features = slice(b * ROWS, (b + 1) * ROWS)
        units = slice(b * SIDE, (b + 1) * SIDE)
        value = mm(low_up, up_right[:, units])
        grad = mt(low_cot, down_left[units, :])
        finish(blocks[b])
        for k in range(FACTORS):
            value = value + mm(arrived[k, :ROWS, features], up[k, b])
            grad = grad + mt(arrived[k, ROWS:, features], down[k, b])
        phi = 0.5 + 0.5 * lax.erf(value * math.sqrt(0.5))
        density = jnp.exp(-0.5 * value * value) * (1.0 / math.sqrt(2.0 * math.pi))
        hidden = (value * phi).astype(BF16)
        pre = (grad * (phi + value * density)).astype(BF16)
        hiddens.append(hidden)
        pres.append(pre)
        low_down = low_down + mm(hidden, down_left[units, :])
        low_pre = low_pre + mt(pre, up_right[:, units])
    packed[...] = fold(jnp.concatenate([low_down, low_pre], axis=1))
    out_going += [copies.start(packed, packed_to.at[n]) for n in range(packed_to.shape[0])]
    for b in range(BLOCKS):
        features = slice(b * ROWS, (b + 1) * ROWS)
        hidden, pre = hiddens[b], pres[b]
        for k in range(FACTORS):
            upper, lower = mm(hidden, down[k, b]), mt(pre, up[k, b])
            if k:
                sent[k - 1, :ROWS, features] = upper.astype(BF16)
                sent[k - 1, ROWS:, features] = lower.astype(BF16)
            else:
                local[:ROWS, features] = upper
                local[ROWS:, features] = lower
    for n, to in enumerate((one_to, two_to, three_to, four_to)):
        out_going.append(copies.start(sent.at[n], to))
    out_going.append(copies.start(local, local_to))
    for b in range(BLOCKS):
        features = slice(b * ROWS, (b + 1) * ROWS)
        hidden, pre = hiddens[b], pres[b]
        left = [arrived[k, :ROWS, features] for k in range(FACTORS)] + [low_up]
        cot = [arrived[k, ROWS:, features] for k in range(FACTORS)]
        for g in range(3):
            rows = jnp.concatenate([left[2 * g], left[2 * g + 1]], axis=1)
            put(g * GROUP + b * SIDE, mm(mt(pair, rows).astype(BF16), pre))
        rows = mt(whole, hidden).astype(BF16)
        put(DOWN_AT + b * FACTORS * ROWS, mm(rows, jnp.concatenate(cot, axis=1)))
    zero = jnp.zeros_like(low_cot)
    upper = mt(pair, jnp.concatenate([low_cot, zero], axis=1)).astype(BF16)
    lower = mt(pair, jnp.concatenate([zero, low_cot], axis=1)).astype(BF16)
    put(
        LEFT_AT,
        mm(upper, jnp.concatenate(hiddens[:2], axis=1))
        + mm(lower, jnp.concatenate(hiddens[2:], axis=1)),
    )
    finish(out_going)


def mini_body(scale, own, pieces, low, mini):
    pair = pick_mini()
    low_down, low_pre = unfold(pieces)
    low[:, :ROWS] = low_down
    low[:, ROWS:] = low_pre
    zero = jnp.zeros_like(low_pre)
    upper = mt(pair, jnp.concatenate([low_pre, zero], axis=1)).astype(BF16)
    lower = mt(pair, jnp.concatenate([zero, low_down], axis=1)).astype(BF16)
    value = mm(upper, own[:ROWS, :]) + mm(lower, own[ROWS:, :])
    mini[...] = (value * scale).astype(BF16)


def last_body(local, one, two, three, four, low, up_left, down_right, out, grad):
    total = local[...]
    for a in (one, two, three, four):
        total = total + a[...].astype(F32)
    out[...] = (total[:ROWS] + mm(low[:, :ROWS], down_right[...])).astype(BF16)
    grad[...] = (total[ROWS:] + mt(low[:, ROWS:], up_left[...])).astype(BF16)


STEPS = 4


def columns_of(n):
    return slice(n * (MAIN // STEPS), (n + 1) * (MAIN // STEPS))


def split_body(a_at, b_at, one_to, two_to, three_to, four_to, a, b, sems):
    copies = Copies(sems)
    coming = [
        [copies.start(at.at[:, columns_of(n)], to.at[:, columns_of(n)]) for at, to in ((a_at, a), (b_at, b))]
        for n in range(STEPS)
    ]
    going = []
    for n in range(STEPS):
        part = columns_of(n)
        finish(coming[n])
        a[:, part] = (a[:, part].astype(F32) + b[:, part].astype(F32)).astype(BF16)
        for m, to in enumerate((one_to, two_to, three_to, four_to)):
            going.append(copies.start(a.at[m * 32 : (m + 1) * 32, part], to.at[:, part]))
    finish(going)


def join_body(one_at, two_at, three_at, four_at, mini_at, out_to, pieces, mini, out, sems):
    copies = Copies(sems)
    coming = [
        [
            copies.start(at.at[:, columns_of(n)], pieces.at[m, :, columns_of(n)])
            for m, at in enumerate((one_at, two_at, three_at, four_at))
        ]
        for n in range(STEPS)
    ]
    last = copies.start(mini_at, mini)
    going = []
    for n in range(STEPS):
        part = columns_of(n)
        finish(coming[n])
        total = pieces[0, :, part].astype(F32) + pieces[1, :, part].astype(F32)
        total = total + pieces[2, :, part].astype(F32) + pieces[3, :, part].astype(F32)
        out[:, part] = total.astype(BF16)
        going.append(copies.start(out.at[:, part], out_to.at[:, part]))
    last.wait()
    total = mini[0].astype(F32)
    for n in range(1, mini.shape[0]):
        total = total + mini[n].astype(F32)
    out[:, MAIN:] = total.astype(BF16)
    going.append(copies.start(out.at[:, MAIN:], out_to.at[:, MAIN:]))
    finish(going)


def unpack_body(pieces, up, up_left, up_right, down, down_left, down_right):
    total = pieces[0].astype(F32)
    for n in range(1, pieces.shape[0]):
        total = total + pieces[n].astype(F32)
    top, low = total[:4].astype(BF16), total[4:].astype(BF16)
    total = total.astype(BF16)
    for b in range(BLOCKS):
        for k in range(FACTORS):
            at = (k // 2) * GROUP + b * SIDE
            up[k, b] = (low if k % 2 else top)[:, at : at + SIDE]
            at = DOWN_AT + (b * FACTORS + k) * ROWS
            down[k, b] = total[:, at : at + ROWS]
    up_right[...] = low[:, 2 * GROUP : 3 * GROUP]
    down_left[:, :SLAB] = top[:, LEFT_AT:MAIN]
    down_left[:, SLAB:] = low[:, LEFT_AT:MAIN]
    up_left[...] = top[:, MAIN:]
    down_right[...] = low[:, MAIN:]


SPACES = {"s": pltpu.SMEM, "v": pltpu.VMEM, "h": pltpu.HBM, "a": pl.ANY, "c": pl.ANY}


def call(body, outs, kinds, scratch=(), copies=0, cost=(0, 0), limit=LIMIT):
    kinds, kinds_out = kinds.split()
    sems = [pltpu.SemaphoreType.DMA((copies,))] if copies else []

    def run(*args):
        args = [
            pltpu.with_memory_space_constraint(a, pltpu.HBM) if k == "h" else a
            for a, k in zip(args, kinds)
        ]
        every = kinds + kinds_out
        shapes = [(a.shape, a.dtype) for a in args] + list(outs)
        staged = [pltpu.VMEM(*shapes[n]) for n, k in enumerate(every) if k == "c"]
        extra = [pltpu.SemaphoreType.DMA((len(staged),))] if staged else []

        def kernel(*refs):
            refs, rest = list(refs[: len(every)]), list(refs[len(every) :])
            if staged:
                buffers, rest = rest[: len(staged)], rest[len(staged) :]
                stage = Copies(rest.pop())
                places = [n for n, k in enumerate(every) if k == "c"]
                pairs = [(n, refs[n], buffer) for n, buffer in zip(places, buffers)]
                coming = [(o, u) for n, o, u in pairs if n < len(kinds)]
                going = [(u, o) for n, o, u in pairs if n >= len(kinds)]
                for n, _, buffer in pairs:
                    refs[n] = buffer
                started = [stage.start(*pair) for pair in coming]
                finish(started)
            body(*refs, *rest)
            if staged:
                finish([stage.start(*pair) for pair in going])

        return pl.pallas_call(
            kernel,
            out_shape=[jax.ShapeDtypeStruct(s, d) for s, d in outs],
            in_specs=[pl.BlockSpec(memory_space=SPACES[k]) for k in kinds],
            out_specs=[pl.BlockSpec(memory_space=SPACES[k]) for k in kinds_out],
            scratch_shapes=staged + [pltpu.VMEM(s, d) for s, d in scratch] + sems + extra,
            compiler_params=pltpu.CompilerParams(vmem_limit_bytes=limit),
            cost_estimate=pl.CostEstimate(
                flops=cost[0], bytes_accessed=cost[1], transcendentals=0
            ),
        )(*args)

    return run


def swap(block, axis, mask):
    count = lax.axis_size(axis)
    return lax.ppermute(block, axis, [(i, i ^ mask) for i in range(count)])


def exchange(block, axis):
    return lax.all_to_all(block, axis, 0, 0)


def all_sum(partial):
    count = SIZES[3] * SIZES[4]
    pieces = exchange(partial.reshape(count, ROWS // count, 2 * ROWS), TENSOR)
    piece = jnp.sum(pieces, axis=0).astype(BF16)
    return exchange(jnp.broadcast_to(piece, pieces.shape), TENSOR).reshape(ROWS, 2 * ROWS)


def body(tokens, cotangent, up_blocks, up_left, up_right, down_blocks, down_left, down_right):
    scale = 1.0 / math.sqrt(ROWS * SIZES[0] * SIZES[1] * SIZES[2])
    index = lax.axis_index
    place = jnp.stack([index("core"), index("x")]).astype(jnp.int32)
    wide, lows = (2 * ROWS, SLAB), (ROWS, 2 * ROWS)
    hops = (("y", 1), ("y", 2), ("zl", 1), ("zl", 2))
    shape = lambda a: (a.shape, a.dtype)

    own, low = call(
        low_body,
        [(wide, BF16), (lows, F32)],
        "hhhh cc",
        [shape(up_left), shape(down_right)],
        4,
        cost=(40_000_000, 2_000_000),
    )(tokens, cotangent, up_left, down_right)
    low = all_sum(low)
    arrived = [swap(own, axis, mask) for axis, mask in hops]

    half = (ROWS, MAIN)
    weights = (up_blocks, up_right, down_blocks, down_left)
    local, *terms, packed, keep, send = call(
        functools.partial(main_body, scale),
        [(wide, F32)] + [(wide, BF16)] * 4 + [((16, LOW, SLAB), BF16), (half, BF16), (half, BF16)],
        "saaaaaahhhh aaaaaaaa",
        [((FACTORS, *wide), BF16), shape(low)]
        + [shape(a) for a in weights]
        + [(wide, F32), ((FACTORS - 1, *wide), BF16), ((LOW, SLAB), BF16), (half, BF16), (half, BF16)],
        80,
        cost=(1_500_000_000, 10_000_000),
    )(place, own, *arrived, low, *weights)

    low = exchange(packed, TENSOR)
    got = swap(send, "core", 1)
    pieces = call(
        split_body,
        [((32, MAIN), BF16)] * 4,
        "aa aaaa",
        [(half, BF16)] * 2,
        6 * STEPS,
        cost=(30_000_000_000, 5_000_000),
    )(keep, got)
    pieces = list(pieces[:1]) + [swap(pieces[mask], "x", mask) for mask in (1, 2, 3)]
    far = [swap(term, axis, mask) for term, (axis, mask) in zip(terms[2:], hops[2:])]

    low, mini = call(
        functools.partial(mini_body, scale),
        [(lows, BF16), ((2 * ROWS, MINI), BF16)],
        "cc cc",
        cost=(40_000_000, 1_000_000),
    )(own, low)
    mini = exchange(mini.reshape(8, -1, MINI), ("x", "core"))

    pieces, far = lax.optimization_barrier((pieces, far))
    pieces = call(
        join_body,
        [((32, MAIN + MINI), BF16)],
        "aaaaa a",
        [((4, 32, MAIN), BF16), (mini.shape, BF16), ((32, MAIN + MINI), BF16)],
        5 * STEPS + 2,
        cost=(1_000_000, 2_000_000),
    )(*pieces, mini)[0]
    near, pieces, low = lax.optimization_barrier((terms[:2], pieces, low))
    pieces = exchange(pieces.reshape(SIZES[0], 8, -1), "zh")
    terms = [swap(term, axis, mask) for term, (axis, mask) in zip(near, hops[:2])] + far

    out, tokens_grad = call(
        last_body, [((ROWS, SLAB), BF16)] * 2, "cccccccc cc", cost=(40_000_000, 2_000_000)
    )(local, *terms, low, up_left, down_right)

    up_g, up_left_g, up_right_g, down_g, down_left_g, down_right_g = call(
        unpack_body,
        [
            ((FACTORS, BLOCKS, 4, SIDE), BF16),
            ((4, SLAB), BF16),
            ((4, HIDDEN), BF16),
            ((FACTORS, BLOCKS, 8, ROWS), BF16),
            ((4, HIDDEN), BF16),
            ((4, SLAB), BF16),
        ],
        "v cccccc",
        cost=(1_000_000, 1_000_000),
        limit=SMALL,
    )(pieces)
    return (out, tokens_grad, up_g, up_left_g.T, up_right_g, down_g, down_left_g.T, down_right_g)


def solution(mesh):
    fine = Mesh(mesh.devices.reshape(SIZES), DP + TENSOR)
    in_specs = (
        P(DP, TENSOR),
        P(DP, TENSOR),
        P(None, TENSOR, None, None),
        P(TENSOR, None),
        P(None, TENSOR),
        P(None, TENSOR, None, None),
        P(TENSOR, None),
        P(None, TENSOR),
    )
    out_specs = (
        P(DP, TENSOR),
        P(DP, TENSOR),
        P(None, TENSOR, DP, None),
        P(TENSOR, DP),
        P(DP, TENSOR),
        P(None, TENSOR, DP, None),
        P(TENSOR, DP),
        P(DP, TENSOR),
    )
    return jax.shard_map(body, mesh=fine, in_specs=in_specs, out_specs=out_specs, check_vma=False)
```

time: 166 us -> 139 us (0.84)
  the two profiles are of different devices: /device:TPU:24 before, /device:TPU:33 now
where the time goes in v3:
time: 139 us; the launch traced here: 138 us
  starting transfers between devices  77 us (55%)
  waiting for transfers between devices  36.3 us (26%)
  Pallas kernels  21.4 us (15%)
  local copies, waits for them, and re-layouts  1.97 us (1%)
    ppermute x12, starting transfers between devices, swap(): return lax.ppermute(block, axis, [(i, i ^ mask) for i in range(count)])  38.6 us
    all_to_all x5, starting transfers between devices, exchange(): return lax.all_to_all(block, axis, 0, 0)  38.4 us
    all_to_all x5, waiting for transfers between devices, exchange(): return lax.all_to_all(block, axis, 0, 0)  23.9 us
    pallas_call x7, Pallas kernels, run(): pl.pallas_call(kernel, out_shape=[jax.ShapeDtypeStruct(s, d) for s, d in...  21.4 us
    ppermute x12, waiting for transfers between devices, swap(): return lax.ppermute(block, axis, [(i, i ^ mask) for i in range(count)])  12.4 us
  transfers between devices with their start and end apart: 17, of which 7 were waited for; matrix products, arithmetic and copies ran while one was open for 1% of the time, Pallas kernels for 6%

profile of v3, /device:TPU:33, one launch (start us, length us, event | category | flops | bytes accessed | tf_op | source)
XLA Modules:
  0.0 138.1 jit_solution(17120571859155327006)
XLA Ops:
  2.7 8.1 %all-to-all-start = ((f32[16,8,256]{2,1,0:T(8,128)}), f32[16,8,256]{2,1,0:T(8,128)S(1)}, u32[]{:S(2)}, u32[]{:S(2)}) async-start(f32[16,8,256]{2,1,0:T(8,128)} %bitcast.10), calls=%async_computation | async-start | bytes 262144 | tf_op jit(solution)/shard_map/all_to_all | solution.py:336
  10.8 4.0 %collective-permute-start.3 = (bf16[256,512]{1,0:T(8,128)(2,1)}, bf16[256,512]{1,0:T(8,128)(2,1)S(1)}, u32[]{:S(2)}, u32[]{:S(2)}) collective-permute-start(bf16[256,512]{1,0:T(8,128)(2,1)} %get-tuple-element.42.refs_1_.refs_0_), channel_id=1, source_target_pairs={{0,8},{4,12},{8,0},{12,4},{1,9},{5,13},{9,1},{13,5},{2,10},{6,14},... | collective-permute-start | bytes 786440 | tf_op jit(solution)/shard_map/ppermute | solution.py:332
  17.0 4.6 %collective-permute-start.1 = (bf16[256,512]{1,0:T(8,128)(2,1)}, bf16[256,512]{1,0:T(8,128)(2,1)S(1)}, u32[]{:S(2)}, u32[]{:S(2)}) collective-permute-start(bf16[256,512]{1,0:T(8,128)(2,1)} %get-tuple-element.42.refs_1_.refs_0_), channel_id=1, source_target_pairs={{0,2},{1,3},{2,0},{3,1},{4,6},{5,7},{6,4},{7,5},{8,10},{9,11},{10,... | collective-permute-start | bytes 786440 | tf_op jit(solution)/shard_map/ppermute | solution.py:332
  24.5 4.5 %all-to-all-start.1 = ((bf16[16,8,256]{2,1,0:T(8,128)(2,1)}), bf16[16,8,256]{2,1,0:T(8,128)(2,1)S(1)}, u32[]{:S(2)}, u32[]{:S(2)}) async-start(bf16[16,8,256]{2,1,0:T(8,128)(2,1)} %broadcast_in_dim.3), calls=%async_computation.1 | async-start | bytes 131072 | tf_op jit(solution)/shard_map/all_to_all | solution.py:336
  29.6 2.5 %collective-permute-done.refs_2_ = bf16[256,512]{1,0:T(8,128)(2,1)S(1)} collective-permute-done((bf16[256,512]{1,0:T(8,128)(2,1)}, bf16[256,512]{1,0:T(8,128)(2,1)S(1)}, u32[]{:S(2)}, u32[]{:S(2)}) %collective-permute-start) | collective-permute-done | bytes 262176 | tf_op jit(solution)/shard_map/ppermute | solution.py:332
  32.1 2.7 %all-to-all-done.1 = bf16[16,8,256]{2,1,0:T(8,128)(2,1)S(1)} async-done(((bf16[16,8,256]{2,1,0:T(8,128)(2,1)}), bf16[16,8,256]{2,1,0:T(8,128)(2,1)S(1)}, u32[]{:S(2)}, u32[]{:S(2)}) %all-to-all-start.1) | async-done | bytes 65568 | tf_op jit(solution)/shard_map/all_to_all | solution.py:336
  35.4 8.3 %shard_map.144 = (f32[256,512]{1,0:T(8,128)}, bf16[256,512]{1,0:T(8,128)(2,1)}, bf16[256,512]{1,0:T(8,128)(2,1)}, bf16[256,512]{1,0:T(8,128)(2,1)}, bf16[256,512...) custom-call(s32[2]{0:T(128)} %pad_add_fusion.refs_0_, ...), custom_call_target="tpu_custom_call" | custom-call | flops 1500000000 | bytes 10000000 | tf_op jit(solution)/shard_map/pallas_call | solution.py:315
  43.7 5.6 %collective-permute-start.4 = (bf16[128,6144]{1,0:T(8,128)(2,1)}, bf16[128,6144]{1,0:T(8,128)(2,1)}, u32[]{:S(2)}, u32[]{:S(2)}) collective-permute-start(bf16[128,6144]{1,0:T(8,128)(2,1)} %get-tuple-element.48), channel_id=1, source_target_pairs={{0,16},{16,0},{1,17},{17,1},{2,18},{18,2},{3,19},{19,3},{4,20},{20... | collective-permute-start | bytes 4718600 | tf_op jit(solution)/shard_map/ppermute | solution.py:332
  49.3 5.7 %all-to-all-start.2 = ((bf16[16,64,512]{2,1,0:T(8,128)(2,1)}), bf16[16,64,512]{2,1,0:T(8,128)(2,1)}, u32[]{:S(2)}, u32[]{:S(2)}) async-start(bf16[16,64,512]{2,1,0:T(8,128)(2,1)} %get-tuple-element.59), calls=%async_computation.2 | async-start | bytes 2097152 | tf_op jit(solution)/shard_map/all_to_all | solution.py:336
  55.0 2.9 %shard_map.145 = (bf16[32,6144]{1,0:T(8,128)(2,1)}, bf16[32,6144]{1,0:T(8,128)(2,1)}, bf16[32,6144]{1,0:T(8,128)(2,1)}, bf16[32,6144]{1,0:T(8,128)(2,1)}) custom-call(bf16[128,6144]{1,0:T(8,128)(2,1)} %get-tuple-element.47.refs_0_, bf16[128,6144]{1,0:T(8,128)(2,1)} %collective-permute-done.4.refs_1_), custom_call_target="tpu_custom_call" | custom-call | flops 30000001024 | bytes 5000000 | tf_op jit(solution)/shard_map/pallas_call | solution.py:315
  58.0 2.9 %collective-permute-start.5 = (bf16[32,6144]{1,0:T(8,128)(2,1)}, bf16[32,6144]{1,0:T(8,128)(2,1)S(1)}, u32[]{:S(2)}, u32[]{:S(2)}) collective-permute-start(bf16[32,6144]{1,0:T(8,128)(2,1)} %get-tuple-element.50), channel_id=1, source_target_pairs={{0,32},{32,0},{64,96},{96,64},{1,33},{33,1},{65,97},{97,65},{2,34}... | collective-permute-start | bytes 1179656 | tf_op jit(solution)/shard_map/ppermute | solution.py:332
  60.9 4.4 %collective-permute-start.6 = (bf16[32,6144]{1,0:T(8,128)(2,1)}, bf16[32,6144]{1,0:T(8,128)(2,1)}, u32[]{:S(2)}, u32[]{:S(2)}) collective-permute-start(bf16[32,6144]{1,0:T(8,128)(2,1)} %get-tuple-element.51), channel_id=1, source_target_pairs={{0,64},{32,96},{64,0},{96,32},{1,65},{33,97},{65,1},{97,33},{2,66}... | collective-permute-start | bytes 1179656 | tf_op jit(solution)/shard_map/ppermute | solution.py:332
  65.2 2.3 %collective-permute-start.7 = (bf16[32,6144]{1,0:T(8,128)(2,1)}, bf16[32,6144]{1,0:T(8,128)(2,1)}, u32[]{:S(2)}, u32[]{:S(2)}) collective-permute-start(bf16[32,6144]{1,0:T(8,128)(2,1)} %get-tuple-element.52), channel_id=1, source_target_pairs={{0,96},{32,64},{64,32},{96,0},{1,97},{33,65},{65,33},{97,1},{2,98}... | collective-permute-start | bytes 1179656 | tf_op jit(solution)/shard_map/ppermute | solution.py:332
  69.8 4.0 %collective-permute-start.9 = (bf16[256,512]{1,0:T(8,128)(2,1)}, bf16[256,512]{1,0:T(8,128)(2,1)}, u32[]{:S(2)}, u32[]{:S(2)}) collective-permute-start(bf16[256,512]{1,0:T(8,128)(2,1)} %get-tuple-element.54), channel_id=1, source_target_pairs={{0,8},{4,12},{8,0},{12,4},{1,9},{5,13},{9,1},{13,5},{2,10},{6,14},... | collective-permute-start | bytes 786440 | tf_op jit(solution)/shard_map/ppermute | solution.py:332
  73.8 7.0 %all-to-all-done.2.refs_1_ = bf16[16,64,512]{2,1,0:T(8,128)(2,1)} async-done(((bf16[16,64,512]{2,1,0:T(8,128)(2,1)}), bf16[16,64,512]{2,1,0:T(8,128)(2,1)}, u32[]{:S(2)}, u32[]{:S(2)}) %all-to-all-start.2) | async-done | bytes 1048608 | tf_op jit(solution)/shard_map/all_to_all | solution.py:336
  80.8 2.6 %shard_map.146 = (bf16[128,256]{1,0:T(8,128)(2,1)}, bf16[256,512]{1,0:T(8,128)(2,1)}) custom-call(bf16[256,512]{1,0:T(8,128)(2,1)} %get-tuple-element.42.refs_1_.refs_0_, bf16[16,64,512]{2,1,0:T(8,128)(2,1)} %all-to-all-done.2.refs_1_), custom_call_target="tpu_custom_call" | custom-call | flops 40000000 | bytes 1000000 | tf_op jit(solution)/shard_map/pallas_call | solution.py:315
  83.4 8.0 %all-to-all-start.3 = ((bf16[8,32,512]{2,1,0:T(8,128)(2,1)}), bf16[8,32,512]{2,1,0:T(8,128)(2,1)S(1)}, u32[]{:S(2)}, u32[]{:S(2)}) async-start(bf16[8,32,512]{2,1,0:T(8,128)(2,1)} %bitcast.9), calls=%async_computation.3 | async-start | bytes 524288 | tf_op jit(solution)/shard_map/all_to_all | solution.py:336
  91.4 6.4 %all-to-all-done.3.refs_4_ = bf16[8,32,512]{2,1,0:T(8,128)(2,1)S(1)} async-done(((bf16[8,32,512]{2,1,0:T(8,128)(2,1)}), bf16[8,32,512]{2,1,0:T(8,128)(2,1)S(1)}, u32[]{:S(2)}, u32[]{:S(2)}) %all-to-all-start.3) | async-done | bytes 262176 | tf_op jit(solution)/shard_map/all_to_all | solution.py:336
  98.6 2.4 %shard_map.147 = bf16[32,6656]{1,0:T(8,128)(2,1)} custom-call(bf16[32,6144]{1,0:T(8,128)(2,1)} %get-tuple-element.55.refs_0_, bf16[32,6144]{1,0:T(8,128)(2,1)} %copy-done.1, bf16[32,6144]{1,0:T(8,128)(2,1)} %collective-permute-done.6.refs_2_, bf16[32,6144]{1,0:T(8,128)(2,1)} %collective-permute-done.7.refs_3_, bf16[8,32,512]{2,1,0:T(8,128)(2,1)} %copy-done), custom_call_target="tpu_custom_call" | custom-call | flops 1000000 | bytes 2000000 | tf_op jit(solution)/shard_map/pallas_call | solution.py:315
  101.0 12.1 %all-to-all-start.4 = ((bf16[4,8,6656]{2,1,0:T(8,128)(2,1)}), bf16[4,8,6656]{2,1,0:T(8,128)(2,1)S(1)}, u32[]{:S(2)}, u32[]{:S(2)}) async-start(bf16[4,8,6656]{2,1,0:T(8,128)(2,1)} %bitcast.8), calls=%async_computation.4 | async-start | bytes 851968 | tf_op jit(solution)/shard_map/all_to_all | solution.py:336
  117.3 4.5 %collective-permute-done.10.refs_1_ = bf16[256,512]{1,0:T(8,128)(2,1)} collective-permute-done((bf16[256,512]{1,0:T(8,128)(2,1)}, bf16[256,512]{1,0:T(8,128)(2,1)}, u32[]{:S(2)}, u32[]{:S(2)}) %collective-permute-start.10) | collective-permute-done | bytes 262176 | tf_op jit(solution)/shard_map/ppermute | solution.py:332
  121.8 5.3 %collective-permute-done.11.refs_2_ = bf16[256,512]{1,0:T(8,128)(2,1)} collective-permute-done((bf16[256,512]{1,0:T(8,128)(2,1)}, bf16[256,512]{1,0:T(8,128)(2,1)}, u32[]{:S(2)}, u32[]{:S(2)}) %collective-permute-start.11) | collective-permute-done | bytes 262176 | tf_op jit(solution)/shard_map/ppermute | solution.py:332
  127.1 2.4 %shard_map.148 = (bf16[128,512]{1,0:T(8,128)(2,1)}, bf16[128,512]{1,0:T(8,128)(2,1)}) custom-call(f32[256,512]{1,0:T(8,128)} %get-tuple-element.44.refs_0_, bf16[256,512]{1,0:T(8,128)(2,1)} %collective-permute-done.10.refs_1_, bf16[256,512]{1,0:T(8,128)(2,1)} %collective-permute-done.11.refs_2_, bf16[256,512]{1,0:T(8,128)(2,1)} %copy-done.2, ...), custom_call_target="tpu_custom_call" | custom-call | flops 40000000 | bytes 2000000 | tf_op jit(solution)/shard_map/pallas_call | solution.py:315
  129.6 7.8 %all-to-all-done.4.refs_0_ = bf16[4,8,6656]{2,1,0:T(8,128)(2,1)S(1)} async-done(((bf16[4,8,6656]{2,1,0:T(8,128)(2,1)}), bf16[4,8,6656]{2,1,0:T(8,128)(2,1)S(1)}, u32[]{:S(2)}, u32[]{:S(2)}) %all-to-all-start.4) | async-done | bytes 426016 | tf_op jit(solution)/shard_map/all_to_all | solution.py:336
  (36 shorter events, 16.1 us)
Async XLA Ops:
  2.7 21.1 %all-to-all-start = ((f32[16,8,256]{2,1,0:T(8,128)}), f32[16,8,256]{2,1,0:T(8,128)S(1)}, u32[]{:S(2)}, u32[]{:S(2)}) async-start(f32[16,8,256]{2,1,0:T(8,128)} %bitcast.10), calls=%async_computation | async-start | bytes 262144 | tf_op jit(solution)/shard_map/all_to_all | solution.py:336
  10.8 18.7 %collective-permute-start.3 = (bf16[256,512]{1,0:T(8,128)(2,1)}, bf16[256,512]{1,0:T(8,128)(2,1)S(1)}, u32[]{:S(2)}, u32[]{:S(2)}) collective-permute-start(bf16[256,512]{1,0:T(8,128)(2,1)} %get-tuple-element.42.refs_1_.refs_0_), channel_id=1, source_target_pairs={{0,8},{4,12},{8,0},{12,4},{1,9},{5,13},{9,1},{13,5},{2,10},{6,14},... | collective-permute-start | bytes 786440 | tf_op jit(solution)/shard_map/ppermute | solution.py:332
  14.8 14.8 %collective-permute-start.2 = (bf16[256,512]{1,0:T(8,128)(2,1)}, bf16[256,512]{1,0:T(8,128)(2,1)S(1)}, u32[]{:S(2)}, u32[]{:S(2)}) collective-permute-start(bf16[256,512]{1,0:T(8,128)(2,1)} %get-tuple-element.42.refs_1_.refs_0_), channel_id=1, source_target_pairs={{0,4},{4,0},{8,12},{12,8},{1,5},{5,1},{9,13},{13,9},{2,6},{6,2},{1... | collective-permute-start | bytes 786440 | tf_op jit(solution)/shard_map/ppermute | solution.py:332
  17.0 12.6 %collective-permute-start.1 = (bf16[256,512]{1,0:T(8,128)(2,1)}, bf16[256,512]{1,0:T(8,128)(2,1)S(1)}, u32[]{:S(2)}, u32[]{:S(2)}) collective-permute-start(bf16[256,512]{1,0:T(8,128)(2,1)} %get-tuple-element.42.refs_1_.refs_0_), channel_id=1, source_target_pairs={{0,2},{1,3},{2,0},{3,1},{4,6},{5,7},{6,4},{7,5},{8,10},{9,11},{10,... | collective-permute-start | bytes 786440 | tf_op jit(solution)/shard_map/ppermute | solution.py:332
  21.6 10.5 %collective-permute-start = (bf16[256,512]{1,0:T(8,128)(2,1)}, bf16[256,512]{1,0:T(8,128)(2,1)S(1)}, u32[]{:S(2)}, u32[]{:S(2)}) collective-permute-start(bf16[256,512]{1,0:T(8,128)(2,1)} %get-tuple-element.42.refs_1_.refs_0_), channel_id=1, source_target_pairs={{0,1},{1,0},{2,3},{3,2},{4,5},{5,4},{6,7},{7,6},{8,9},{9,8},{10,11... | collective-permute-start | bytes 786440 | tf_op jit(solution)/shard_map/ppermute | solution.py:332
  24.5 10.3 %all-to-all-start.1 = ((bf16[16,8,256]{2,1,0:T(8,128)(2,1)}), bf16[16,8,256]{2,1,0:T(8,128)(2,1)S(1)}, u32[]{:S(2)}, u32[]{:S(2)}) async-start(bf16[16,8,256]{2,1,0:T(8,128)(2,1)} %broadcast_in_dim.3), calls=%async_computation.1 | async-start | bytes 131072 | tf_op jit(solution)/shard_map/all_to_all | solution.py:336
  29.5 5.2 %copy-start.4 = (bf16[256,512]{1,0:T(8,128)(2,1)}, bf16[256,512]{1,0:T(8,128)(2,1)S(1)}, u32[]{:S(2)}) copy-start(bf16[256,512]{1,0:T(8,128)(2,1)S(1)} %collective-permute-done.3.refs_5_) | copy-start | bytes 786436
  29.5 5.2 %copy-start.5 = (bf16[256,512]{1,0:T(8,128)(2,1)}, bf16[256,512]{1,0:T(8,128)(2,1)S(1)}, u32[]{:S(2)}) copy-start(bf16[256,512]{1,0:T(8,128)(2,1)S(1)} %collective-permute-done.2.refs_4_) | copy-start | bytes 786436
  29.6 5.2 %copy-start.6 = (bf16[256,512]{1,0:T(8,128)(2,1)}, bf16[256,512]{1,0:T(8,128)(2,1)S(1)}, u32[]{:S(2)}) copy-start(bf16[256,512]{1,0:T(8,128)(2,1)S(1)} %collective-permute-done.1.refs_3_) | copy-start | bytes 786436
  32.1 2.7 %copy-start.7 = (bf16[256,512]{1,0:T(8,128)(2,1)}, bf16[256,512]{1,0:T(8,128)(2,1)S(1)}, u32[]{:S(2)}) copy-start(bf16[256,512]{1,0:T(8,128)(2,1)S(1)} %collective-permute-done.refs_2_) | copy-start | bytes 786436
  43.7 11.3 %collective-permute-start.4 = (bf16[128,6144]{1,0:T(8,128)(2,1)}, bf16[128,6144]{1,0:T(8,128)(2,1)}, u32[]{:S(2)}, u32[]{:S(2)}) collective-permute-start(bf16[128,6144]{1,0:T(8,128)(2,1)} %get-tuple-element.48), channel_id=1, source_target_pairs={{0,16},{16,0},{1,17},{17,1},{2,18},{18,2},{3,19},{19,3},{4,20},{20... | collective-permute-start | bytes 4718600 | tf_op jit(solution)/shard_map/ppermute | solution.py:332
  49.3 31.5 %all-to-all-start.2 = ((bf16[16,64,512]{2,1,0:T(8,128)(2,1)}), bf16[16,64,512]{2,1,0:T(8,128)(2,1)}, u32[]{:S(2)}, u32[]{:S(2)}) async-start(bf16[16,64,512]{2,1,0:T(8,128)(2,1)} %get-tuple-element.59), calls=%async_computation.2 | async-start | bytes 2097152 | tf_op jit(solution)/shard_map/all_to_all | solution.py:336
  58.0 33.4 %collective-permute-start.5 = (bf16[32,6144]{1,0:T(8,128)(2,1)}, bf16[32,6144]{1,0:T(8,128)(2,1)S(1)}, u32[]{:S(2)}, u32[]{:S(2)}) collective-permute-start(bf16[32,6144]{1,0:T(8,128)(2,1)} %get-tuple-element.50), channel_id=1, source_target_pairs={{0,32},{32,0},{64,96},{96,64},{1,33},{33,1},{65,97},{97,65},{2,34}... | collective-permute-start | bytes 1179656 | tf_op jit(solution)/shard_map/ppermute | solution.py:332
  60.9 30.5 %collective-permute-start.6 = (bf16[32,6144]{1,0:T(8,128)(2,1)}, bf16[32,6144]{1,0:T(8,128)(2,1)}, u32[]{:S(2)}, u32[]{:S(2)}) collective-permute-start(bf16[32,6144]{1,0:T(8,128)(2,1)} %get-tuple-element.51), channel_id=1, source_target_pairs={{0,64},{32,96},{64,0},{96,32},{1,65},{33,97},{65,1},{97,33},{2,66}... | collective-permute-start | bytes 1179656 | tf_op jit(solution)/shard_map/ppermute | solution.py:332
  65.2 26.2 %collective-permute-start.7 = (bf16[32,6144]{1,0:T(8,128)(2,1)}, bf16[32,6144]{1,0:T(8,128)(2,1)}, u32[]{:S(2)}, u32[]{:S(2)}) collective-permute-start(bf16[32,6144]{1,0:T(8,128)(2,1)} %get-tuple-element.52), channel_id=1, source_target_pairs={{0,96},{32,64},{64,32},{96,0},{1,97},{33,65},{65,33},{97,1},{2,98}... | collective-permute-start | bytes 1179656 | tf_op jit(solution)/shard_map/ppermute | solution.py:332
  67.6 23.8 %collective-permute-start.8 = (bf16[256,512]{1,0:T(8,128)(2,1)}, bf16[256,512]{1,0:T(8,128)(2,1)S(1)}, u32[]{:S(2)}, u32[]{:S(2)}) collective-permute-start(bf16[256,512]{1,0:T(8,128)(2,1)} %get-tuple-element.53), channel_id=1, source_target_pairs={{0,4},{4,0},{8,12},{12,8},{1,5},{5,1},{9,13},{13,9},{2,6},{6,2},{1... | collective-permute-start | bytes 786440 | tf_op jit(solution)/shard_map/ppermute | solution.py:332
  69.8 21.6 %collective-permute-start.9 = (bf16[256,512]{1,0:T(8,128)(2,1)}, bf16[256,512]{1,0:T(8,128)(2,1)}, u32[]{:S(2)}, u32[]{:S(2)}) collective-permute-start(bf16[256,512]{1,0:T(8,128)(2,1)} %get-tuple-element.54), channel_id=1, source_target_pairs={{0,8},{4,12},{8,0},{12,4},{1,9},{5,13},{9,1},{13,5},{2,10},{6,14},... | collective-permute-start | bytes 786440 | tf_op jit(solution)/shard_map/ppermute | solution.py:332
  83.4 14.5 %all-to-all-start.3 = ((bf16[8,32,512]{2,1,0:T(8,128)(2,1)}), bf16[8,32,512]{2,1,0:T(8,128)(2,1)S(1)}, u32[]{:S(2)}, u32[]{:S(2)}) async-start(bf16[8,32,512]{2,1,0:T(8,128)(2,1)} %bitcast.9), calls=%async_computation.3 | async-start | bytes 524288 | tf_op jit(solution)/shard_map/all_to_all | solution.py:336
  91.4 35.7 %copy-start.2 = (bf16[256,512]{1,0:T(8,128)(2,1)}, bf16[256,512]{1,0:T(8,128)(2,1)S(1)}, u32[]{:S(2)}) copy-start(bf16[256,512]{1,0:T(8,128)(2,1)S(1)} %collective-permute-done.8.refs_3_) | copy-start | bytes 786436
  91.4 6.5 %copy-start.1 = (bf16[32,6144]{1,0:T(8,128)(2,1)}, bf16[32,6144]{1,0:T(8,128)(2,1)S(1)}, u32[]{:S(2)}) copy-start(bf16[32,6144]{1,0:T(8,128)(2,1)S(1)} %collective-permute-done.5.refs_1_) | copy-start | bytes 1179652
  97.9 0.7 copy-start
  101.0 36.4 %all-to-all-start.4 = ((bf16[4,8,6656]{2,1,0:T(8,128)(2,1)}), bf16[4,8,6656]{2,1,0:T(8,128)(2,1)S(1)}, u32[]{:S(2)}, u32[]{:S(2)}) async-start(bf16[4,8,6656]{2,1,0:T(8,128)(2,1)} %bitcast.8), calls=%async_computation.4 | async-start | bytes 851968 | tf_op jit(solution)/shard_map/all_to_all | solution.py:336
  113.1 8.7 %collective-permute-start.10 = (bf16[256,512]{1,0:T(8,128)(2,1)}, bf16[256,512]{1,0:T(8,128)(2,1)}, u32[]{:S(2)}, u32[]{:S(2)}) collective-permute-start(bf16[256,512]{1,0:T(8,128)(2,1)} %get-tuple-element.62), channel_id=1, source_target_pairs={{0,1},{1,0},{2,3},{3,2},{4,5},{5,4},{6,7},{7,6},{8,9},{9,8},{10,11... | collective-permute-start | bytes 786440 | tf_op jit(solution)/shard_map/ppermute | solution.py:332
  115.0 12.1 %collective-permute-start.11 = (bf16[256,512]{1,0:T(8,128)(2,1)}, bf16[256,512]{1,0:T(8,128)(2,1)}, u32[]{:S(2)}, u32[]{:S(2)}) collective-permute-start(bf16[256,512]{1,0:T(8,128)(2,1)} %get-tuple-element.63), channel_id=1, source_target_pairs={{0,2},{1,3},{2,0},{3,1},{4,6},{5,7},{6,4},{7,5},{8,10},{9,11},{10,... | collective-permute-start | bytes 786440 | tf_op jit(solution)/shard_map/ppermute | solution.py:332
  (1 other events, 0.6 us)

commit v4 on v3

--- a/solution.py
+++ b/solution.py
@@ -77,16 +77,6 @@
 
 def fold(low):
     return jnp.concatenate([low[:LOW], low[LOW:]], axis=1).astype(BF16)
-
-
-def unfold(pieces):
-    total = pieces[0].astype(F32)
-    for n in range(1, pieces.shape[0]):
-        total = total + pieces[n].astype(F32)
-    total = total.astype(BF16)
-    first = jnp.concatenate([total[:, :ROWS], total[:, 2 * ROWS : 3 * ROWS]], axis=0)
-    second = jnp.concatenate([total[:, ROWS : 2 * ROWS], total[:, 3 * ROWS :]], axis=0)
-    return first, second
 
 
 def low_body(tokens, cotangent, up_left, down_right, own, low, u, d, sems):
@@ -189,14 +179,25 @@
     finish(out_going)
 
 
-def mini_body(scale, own, pieces, low, mini):
+def mini_body(scale, own_at, pieces_at, low, mini, own, pieces, sems):
+    copies = Copies(sems)
+    coming = [copies.start(pieces_at.at[n : n + 4], pieces.at[n : n + 4]) for n in range(0, pieces.shape[0], 4)]
+    last = copies.start(own_at, own)
     pair = pick_mini()
-    low_down, low_pre = unfold(pieces)
+    total = jnp.zeros((LOW, SLAB), F32)
+    for n, copy in enumerate(coming):
+        copy.wait()
+        for m in range(4 * n, 4 * n + 4):
+            total = total + pieces[m].astype(F32)
+    total = total.astype(BF16)
+    low_down = jnp.concatenate([total[:, :ROWS], total[:, 2 * ROWS : 3 * ROWS]], axis=0)
+    low_pre = jnp.concatenate([total[:, ROWS : 2 * ROWS], total[:, 3 * ROWS :]], axis=0)
     low[:, :ROWS] = low_down
     low[:, ROWS:] = low_pre
     zero = jnp.zeros_like(low_pre)
     upper = mt(pair, jnp.concatenate([low_pre, zero], axis=1)).astype(BF16)
     lower = mt(pair, jnp.concatenate([zero, low_down], axis=1)).astype(BF16)
+    last.wait()
     value = mm(upper, own[:ROWS, :]) + mm(lower, own[ROWS:, :])
     mini[...] = (value * scale).astype(BF16)
 
@@ -380,18 +381,22 @@
     pieces = call(
         split_body,
         [((32, MAIN), BF16)] * 4,
-        "aa aaaa",
+        "ha aaaa",
         [(half, BF16)] * 2,
         6 * STEPS,
         cost=(30_000_000_000, 5_000_000),
+        limit=SMALL,
     )(keep, got)
-    pieces = list(pieces[:1]) + [swap(pieces[mask], "x", mask) for mask in (1, 2, 3)]
+    two_off = swap(pieces[2], "x", 2)
+    pieces = [pieces[0], two_off] + [swap(pieces[mask], "x", mask) for mask in (1, 3)]
     far = [swap(term, axis, mask) for term, (axis, mask) in zip(terms[2:], hops[2:])]
 
     low, mini = call(
         functools.partial(mini_body, scale),
         [(lows, BF16), ((2 * ROWS, MINI), BF16)],
-        "cc cc",
+        "aa cc",
+        [shape(own), shape(low)],
+        5,
         cost=(40_000_000, 1_000_000),
     )(own, low)
     mini = exchange(mini.reshape(8, -1, MINI), ("x", "core"))
@@ -404,6 +409,7 @@
         [((4, 32, MAIN), BF16), (mini.shape, BF16), ((32, MAIN + MINI), BF16)],
         5 * STEPS + 2,
         cost=(1_000_000, 2_000_000),
+        limit=SMALL,
     )(*pieces, mini)[0]
     near, pieces, low = lax.optimization_barrier((terms[:2], pieces, low))
     pieces = exchange(pieces.reshape(SIZES[0], 8, -1), "zh")

time: 139 us -> 138 us (level)
  transfers between devices with their start and end apart: 17 -> 17, of which waited for: 7 -> 7; matrix products, arithmetic and copies ran while one was open for 1% -> 1% of each run, Pallas kernels for 6% -> 5%
where the time goes in v4:
time: 138 us; the launch traced here: 137 us
  starting transfers between devices  76.5 us (55%)
  waiting for transfers between devices  36.5 us (26%)
  Pallas kernels  20.7 us (15%)
  local copies, waits for them, and re-layouts  1.99 us (1%)
    all_to_all x5, starting transfers between devices, exchange(): return lax.all_to_all(block, axis, 0, 0)  38.4 us
    ppermute x12, starting transfers between devices, swap(): return lax.ppermute(block, axis, [(i, i ^ mask) for i in range(count)])  38.1 us
    all_to_all x5, waiting for transfers between devices, exchange(): return lax.all_to_all(block, axis, 0, 0)  24.4 us
    pallas_call x7, Pallas kernels, run(): pl.pallas_call(kernel, out_shape=[jax.ShapeDtypeStruct(s, d) for s, d in...  20.7 us
    ppermute x12, waiting for transfers between devices, swap(): return lax.ppermute(block, axis, [(i, i ^ mask) for i in range(count)])  12 us
  transfers between devices with their start and end apart: 17, of which 7 were waited for; matrix products, arithmetic and copies ran while one was open for 1% of the time, Pallas kernels for 5%

profile of v4, /device:TPU:33, one launch (start us, length us, event | category | flops | bytes accessed | tf_op | source)
XLA Modules:
  0.0 137.1 jit_solution(17077817735673058531)
XLA Ops:
  2.7 8.1 %all-to-all-start = ((f32[16,8,256]{2,1,0:T(8,128)}), f32[16,8,256]{2,1,0:T(8,128)S(1)}, u32[]{:S(2)}, u32[]{:S(2)}) async-start(f32[16,8,256]{2,1,0:T(8,128)} %bitcast.9), calls=%async_computation | async-start | bytes 262144 | tf_op jit(solution)/shard_map/all_to_all | solution.py:337
  10.8 4.0 %collective-permute-start.3 = (bf16[256,512]{1,0:T(8,128)(2,1)}, bf16[256,512]{1,0:T(8,128)(2,1)S(1)}, u32[]{:S(2)}, u32[]{:S(2)}) collective-permute-start(bf16[256,512]{1,0:T(8,128)(2,1)} %get-tuple-element.42.refs_1_.refs_0_), channel_id=1, source_target_pairs={{0,8},{4,12},{8,0},{12,4},{1,9},{5,13},{9,1},{13,5},{2,10},{6,14},... | collective-permute-start | bytes 786440 | tf_op jit(solution)/shard_map/ppermute | solution.py:333
  17.0 4.6 %collective-permute-start.1 = (bf16[256,512]{1,0:T(8,128)(2,1)}, bf16[256,512]{1,0:T(8,128)(2,1)S(1)}, u32[]{:S(2)}, u32[]{:S(2)}) collective-permute-start(bf16[256,512]{1,0:T(8,128)(2,1)} %get-tuple-element.42.refs_1_.refs_0_), channel_id=1, source_target_pairs={{0,2},{1,3},{2,0},{3,1},{4,6},{5,7},{6,4},{7,5},{8,10},{9,11},{10,... | collective-permute-start | bytes 786440 | tf_op jit(solution)/shard_map/ppermute | solution.py:333
  24.5 4.5 %all-to-all-start.1 = ((bf16[16,8,256]{2,1,0:T(8,128)(2,1)}), bf16[16,8,256]{2,1,0:T(8,128)(2,1)S(1)}, u32[]{:S(2)}, u32[]{:S(2)}) async-start(bf16[16,8,256]{2,1,0:T(8,128)(2,1)} %broadcast_in_dim.3), calls=%async_computation.1 | async-start | bytes 131072 | tf_op jit(solution)/shard_map/all_to_all | solution.py:337
  29.6 2.5 %collective-permute-done.refs_2_ = bf16[256,512]{1,0:T(8,128)(2,1)S(1)} collective-permute-done((bf16[256,512]{1,0:T(8,128)(2,1)}, bf16[256,512]{1,0:T(8,128)(2,1)S(1)}, u32[]{:S(2)}, u32[]{:S(2)}) %collective-permute-start) | collective-permute-done | bytes 262176 | tf_op jit(solution)/shard_map/ppermute | solution.py:333
  32.1 2.7 %all-to-all-done.1 = bf16[16,8,256]{2,1,0:T(8,128)(2,1)S(1)} async-done(((bf16[16,8,256]{2,1,0:T(8,128)(2,1)}), bf16[16,8,256]{2,1,0:T(8,128)(2,1)S(1)}, u32[]{:S(2)}, u32[]{:S(2)}) %all-to-all-start.1) | async-done | bytes 65568 | tf_op jit(solution)/shard_map/all_to_all | solution.py:337
  35.4 8.3 %shard_map.144 = (f32[256,512]{1,0:T(8,128)}, bf16[256,512]{1,0:T(8,128)(2,1)}, bf16[256,512]{1,0:T(8,128)(2,1)}, bf16[256,512]{1,0:T(8,128)(2,1)}, bf16[256,512...) custom-call(s32[2]{0:T(128)} %pad_add_fusion.refs_0_, ...), custom_call_target="tpu_custom_call" | custom-call | flops 1500000000 | bytes 10000000 | tf_op jit(solution)/shard_map/pallas_call | solution.py:316
  43.7 5.6 %collective-permute-start.4 = (bf16[128,6144]{1,0:T(8,128)(2,1)}, bf16[128,6144]{1,0:T(8,128)(2,1)S(1)}, u32[]{:S(2)}, u32[]{:S(2)}) collective-permute-start(bf16[128,6144]{1,0:T(8,128)(2,1)} %get-tuple-element.48), channel_id=1, source_target_pairs={{0,16},{16,0},{1,17},{17,1},{2,18},{18,2},{3,19},{19,3},{4,20},{20... | collective-permute-start | bytes 4718600 | tf_op jit(solution)/shard_map/ppermute | solution.py:333
  49.3 5.7 %all-to-all-start.2 = ((bf16[16,64,512]{2,1,0:T(8,128)(2,1)}), bf16[16,64,512]{2,1,0:T(8,128)(2,1)}, u32[]{:S(2)}, u32[]{:S(2)}) async-start(bf16[16,64,512]{2,1,0:T(8,128)(2,1)} %get-tuple-element.59), calls=%async_computation.2 | async-start | bytes 2097152 | tf_op jit(solution)/shard_map/all_to_all | solution.py:337
  55.0 2.5 %shard_map.145 = (bf16[32,6144]{1,0:T(8,128)(2,1)S(1)}, bf16[32,6144]{1,0:T(8,128)(2,1)}, bf16[32,6144]{1,0:T(8,128)(2,1)}, bf16[32,6144]{1,0:T(8,128)(2,1)}) custom-call(bf16[128,6144]{1,0:T(8,128)(2,1)} %get-tuple-element.47.refs_0_, bf16[128,6144]{1,0:T(8,128)(2,1)S(1)} %collective-permute-done.4.refs_1_), custom_call_target="tpu_custom_call" | custom-call | flops 30000001024 | bytes 5000000 | tf_op jit(solution)/shard_map/pallas_call | solution.py:316
  57.5 4.4 %collective-permute-start.5 = (bf16[32,6144]{1,0:T(8,128)(2,1)}, bf16[32,6144]{1,0:T(8,128)(2,1)S(1)}, u32[]{:S(2)}, u32[]{:S(2)}) collective-permute-start(bf16[32,6144]{1,0:T(8,128)(2,1)} %get-tuple-element.50), channel_id=1, source_target_pairs={{0,64},{32,96},{64,0},{96,32},{1,65},{33,97},{65,1},{97,33},{2,66}... | collective-permute-start | bytes 1179656 | tf_op jit(solution)/shard_map/ppermute | solution.py:333
  64.2 2.5 %collective-permute-start.7 = (bf16[32,6144]{1,0:T(8,128)(2,1)}, bf16[32,6144]{1,0:T(8,128)(2,1)}, u32[]{:S(2)}, u32[]{:S(2)}) collective-permute-start(bf16[32,6144]{1,0:T(8,128)(2,1)} %get-tuple-element.52), channel_id=1, source_target_pairs={{0,96},{32,64},{64,32},{96,0},{1,97},{33,65},{65,33},{97,1},{2,98}... | collective-permute-start | bytes 1179656 | tf_op jit(solution)/shard_map/ppermute | solution.py:333
  68.9 4.0 %collective-permute-start.9 = (bf16[256,512]{1,0:T(8,128)(2,1)}, bf16[256,512]{1,0:T(8,128)(2,1)}, u32[]{:S(2)}, u32[]{:S(2)}) collective-permute-start(bf16[256,512]{1,0:T(8,128)(2,1)} %get-tuple-element.54), channel_id=1, source_target_pairs={{0,8},{4,12},{8,0},{12,4},{1,9},{5,13},{9,1},{13,5},{2,10},{6,14},... | collective-permute-start | bytes 786440 | tf_op jit(solution)/shard_map/ppermute | solution.py:333
  72.9 7.9 %all-to-all-done.2.refs_1_ = bf16[16,64,512]{2,1,0:T(8,128)(2,1)} async-done(((bf16[16,64,512]{2,1,0:T(8,128)(2,1)}), bf16[16,64,512]{2,1,0:T(8,128)(2,1)}, u32[]{:S(2)}, u32[]{:S(2)}) %all-to-all-start.2) | async-done | bytes 1048608 | tf_op jit(solution)/shard_map/all_to_all | solution.py:337
  80.8 2.5 %shard_map.146 = (bf16[128,256]{1,0:T(8,128)(2,1)}, bf16[256,512]{1,0:T(8,128)(2,1)}) custom-call(bf16[256,512]{1,0:T(8,128)(2,1)} %get-tuple-element.42.refs_1_.refs_0_, bf16[16,64,512]{2,1,0:T(8,128)(2,1)} %all-to-all-done.2.refs_1_), custom_call_target="tpu_custom_call" | custom-call | flops 40000000 | bytes 1000000 | tf_op jit(solution)/shard_map/pallas_call | solution.py:316
  83.3 8.0 %all-to-all-start.3 = ((bf16[8,32,512]{2,1,0:T(8,128)(2,1)}), bf16[8,32,512]{2,1,0:T(8,128)(2,1)S(1)}, u32[]{:S(2)}, u32[]{:S(2)}) async-start(bf16[8,32,512]{2,1,0:T(8,128)(2,1)} %bitcast.8), calls=%async_computation.3 | async-start | bytes 524288 | tf_op jit(solution)/shard_map/all_to_all | solution.py:337
  91.3 6.5 %all-to-all-done.3.refs_4_ = bf16[8,32,512]{2,1,0:T(8,128)(2,1)S(1)} async-done(((bf16[8,32,512]{2,1,0:T(8,128)(2,1)}), bf16[8,32,512]{2,1,0:T(8,128)(2,1)S(1)}, u32[]{:S(2)}, u32[]{:S(2)}) %all-to-all-start.3) | async-done | bytes 262176 | tf_op jit(solution)/shard_map/all_to_all | solution.py:337
  97.8 2.2 %shard_map.147 = bf16[32,6656]{1,0:T(8,128)(2,1)} custom-call(bf16[32,6144]{1,0:T(8,128)(2,1)S(1)} %get-tuple-element.55.refs_0_, bf16[32,6144]{1,0:T(8,128)(2,1)S(1)} %collective-permute-done.5.refs_1_, bf16[32,6144]{1,0:T(8,128)(2,1)} %collective-permute-done.6.refs_2_, bf16[32,6144]{1,0:T(8,128)(2,1)} %collective-permute-done.7.refs_3_, ...), custom_call_target="tpu_custom_call" | custom-call | flops 1000000 | bytes 2000000 | tf_op jit(solution)/shard_map/pallas_call | solution.py:316
  100.0 12.1 %all-to-all-start.4 = ((bf16[4,8,6656]{2,1,0:T(8,128)(2,1)}), bf16[4,8,6656]{2,1,0:T(8,128)(2,1)S(1)}, u32[]{:S(2)}, u32[]{:S(2)}) async-start(bf16[4,8,6656]{2,1,0:T(8,128)(2,1)} %bitcast.5), calls=%async_computation.4 | async-start | bytes 851968 | tf_op jit(solution)/shard_map/all_to_all | solution.py:337
  114.0 2.3 %collective-permute-start.11 = (bf16[256,512]{1,0:T(8,128)(2,1)S(1)}, bf16[256,512]{1,0:T(8,128)(2,1)S(1)}, u32[]{:S(2)}, u32[]{:S(2)}) collective-permute-start(bf16[256,512]{1,0:T(8,128)(2,1)S(1)} %copy-done.3), channel_id=1, source_target_pairs={{0,2},{1,3},{2,0},{3,1},{4,6},{5,7},{6,4},{7,5},{8,10},{9,11},{10,... | collective-permute-start | bytes 786440 | tf_op jit(solution)/shard_map/ppermute | solution.py:333
  116.3 4.1 %collective-permute-done.10.refs_1_ = bf16[256,512]{1,0:T(8,128)(2,1)S(1)} collective-permute-done((bf16[256,512]{1,0:T(8,128)(2,1)S(1)}, bf16[256,512]{1,0:T(8,128)(2,1)S(1)}, u32[]{:S(2)}, u32[]{:S(2)}) %collective-permute-start.10) | collective-permute-done | bytes 262176 | tf_op jit(solution)/shard_map/ppermute | solution.py:333
  120.5 5.4 %collective-permute-done.11.refs_2_ = bf16[256,512]{1,0:T(8,128)(2,1)S(1)} collective-permute-done((bf16[256,512]{1,0:T(8,128)(2,1)S(1)}, bf16[256,512]{1,0:T(8,128)(2,1)S(1)}, u32[]{:S(2)}, u32[]{:S(2)}) %collective-permute-start.11) | collective-permute-done | bytes 262176 | tf_op jit(solution)/shard_map/ppermute | solution.py:333
  126.5 2.4 %shard_map.148 = (bf16[128,512]{1,0:T(8,128)(2,1)}, bf16[128,512]{1,0:T(8,128)(2,1)}) custom-call(f32[256,512]{1,0:T(8,128)} %get-tuple-element.44.refs_0_, bf16[256,512]{1,0:T(8,128)(2,1)} %copy-done, bf16[256,512]{1,0:T(8,128)(2,1)} %copy-done.1, bf16[256,512]{1,0:T(8,128)(2,1)} %collective-permute-done.8.refs_3_, ...), custom_call_target="tpu_custom_call" | custom-call | flops 40000000 | bytes 2000000 | tf_op jit(solution)/shard_map/pallas_call | solution.py:316
  129.0 7.4 %all-to-all-done.4.refs_0_ = bf16[4,8,6656]{2,1,0:T(8,128)(2,1)S(1)} async-done(((bf16[4,8,6656]{2,1,0:T(8,128)(2,1)}), bf16[4,8,6656]{2,1,0:T(8,128)(2,1)S(1)}, u32[]{:S(2)}, u32[]{:S(2)}) %all-to-all-start.4) | async-done | bytes 426016 | tf_op jit(solution)/shard_map/all_to_all | solution.py:337
  (38 shorter events, 16.1 us)
Async XLA Ops:
  2.7 21.1 %all-to-all-start = ((f32[16,8,256]{2,1,0:T(8,128)}), f32[16,8,256]{2,1,0:T(8,128)S(1)}, u32[]{:S(2)}, u32[]{:S(2)}) async-start(f32[16,8,256]{2,1,0:T(8,128)} %bitcast.9), calls=%async_computation | async-start | bytes 262144 | tf_op jit(solution)/shard_map/all_to_all | solution.py:337
  10.8 18.7 %collective-permute-start.3 = (bf16[256,512]{1,0:T(8,128)(2,1)}, bf16[256,512]{1,0:T(8,128)(2,1)S(1)}, u32[]{:S(2)}, u32[]{:S(2)}) collective-permute-start(bf16[256,512]{1,0:T(8,128)(2,1)} %get-tuple-element.42.refs_1_.refs_0_), channel_id=1, source_target_pairs={{0,8},{4,12},{8,0},{12,4},{1,9},{5,13},{9,1},{13,5},{2,10},{6,14},... | collective-permute-start | bytes 786440 | tf_op jit(solution)/shard_map/ppermute | solution.py:333
  14.8 14.8 %collective-permute-start.2 = (bf16[256,512]{1,0:T(8,128)(2,1)}, bf16[256,512]{1,0:T(8,128)(2,1)S(1)}, u32[]{:S(2)}, u32[]{:S(2)}) collective-permute-start(bf16[256,512]{1,0:T(8,128)(2,1)} %get-tuple-element.42.refs_1_.refs_0_), channel_id=1, source_target_pairs={{0,4},{4,0},{8,12},{12,8},{1,5},{5,1},{9,13},{13,9},{2,6},{6,2},{1... | collective-permute-start | bytes 786440 | tf_op jit(solution)/shard_map/ppermute | solution.py:333
  17.0 12.6 %collective-permute-start.1 = (bf16[256,512]{1,0:T(8,128)(2,1)}, bf16[256,512]{1,0:T(8,128)(2,1)S(1)}, u32[]{:S(2)}, u32[]{:S(2)}) collective-permute-start(bf16[256,512]{1,0:T(8,128)(2,1)} %get-tuple-element.42.refs_1_.refs_0_), channel_id=1, source_target_pairs={{0,2},{1,3},{2,0},{3,1},{4,6},{5,7},{6,4},{7,5},{8,10},{9,11},{10,... | collective-permute-start | bytes 786440 | tf_op jit(solution)/shard_map/ppermute | solution.py:333
  21.6 10.5 %collective-permute-start = (bf16[256,512]{1,0:T(8,128)(2,1)}, bf16[256,512]{1,0:T(8,128)(2,1)S(1)}, u32[]{:S(2)}, u32[]{:S(2)}) collective-permute-start(bf16[256,512]{1,0:T(8,128)(2,1)} %get-tuple-element.42.refs_1_.refs_0_), channel_id=1, source_target_pairs={{0,1},{1,0},{2,3},{3,2},{4,5},{5,4},{6,7},{7,6},{8,9},{9,8},{10,11... | collective-permute-start | bytes 786440 | tf_op jit(solution)/shard_map/ppermute | solution.py:333
  24.5 10.3 %all-to-all-start.1 = ((bf16[16,8,256]{2,1,0:T(8,128)(2,1)}), bf16[16,8,256]{2,1,0:T(8,128)(2,1)S(1)}, u32[]{:S(2)}, u32[]{:S(2)}) async-start(bf16[16,8,256]{2,1,0:T(8,128)(2,1)} %broadcast_in_dim.3), calls=%async_computation.1 | async-start | bytes 131072 | tf_op jit(solution)/shard_map/all_to_all | solution.py:337
  29.5 5.2 %copy-start.5 = (bf16[256,512]{1,0:T(8,128)(2,1)}, bf16[256,512]{1,0:T(8,128)(2,1)S(1)}, u32[]{:S(2)}) copy-start(bf16[256,512]{1,0:T(8,128)(2,1)S(1)} %collective-permute-done.3.refs_5_) | copy-start | bytes 786436
  29.5 5.2 %copy-start.6 = (bf16[256,512]{1,0:T(8,128)(2,1)}, bf16[256,512]{1,0:T(8,128)(2,1)S(1)}, u32[]{:S(2)}) copy-start(bf16[256,512]{1,0:T(8,128)(2,1)S(1)} %collective-permute-done.2.refs_4_) | copy-start | bytes 786436
  29.6 5.2 %copy-start.7 = (bf16[256,512]{1,0:T(8,128)(2,1)}, bf16[256,512]{1,0:T(8,128)(2,1)S(1)}, u32[]{:S(2)}) copy-start(bf16[256,512]{1,0:T(8,128)(2,1)S(1)} %collective-permute-done.1.refs_3_) | copy-start | bytes 786436
  32.1 2.7 %copy-start.8 = (bf16[256,512]{1,0:T(8,128)(2,1)}, bf16[256,512]{1,0:T(8,128)(2,1)S(1)}, u32[]{:S(2)}) copy-start(bf16[256,512]{1,0:T(8,128)(2,1)S(1)} %collective-permute-done.refs_2_) | copy-start | bytes 786436
  43.7 11.3 %collective-permute-start.4 = (bf16[128,6144]{1,0:T(8,128)(2,1)}, bf16[128,6144]{1,0:T(8,128)(2,1)S(1)}, u32[]{:S(2)}, u32[]{:S(2)}) collective-permute-start(bf16[128,6144]{1,0:T(8,128)(2,1)} %get-tuple-element.48), channel_id=1, source_target_pairs={{0,16},{16,0},{1,17},{17,1},{2,18},{18,2},{3,19},{19,3},{4,20},{20... | collective-permute-start | bytes 4718600 | tf_op jit(solution)/shard_map/ppermute | solution.py:333
  49.3 31.5 %all-to-all-start.2 = ((bf16[16,64,512]{2,1,0:T(8,128)(2,1)}), bf16[16,64,512]{2,1,0:T(8,128)(2,1)}, u32[]{:S(2)}, u32[]{:S(2)}) async-start(bf16[16,64,512]{2,1,0:T(8,128)(2,1)} %get-tuple-element.59), calls=%async_computation.2 | async-start | bytes 2097152 | tf_op jit(solution)/shard_map/all_to_all | solution.py:337
  57.5 33.7 %collective-permute-start.5 = (bf16[32,6144]{1,0:T(8,128)(2,1)}, bf16[32,6144]{1,0:T(8,128)(2,1)S(1)}, u32[]{:S(2)}, u32[]{:S(2)}) collective-permute-start(bf16[32,6144]{1,0:T(8,128)(2,1)} %get-tuple-element.50), channel_id=1, source_target_pairs={{0,64},{32,96},{64,0},{96,32},{1,65},{33,97},{65,1},{97,33},{2,66}... | collective-permute-start | bytes 1179656 | tf_op jit(solution)/shard_map/ppermute | solution.py:333
  62.0 29.3 %collective-permute-start.6 = (bf16[32,6144]{1,0:T(8,128)(2,1)}, bf16[32,6144]{1,0:T(8,128)(2,1)}, u32[]{:S(2)}, u32[]{:S(2)}) collective-permute-start(bf16[32,6144]{1,0:T(8,128)(2,1)} %get-tuple-element.51), channel_id=1, source_target_pairs={{0,32},{32,0},{64,96},{96,64},{1,33},{33,1},{65,97},{97,65},{2,34}... | collective-permute-start | bytes 1179656 | tf_op jit(solution)/shard_map/ppermute | solution.py:333
  64.2 27.1 %collective-permute-start.7 = (bf16[32,6144]{1,0:T(8,128)(2,1)}, bf16[32,6144]{1,0:T(8,128)(2,1)}, u32[]{:S(2)}, u32[]{:S(2)}) collective-permute-start(bf16[32,6144]{1,0:T(8,128)(2,1)} %get-tuple-element.52), channel_id=1, source_target_pairs={{0,96},{32,64},{64,32},{96,0},{1,97},{33,65},{65,33},{97,1},{2,98}... | collective-permute-start | bytes 1179656 | tf_op jit(solution)/shard_map/ppermute | solution.py:333
  66.7 24.6 %collective-permute-start.8 = (bf16[256,512]{1,0:T(8,128)(2,1)}, bf16[256,512]{1,0:T(8,128)(2,1)}, u32[]{:S(2)}, u32[]{:S(2)}) collective-permute-start(bf16[256,512]{1,0:T(8,128)(2,1)} %get-tuple-element.53), channel_id=1, source_target_pairs={{0,4},{4,0},{8,12},{12,8},{1,5},{5,1},{9,13},{13,9},{2,6},{6,2},{1... | collective-permute-start | bytes 786440 | tf_op jit(solution)/shard_map/ppermute | solution.py:333
  68.9 22.4 %collective-permute-start.9 = (bf16[256,512]{1,0:T(8,128)(2,1)}, bf16[256,512]{1,0:T(8,128)(2,1)}, u32[]{:S(2)}, u32[]{:S(2)}) collective-permute-start(bf16[256,512]{1,0:T(8,128)(2,1)} %get-tuple-element.54), channel_id=1, source_target_pairs={{0,8},{4,12},{8,0},{12,4},{1,9},{5,13},{9,1},{13,5},{2,10},{6,14},... | collective-permute-start | bytes 786440 | tf_op jit(solution)/shard_map/ppermute | solution.py:333
  83.3 14.5 %all-to-all-start.3 = ((bf16[8,32,512]{2,1,0:T(8,128)(2,1)}), bf16[8,32,512]{2,1,0:T(8,128)(2,1)S(1)}, u32[]{:S(2)}, u32[]{:S(2)}) async-start(bf16[8,32,512]{2,1,0:T(8,128)(2,1)} %bitcast.8), calls=%async_computation.3 | async-start | bytes 524288 | tf_op jit(solution)/shard_map/all_to_all | solution.py:337
  91.3 20.9 %copy-start.4 = (bf16[256,512]{1,0:T(8,128)(2,1)S(1)}, bf16[256,512]{1,0:T(8,128)(2,1)}, u32[]{:S(2)}) copy-start(bf16[256,512]{1,0:T(8,128)(2,1)} %get-tuple-element.62) | copy-start | bytes 786436
  91.3 22.8 %copy-start.3 = (bf16[256,512]{1,0:T(8,128)(2,1)S(1)}, bf16[256,512]{1,0:T(8,128)(2,1)}, u32[]{:S(2)}) copy-start(bf16[256,512]{1,0:T(8,128)(2,1)} %get-tuple-element.63) | copy-start | bytes 786436
  100.0 36.4 %all-to-all-start.4 = ((bf16[4,8,6656]{2,1,0:T(8,128)(2,1)}), bf16[4,8,6656]{2,1,0:T(8,128)(2,1)S(1)}, u32[]{:S(2)}, u32[]{:S(2)}) async-start(bf16[4,8,6656]{2,1,0:T(8,128)(2,1)} %bitcast.5), calls=%async_computation.4 | async-start | bytes 851968 | tf_op jit(solution)/shard_map/all_to_all | solution.py:337
  112.1 8.4 %collective-permute-start.10 = (bf16[256,512]{1,0:T(8,128)(2,1)S(1)}, bf16[256,512]{1,0:T(8,128)(2,1)S(1)}, u32[]{:S(2)}, u32[]{:S(2)}) collective-permute-start(bf16[256,512]{1,0:T(8,128)(2,1)S(1)} %copy-done.4), channel_id=1, source_target_pairs={{0,1},{1,0},{2,3},{3,2},{4,5},{5,4},{6,7},{7,6},{8,9},{9,8},{10,11... | collective-permute-start | bytes 786440 | tf_op jit(solution)/shard_map/ppermute | solution.py:333
  114.0 11.8 %collective-permute-start.11 = (bf16[256,512]{1,0:T(8,128)(2,1)S(1)}, bf16[256,512]{1,0:T(8,128)(2,1)S(1)}, u32[]{:S(2)}, u32[]{:S(2)}) collective-permute-start(bf16[256,512]{1,0:T(8,128)(2,1)S(1)} %copy-done.3), channel_id=1, source_target_pairs={{0,2},{1,3},{2,0},{3,1},{4,6},{5,7},{6,4},{7,5},{8,10},{9,11},{10,... | collective-permute-start | bytes 786440 | tf_op jit(solution)/shard_map/ppermute | solution.py:333
  120.5 5.4 %copy-start = (bf16[256,512]{1,0:T(8,128)(2,1)}, bf16[256,512]{1,0:T(8,128)(2,1)S(1)}, u32[]{:S(2)}) copy-start(bf16[256,512]{1,0:T(8,128)(2,1)S(1)} %collective-permute-done.10.refs_1_) | copy-start | bytes 786436
  (2 other events, 1.3 us)

commit v5 on v3

--- a/solution.py
+++ b/solution.py
@@ -153,7 +153,7 @@
         low_down = low_down + mm(hidden, down_left[units, :])
         low_pre = low_pre + mt(pre, up_right[:, units])
     packed[...] = fold(jnp.concatenate([low_down, low_pre], axis=1))
-    out_going += [copies.start(packed, packed_to.at[n]) for n in range(packed_to.shape[0])]
+    out_going += [copies.start(packed, packed_to.at[n]) for n in range(4)]
     for b in range(BLOCKS):
         features = slice(b * ROWS, (b + 1) * ROWS)
         hidden, pre = hiddens[b], pres[b]
@@ -189,14 +189,28 @@
     finish(out_going)
 
 
-def mini_body(scale, own, pieces, low, mini):
+def spread_body(pieces, out):
+    total = pieces[0].astype(F32)
+    for n in range(1, 4):
+        total = total + pieces[n].astype(F32)
+    total = total.astype(BF16)
+    for n in range(4):
+        out[n] = total
+
+
+def mini_body(scale, own_at, pieces_at, low, mini, own, pieces, sems):
+    copies = Copies(sems)
+    first = copies.start(pieces_at, pieces)
+    last = copies.start(own_at, own)
     pair = pick_mini()
+    first.wait()
     low_down, low_pre = unfold(pieces)
     low[:, :ROWS] = low_down
     low[:, ROWS:] = low_pre
     zero = jnp.zeros_like(low_pre)
     upper = mt(pair, jnp.concatenate([low_pre, zero], axis=1)).astype(BF16)
     lower = mt(pair, jnp.concatenate([zero, low_down], axis=1)).astype(BF16)
+    last.wait()
     value = mm(upper, own[:ROWS, :]) + mm(lower, own[ROWS:, :])
     mini[...] = (value * scale).astype(BF16)
 
@@ -282,7 +296,7 @@
 
 
 def call(body, outs, kinds, scratch=(), copies=0, cost=(0, 0), limit=LIMIT):
-    kinds, kinds_out = kinds.split()
+    kinds, kinds_out = kinds.split(" ")
     sems = [pltpu.SemaphoreType.DMA((copies,))] if copies else []
 
     def run(*args):
@@ -366,7 +380,7 @@
     weights = (up_blocks, up_right, down_blocks, down_left)
     local, *terms, packed, keep, send = call(
         functools.partial(main_body, scale),
-        [(wide, F32)] + [(wide, BF16)] * 4 + [((16, LOW, SLAB), BF16), (half, BF16), (half, BF16)],
+        [(wide, F32)] + [(wide, BF16)] * 4 + [((4, LOW, SLAB), BF16), (half, BF16), (half, BF16)],
         "saaaaaahhhh aaaaaaaa",
         [((FACTORS, *wide), BF16), shape(low)]
         + [shape(a) for a in weights]
@@ -375,23 +389,30 @@
         cost=(1_500_000_000, 10_000_000),
     )(place, own, *arrived, low, *weights)
 
-    low = exchange(packed, TENSOR)
+    low = exchange(packed, "y")
     got = swap(send, "core", 1)
     pieces = call(
         split_body,
         [((32, MAIN), BF16)] * 4,
-        "aa aaaa",
+        "ha aaaa",
         [(half, BF16)] * 2,
         6 * STEPS,
         cost=(30_000_000_000, 5_000_000),
+        limit=SMALL,
     )(keep, got)
-    pieces = list(pieces[:1]) + [swap(pieces[mask], "x", mask) for mask in (1, 2, 3)]
+    low, terms, pieces = lax.optimization_barrier((low, terms, pieces))
+    low = call(spread_body, [(low.shape, BF16)], "v v", cost=(30_000_000_000, 500_000), limit=SMALL)(low)[0]
+    low = exchange(low, "zl")
+    two_off = swap(pieces[2], "x", 2)
+    pieces = [pieces[0], two_off] + [swap(pieces[mask], "x", mask) for mask in (1, 3)]
     far = [swap(term, axis, mask) for term, (axis, mask) in zip(terms[2:], hops[2:])]
 
     low, mini = call(
         functools.partial(mini_body, scale),
         [(lows, BF16), ((2 * ROWS, MINI), BF16)],
-        "cc cc",
+        "aa cc",
+        [shape(own), shape(low)],
+        2,
         cost=(40_000_000, 1_000_000),
     )(own, low)
     mini = exchange(mini.reshape(8, -1, MINI), ("x", "core"))
@@ -404,6 +425,7 @@
         [((4, 32, MAIN), BF16), (mini.shape, BF16), ((32, MAIN + MINI), BF16)],
         5 * STEPS + 2,
         cost=(1_000_000, 2_000_000),
+        limit=SMALL,
     )(*pieces, mini)[0]
     near, pieces, low = lax.optimization_barrier((terms[:2], pieces, low))
     pieces = exchange(pieces.reshape(SIZES[0], 8, -1), "zh")

time: 139 us -> 138 us (level)
  the two profiles are of different devices: /device:TPU:33 before, /device:TPU:64 now
where the time goes in v5:
time: 138 us; the launch traced here: 137 us
  starting transfers between devices  77.9 us (56%)
  waiting for transfers between devices  34.6 us (25%)
  Pallas kernels  21.1 us (15%)
  local copies, waits for them, and re-layouts  1.97 us (1%)
    all_to_all x6, starting transfers between devices, exchange(): return lax.all_to_all(block, axis, 0, 0)  40.8 us
    ppermute x12, starting transfers between devices, swap(): return lax.ppermute(block, axis, [(i, i ^ mask) for i in range(count)])  37.2 us
    pallas_call x8, Pallas kernels, run(): pl.pallas_call(kernel, out_shape=[jax.ShapeDtypeStruct(s, d) for s, d in...  21.1 us
    all_to_all x6, waiting for transfers between devices, exchange(): return lax.all_to_all(block, axis, 0, 0)  19.7 us
    ppermute x12, waiting for transfers between devices, swap(): return lax.ppermute(block, axis, [(i, i ^ mask) for i in range(count)])  14.9 us
  transfers between devices with their start and end apart: 18, of which 9 were waited for; matrix products, arithmetic and copies ran while one was open for 1% of the time, Pallas kernels for 5%

profile of v5, /device:TPU:64, one launch (start us, length us, event | category | flops | bytes accessed | tf_op | source)
XLA Modules:
  0.0 137.1 jit_solution(11236588680754578276)
XLA Ops:
  2.7 8.4 %all-to-all-start = ((f32[16,8,256]{2,1,0:T(8,128)}), f32[16,8,256]{2,1,0:T(8,128)S(1)}, u32[]{:S(2)}, u32[]{:S(2)}) async-start(f32[16,8,256]{2,1,0:T(8,128)} %bitcast.9), calls=%async_computation | async-start | bytes 262144 | tf_op jit(solution)/shard_map/all_to_all | solution.py:350
  13.2 3.7 %collective-permute-start.2 = (bf16[256,512]{1,0:T(8,128)(2,1)}, bf16[256,512]{1,0:T(8,128)(2,1)S(1)}, u32[]{:S(2)}, u32[]{:S(2)}) collective-permute-start(bf16[256,512]{1,0:T(8,128)(2,1)} %get-tuple-element.51.refs_1_.refs_0_), channel_id=1, source_target_pairs={{0,4},{4,0},{8,12},{12,8},{1,5},{5,1},{9,13},{13,9},{2,6},{6,2},{1... | collective-permute-start | bytes 786440 | tf_op jit(solution)/shard_map/ppermute | solution.py:346
  16.9 4.9 %collective-permute-start.1 = (bf16[256,512]{1,0:T(8,128)(2,1)}, bf16[256,512]{1,0:T(8,128)(2,1)S(1)}, u32[]{:S(2)}, u32[]{:S(2)}) collective-permute-start(bf16[256,512]{1,0:T(8,128)(2,1)} %get-tuple-element.51.refs_1_.refs_0_), channel_id=1, source_target_pairs={{0,2},{1,3},{2,0},{3,1},{4,6},{5,7},{6,4},{7,5},{8,10},{9,11},{10,... | collective-permute-start | bytes 786440 | tf_op jit(solution)/shard_map/ppermute | solution.py:346
  21.8 2.5 %collective-permute-start = (bf16[256,512]{1,0:T(8,128)(2,1)}, bf16[256,512]{1,0:T(8,128)(2,1)S(1)}, u32[]{:S(2)}, u32[]{:S(2)}) collective-permute-start(bf16[256,512]{1,0:T(8,128)(2,1)} %get-tuple-element.51.refs_1_.refs_0_), channel_id=1, source_target_pairs={{0,1},{1,0},{2,3},{3,2},{4,5},{5,4},{6,7},{7,6},{8,9},{9,8},{10,11... | collective-permute-start | bytes 786440 | tf_op jit(solution)/shard_map/ppermute | solution.py:346
  24.9 5.8 %all-to-all-start.1 = ((bf16[16,8,256]{2,1,0:T(8,128)(2,1)}), bf16[16,8,256]{2,1,0:T(8,128)(2,1)S(1)}, u32[]{:S(2)}, u32[]{:S(2)}) async-start(bf16[16,8,256]{2,1,0:T(8,128)(2,1)} %broadcast_in_dim.3), calls=%async_computation.1 | async-start | bytes 131072 | tf_op jit(solution)/shard_map/all_to_all | solution.py:350
  33.2 3.3 %all-to-all-done.1 = bf16[16,8,256]{2,1,0:T(8,128)(2,1)S(1)} async-done(((bf16[16,8,256]{2,1,0:T(8,128)(2,1)}), bf16[16,8,256]{2,1,0:T(8,128)(2,1)S(1)}, u32[]{:S(2)}, u32[]{:S(2)}) %all-to-all-start.1) | async-done | bytes 65568 | tf_op jit(solution)/shard_map/all_to_all | solution.py:350
  37.2 8.3 %shard_map.144 = (f32[256,512]{1,0:T(8,128)}, bf16[256,512]{1,0:T(8,128)(2,1)}, bf16[256,512]{1,0:T(8,128)(2,1)}, bf16[256,512]{1,0:T(8,128)(2,1)}, bf16[256,512...) custom-call(s32[2]{0:T(128)} %pad_add_fusion.refs_0_, ...), custom_call_target="tpu_custom_call" | custom-call | flops 1500000000 | bytes 10000000 | tf_op jit(solution)/shard_map/pallas_call | solution.py:329
  47.4 3.4 %all-to-all-start.2 = ((bf16[4,64,512]{2,1,0:T(8,128)(2,1)}), bf16[4,64,512]{2,1,0:T(8,128)(2,1)S(1)}, u32[]{:S(2)}, u32[]{:S(2)}) async-start(bf16[4,64,512]{2,1,0:T(8,128)(2,1)} %get-tuple-element.54), calls=%async_computation.2 | async-start | bytes 524288 | tf_op jit(solution)/shard_map/all_to_all | solution.py:350
  51.0 2.5 %shard_map.145 = (bf16[32,6144]{1,0:T(8,128)(2,1)S(1)}, bf16[32,6144]{1,0:T(8,128)(2,1)}, bf16[32,6144]{1,0:T(8,128)(2,1)}, bf16[32,6144]{1,0:T(8,128)(2,1)}) custom-call(bf16[128,6144]{1,0:T(8,128)(2,1)} %get-tuple-element.59.refs_0_, bf16[128,6144]{1,0:T(8,128)(2,1)S(1)} %collective-permute-done.4.refs_1_), custom_call_target="tpu_custom_call" | custom-call | flops 30000001024 | bytes 5000000 | tf_op jit(solution)/shard_map/pallas_call | solution.py:329
  53.5 4.9 %all-to-all-done.2.refs_0_ = bf16[4,64,512]{2,1,0:T(8,128)(2,1)S(1)} async-done(((bf16[4,64,512]{2,1,0:T(8,128)(2,1)}), bf16[4,64,512]{2,1,0:T(8,128)(2,1)S(1)}, u32[]{:S(2)}, u32[]{:S(2)}) %all-to-all-start.2) | async-done | bytes 262176 | tf_op jit(solution)/shard_map/all_to_all | solution.py:350
  59.1 6.7 %all-to-all-start.3 = ((bf16[4,64,512]{2,1,0:T(8,128)(2,1)}), bf16[4,64,512]{2,1,0:T(8,128)(2,1)}, u32[]{:S(2)}, u32[]{:S(2)}) async-start(bf16[4,64,512]{2,1,0:T(8,128)(2,1)} %shard_map.146), calls=%async_computation.3 | async-start | bytes 524288 | tf_op jit(solution)/shard_map/all_to_all | solution.py:350
  65.8 4.7 %collective-permute-start.5 = (bf16[32,6144]{1,0:T(8,128)(2,1)}, bf16[32,6144]{1,0:T(8,128)(2,1)S(1)}, u32[]{:S(2)}, u32[]{:S(2)}) collective-permute-start(bf16[32,6144]{1,0:T(8,128)(2,1)} %get-tuple-element.68), channel_id=1, source_target_pairs={{0,64},{32,96},{64,0},{96,32},{1,65},{33,97},{65,1},{97,33},{2,66}... | collective-permute-start | bytes 1179656 | tf_op jit(solution)/shard_map/ppermute | solution.py:346
  70.5 2.5 %collective-permute-start.6 = (bf16[32,6144]{1,0:T(8,128)(2,1)}, bf16[32,6144]{1,0:T(8,128)(2,1)}, u32[]{:S(2)}, u32[]{:S(2)}) collective-permute-start(bf16[32,6144]{1,0:T(8,128)(2,1)} %get-tuple-element.69), channel_id=1, source_target_pairs={{0,32},{32,0},{64,96},{96,64},{1,33},{33,1},{65,97},{97,65},{2,34}... | collective-permute-start | bytes 1179656 | tf_op jit(solution)/shard_map/ppermute | solution.py:346
  73.1 2.6 %collective-permute-start.7 = (bf16[32,6144]{1,0:T(8,128)(2,1)}, bf16[32,6144]{1,0:T(8,128)(2,1)}, u32[]{:S(2)}, u32[]{:S(2)}) collective-permute-start(bf16[32,6144]{1,0:T(8,128)(2,1)} %get-tuple-element.70), channel_id=1, source_target_pairs={{0,96},{32,64},{64,32},{96,0},{1,97},{33,65},{65,33},{97,1},{2,98}... | collective-permute-start | bytes 1179656 | tf_op jit(solution)/shard_map/ppermute | solution.py:346
  75.7 3.4 %collective-permute-start.8 = (bf16[256,512]{1,0:T(8,128)(2,1)}, bf16[256,512]{1,0:T(8,128)(2,1)}, u32[]{:S(2)}, u32[]{:S(2)}) collective-permute-start(bf16[256,512]{1,0:T(8,128)(2,1)} %get-tuple-element.71), channel_id=1, source_target_pairs={{0,4},{4,0},{8,12},{12,8},{1,5},{5,1},{9,13},{13,9},{2,6},{6,2},{1... | collective-permute-start | bytes 786440 | tf_op jit(solution)/shard_map/ppermute | solution.py:346
  79.1 2.5 %collective-permute-start.9 = (bf16[256,512]{1,0:T(8,128)(2,1)}, bf16[256,512]{1,0:T(8,128)(2,1)}, u32[]{:S(2)}, u32[]{:S(2)}) collective-permute-start(bf16[256,512]{1,0:T(8,128)(2,1)} %get-tuple-element.72), channel_id=1, source_target_pairs={{0,8},{4,12},{8,0},{12,4},{1,9},{5,13},{9,1},{13,5},{2,10},{6,14},... | collective-permute-start | bytes 786440 | tf_op jit(solution)/shard_map/ppermute | solution.py:346
  83.8 4.1 %all-to-all-start.4 = ((bf16[8,32,512]{2,1,0:T(8,128)(2,1)}), bf16[8,32,512]{2,1,0:T(8,128)(2,1)S(1)}, u32[]{:S(2)}, u32[]{:S(2)}) async-start(bf16[8,32,512]{2,1,0:T(8,128)(2,1)} %bitcast.8), calls=%async_computation.4 | async-start | bytes 524288 | tf_op jit(solution)/shard_map/all_to_all | solution.py:350
  87.9 3.8 %collective-permute-done.9.refs_4_ = bf16[256,512]{1,0:T(8,128)(2,1)} collective-permute-done((bf16[256,512]{1,0:T(8,128)(2,1)}, bf16[256,512]{1,0:T(8,128)(2,1)}, u32[]{:S(2)}, u32[]{:S(2)}) %collective-permute-start.9) | collective-permute-done | bytes 262176 | tf_op jit(solution)/shard_map/ppermute | solution.py:346
  91.7 3.7 %all-to-all-done.4.refs_4_ = bf16[8,32,512]{2,1,0:T(8,128)(2,1)S(1)} async-done(((bf16[8,32,512]{2,1,0:T(8,128)(2,1)}), bf16[8,32,512]{2,1,0:T(8,128)(2,1)S(1)}, u32[]{:S(2)}, u32[]{:S(2)}) %all-to-all-start.4) | async-done | bytes 262176 | tf_op jit(solution)/shard_map/all_to_all | solution.py:350
  97.6 12.4 %all-to-all-start.5 = ((bf16[4,8,6656]{2,1,0:T(8,128)(2,1)}), bf16[4,8,6656]{2,1,0:T(8,128)(2,1)S(1)}, u32[]{:S(2)}, u32[]{:S(2)}) async-start(bf16[4,8,6656]{2,1,0:T(8,128)(2,1)} %bitcast.5), calls=%async_computation.5 | async-start | bytes 851968 | tf_op jit(solution)/shard_map/all_to_all | solution.py:350
  112.5 4.0 %collective-permute-start.11 = (bf16[256,512]{1,0:T(8,128)(2,1)S(1)}, bf16[256,512]{1,0:T(8,128)(2,1)S(1)}, u32[]{:S(2)}, u32[]{:S(2)}) collective-permute-start(bf16[256,512]{1,0:T(8,128)(2,1)S(1)} %copy-done.3), channel_id=1, source_target_pairs={{0,2},{1,3},{2,0},{3,1},{4,6},{5,7},{6,4},{7,5},{8,10},{9,11},{10,... | collective-permute-start | bytes 786440 | tf_op jit(solution)/shard_map/ppermute | solution.py:346
  116.5 4.7 %collective-permute-done.10.refs_1_ = bf16[256,512]{1,0:T(8,128)(2,1)S(1)} collective-permute-done((bf16[256,512]{1,0:T(8,128)(2,1)S(1)}, bf16[256,512]{1,0:T(8,128)(2,1)S(1)}, u32[]{:S(2)}, u32[]{:S(2)}) %collective-permute-start.10) | collective-permute-done | bytes 262176 | tf_op jit(solution)/shard_map/ppermute | solution.py:346
  121.1 4.4 %collective-permute-done.11.refs_2_ = bf16[256,512]{1,0:T(8,128)(2,1)S(1)} collective-permute-done((bf16[256,512]{1,0:T(8,128)(2,1)S(1)}, bf16[256,512]{1,0:T(8,128)(2,1)S(1)}, u32[]{:S(2)}, u32[]{:S(2)}) %collective-permute-start.11) | collective-permute-done | bytes 262176 | tf_op jit(solution)/shard_map/ppermute | solution.py:346
  128.6 7.7 %all-to-all-done.5.refs_0_ = bf16[4,8,6656]{2,1,0:T(8,128)(2,1)S(1)} async-done(((bf16[4,8,6656]{2,1,0:T(8,128)(2,1)}), bf16[4,8,6656]{2,1,0:T(8,128)(2,1)S(1)}, u32[]{:S(2)}, u32[]{:S(2)}) %all-to-all-start.5) | async-done | bytes 426016 | tf_op jit(solution)/shard_map/all_to_all | solution.py:350
  (41 shorter events, 21.5 us)
Async XLA Ops:
  2.7 21.6 %all-to-all-start = ((f32[16,8,256]{2,1,0:T(8,128)}), f32[16,8,256]{2,1,0:T(8,128)S(1)}, u32[]{:S(2)}, u32[]{:S(2)}) async-start(f32[16,8,256]{2,1,0:T(8,128)} %bitcast.9), calls=%async_computation | async-start | bytes 262144 | tf_op jit(solution)/shard_map/all_to_all | solution.py:350
  11.1 20.2 %collective-permute-start.3 = (bf16[256,512]{1,0:T(8,128)(2,1)}, bf16[256,512]{1,0:T(8,128)(2,1)S(1)}, u32[]{:S(2)}, u32[]{:S(2)}) collective-permute-start(bf16[256,512]{1,0:T(8,128)(2,1)} %get-tuple-element.51.refs_1_.refs_0_), channel_id=1, source_target_pairs={{0,8},{4,12},{8,0},{12,4},{1,9},{5,13},{9,1},{13,5},{2,10},{6,14},... | collective-permute-start | bytes 786440 | tf_op jit(solution)/shard_map/ppermute | solution.py:346
  13.2 18.1 %collective-permute-start.2 = (bf16[256,512]{1,0:T(8,128)(2,1)}, bf16[256,512]{1,0:T(8,128)(2,1)S(1)}, u32[]{:S(2)}, u32[]{:S(2)}) collective-permute-start(bf16[256,512]{1,0:T(8,128)(2,1)} %get-tuple-element.51.refs_1_.refs_0_), channel_id=1, source_target_pairs={{0,4},{4,0},{8,12},{12,8},{1,5},{5,1},{9,13},{13,9},{2,6},{6,2},{1... | collective-permute-start | bytes 786440 | tf_op jit(solution)/shard_map/ppermute | solution.py:346
  16.9 14.4 %collective-permute-start.1 = (bf16[256,512]{1,0:T(8,128)(2,1)}, bf16[256,512]{1,0:T(8,128)(2,1)S(1)}, u32[]{:S(2)}, u32[]{:S(2)}) collective-permute-start(bf16[256,512]{1,0:T(8,128)(2,1)} %get-tuple-element.51.refs_1_.refs_0_), channel_id=1, source_target_pairs={{0,2},{1,3},{2,0},{3,1},{4,6},{5,7},{6,4},{7,5},{8,10},{9,11},{10,... | collective-permute-start | bytes 786440 | tf_op jit(solution)/shard_map/ppermute | solution.py:346
  21.8 11.5 %collective-permute-start = (bf16[256,512]{1,0:T(8,128)(2,1)}, bf16[256,512]{1,0:T(8,128)(2,1)S(1)}, u32[]{:S(2)}, u32[]{:S(2)}) collective-permute-start(bf16[256,512]{1,0:T(8,128)(2,1)} %get-tuple-element.51.refs_1_.refs_0_), channel_id=1, source_target_pairs={{0,1},{1,0},{2,3},{3,2},{4,5},{5,4},{6,7},{7,6},{8,9},{9,8},{10,11... | collective-permute-start | bytes 786440 | tf_op jit(solution)/shard_map/ppermute | solution.py:346
  24.9 11.6 %all-to-all-start.1 = ((bf16[16,8,256]{2,1,0:T(8,128)(2,1)}), bf16[16,8,256]{2,1,0:T(8,128)(2,1)S(1)}, u32[]{:S(2)}, u32[]{:S(2)}) async-start(bf16[16,8,256]{2,1,0:T(8,128)(2,1)} %broadcast_in_dim.3), calls=%async_computation.1 | async-start | bytes 131072 | tf_op jit(solution)/shard_map/all_to_all | solution.py:350
  31.3 5.3 %copy-start.5 = (bf16[256,512]{1,0:T(8,128)(2,1)}, bf16[256,512]{1,0:T(8,128)(2,1)S(1)}, u32[]{:S(2)}) copy-start(bf16[256,512]{1,0:T(8,128)(2,1)S(1)} %collective-permute-done.3.refs_5_) | copy-start | bytes 786436
  31.3 5.3 %copy-start.6 = (bf16[256,512]{1,0:T(8,128)(2,1)}, bf16[256,512]{1,0:T(8,128)(2,1)S(1)}, u32[]{:S(2)}) copy-start(bf16[256,512]{1,0:T(8,128)(2,1)S(1)} %collective-permute-done.2.refs_4_) | copy-start | bytes 786436
  31.3 5.2 %copy-start.7 = (bf16[256,512]{1,0:T(8,128)(2,1)}, bf16[256,512]{1,0:T(8,128)(2,1)S(1)}, u32[]{:S(2)}) copy-start(bf16[256,512]{1,0:T(8,128)(2,1)S(1)} %collective-permute-done.1.refs_3_) | copy-start | bytes 786436
  45.5 5.5 %collective-permute-start.4 = (bf16[128,6144]{1,0:T(8,128)(2,1)}, bf16[128,6144]{1,0:T(8,128)(2,1)S(1)}, u32[]{:S(2)}, u32[]{:S(2)}) collective-permute-start(bf16[128,6144]{1,0:T(8,128)(2,1)} %get-tuple-element.60), channel_id=1, source_target_pairs={{0,16},{16,0},{1,17},{17,1},{2,18},{18,2},{3,19},{19,3},{4,20},{20... | collective-permute-start | bytes 4718600 | tf_op jit(solution)/shard_map/ppermute | solution.py:346
  47.4 11.0 %all-to-all-start.2 = ((bf16[4,64,512]{2,1,0:T(8,128)(2,1)}), bf16[4,64,512]{2,1,0:T(8,128)(2,1)S(1)}, u32[]{:S(2)}, u32[]{:S(2)}) async-start(bf16[4,64,512]{2,1,0:T(8,128)(2,1)} %get-tuple-element.54), calls=%async_computation.2 | async-start | bytes 524288 | tf_op jit(solution)/shard_map/all_to_all | solution.py:350
  59.1 22.4 %all-to-all-start.3 = ((bf16[4,64,512]{2,1,0:T(8,128)(2,1)}), bf16[4,64,512]{2,1,0:T(8,128)(2,1)}, u32[]{:S(2)}, u32[]{:S(2)}) async-start(bf16[4,64,512]{2,1,0:T(8,128)(2,1)} %shard_map.146), calls=%async_computation.3 | async-start | bytes 524288 | tf_op jit(solution)/shard_map/all_to_all | solution.py:350
  65.8 25.8 %collective-permute-start.5 = (bf16[32,6144]{1,0:T(8,128)(2,1)}, bf16[32,6144]{1,0:T(8,128)(2,1)S(1)}, u32[]{:S(2)}, u32[]{:S(2)}) collective-permute-start(bf16[32,6144]{1,0:T(8,128)(2,1)} %get-tuple-element.68), channel_id=1, source_target_pairs={{0,64},{32,96},{64,0},{96,32},{1,65},{33,97},{65,1},{97,33},{2,66}... | collective-permute-start | bytes 1179656 | tf_op jit(solution)/shard_map/ppermute | solution.py:346
  70.5 21.1 %collective-permute-start.6 = (bf16[32,6144]{1,0:T(8,128)(2,1)}, bf16[32,6144]{1,0:T(8,128)(2,1)}, u32[]{:S(2)}, u32[]{:S(2)}) collective-permute-start(bf16[32,6144]{1,0:T(8,128)(2,1)} %get-tuple-element.69), channel_id=1, source_target_pairs={{0,32},{32,0},{64,96},{96,64},{1,33},{33,1},{65,97},{97,65},{2,34}... | collective-permute-start | bytes 1179656 | tf_op jit(solution)/shard_map/ppermute | solution.py:346
  73.1 18.6 %collective-permute-start.7 = (bf16[32,6144]{1,0:T(8,128)(2,1)}, bf16[32,6144]{1,0:T(8,128)(2,1)}, u32[]{:S(2)}, u32[]{:S(2)}) collective-permute-start(bf16[32,6144]{1,0:T(8,128)(2,1)} %get-tuple-element.70), channel_id=1, source_target_pairs={{0,96},{32,64},{64,32},{96,0},{1,97},{33,65},{65,33},{97,1},{2,98}... | collective-permute-start | bytes 1179656 | tf_op jit(solution)/shard_map/ppermute | solution.py:346
  75.7 12.2 %collective-permute-start.8 = (bf16[256,512]{1,0:T(8,128)(2,1)}, bf16[256,512]{1,0:T(8,128)(2,1)}, u32[]{:S(2)}, u32[]{:S(2)}) collective-permute-start(bf16[256,512]{1,0:T(8,128)(2,1)} %get-tuple-element.71), channel_id=1, source_target_pairs={{0,4},{4,0},{8,12},{12,8},{1,5},{5,1},{9,13},{13,9},{2,6},{6,2},{1... | collective-permute-start | bytes 786440 | tf_op jit(solution)/shard_map/ppermute | solution.py:346
  79.1 12.6 %collective-permute-start.9 = (bf16[256,512]{1,0:T(8,128)(2,1)}, bf16[256,512]{1,0:T(8,128)(2,1)}, u32[]{:S(2)}, u32[]{:S(2)}) collective-permute-start(bf16[256,512]{1,0:T(8,128)(2,1)} %get-tuple-element.72), channel_id=1, source_target_pairs={{0,8},{4,12},{8,0},{12,4},{1,9},{5,13},{9,1},{13,5},{2,10},{6,14},... | collective-permute-start | bytes 786440 | tf_op jit(solution)/shard_map/ppermute | solution.py:346
  83.8 11.6 %all-to-all-start.4 = ((bf16[8,32,512]{2,1,0:T(8,128)(2,1)}), bf16[8,32,512]{2,1,0:T(8,128)(2,1)S(1)}, u32[]{:S(2)}, u32[]{:S(2)}) async-start(bf16[8,32,512]{2,1,0:T(8,128)(2,1)} %bitcast.8), calls=%async_computation.4 | async-start | bytes 524288 | tf_op jit(solution)/shard_map/all_to_all | solution.py:350
  87.8 22.2 %copy-start.4 = (bf16[256,512]{1,0:T(8,128)(2,1)S(1)}, bf16[256,512]{1,0:T(8,128)(2,1)}, u32[]{:S(2)}) copy-start(bf16[256,512]{1,0:T(8,128)(2,1)} %get-tuple-element.80) | copy-start | bytes 786436
  87.9 24.6 %copy-start.3 = (bf16[256,512]{1,0:T(8,128)(2,1)S(1)}, bf16[256,512]{1,0:T(8,128)(2,1)}, u32[]{:S(2)}) copy-start(bf16[256,512]{1,0:T(8,128)(2,1)} %get-tuple-element.81) | copy-start | bytes 786436
  97.6 38.8 %all-to-all-start.5 = ((bf16[4,8,6656]{2,1,0:T(8,128)(2,1)}), bf16[4,8,6656]{2,1,0:T(8,128)(2,1)S(1)}, u32[]{:S(2)}, u32[]{:S(2)}) async-start(bf16[4,8,6656]{2,1,0:T(8,128)(2,1)} %bitcast.5), calls=%async_computation.5 | async-start | bytes 851968 | tf_op jit(solution)/shard_map/all_to_all | solution.py:350
  110.0 11.1 %collective-permute-start.10 = (bf16[256,512]{1,0:T(8,128)(2,1)S(1)}, bf16[256,512]{1,0:T(8,128)(2,1)S(1)}, u32[]{:S(2)}, u32[]{:S(2)}) collective-permute-start(bf16[256,512]{1,0:T(8,128)(2,1)S(1)} %copy-done.4), channel_id=1, source_target_pairs={{0,1},{1,0},{2,3},{3,2},{4,5},{5,4},{6,7},{7,6},{8,9},{9,8},{10,11... | collective-permute-start | bytes 786440 | tf_op jit(solution)/shard_map/ppermute | solution.py:346
  112.5 13.0 %collective-permute-start.11 = (bf16[256,512]{1,0:T(8,128)(2,1)S(1)}, bf16[256,512]{1,0:T(8,128)(2,1)S(1)}, u32[]{:S(2)}, u32[]{:S(2)}) collective-permute-start(bf16[256,512]{1,0:T(8,128)(2,1)S(1)} %copy-done.3), channel_id=1, source_target_pairs={{0,2},{1,3},{2,0},{3,1},{4,6},{5,7},{6,4},{7,5},{8,10},{9,11},{10,... | collective-permute-start | bytes 786440 | tf_op jit(solution)/shard_map/ppermute | solution.py:346
  121.1 4.4 %copy-start = (bf16[256,512]{1,0:T(8,128)(2,1)}, bf16[256,512]{1,0:T(8,128)(2,1)S(1)}, u32[]{:S(2)}) copy-start(bf16[256,512]{1,0:T(8,128)(2,1)S(1)} %collective-permute-done.10.refs_1_) | copy-start | bytes 786436
  (3 other events, 4.6 us)
